TPU v7x, 128 devices: a whole 4x4x4 slice. The times are simulated.
128 devices in a mesh: seq: 8 (over x, core), fsdp: 16 (over z, y).
Axes of the slice: x: 4, y: 4, z: 4, core: 2. Of those that a mesh axis runs over, the one named last changes fastest.
Arguments:
- bytes_in: bfloat16 [8, 4096, 1280], P('seq', 'fsdp'), may hold values from -12 to 12, as said below
- doc_lengths: int32 [32], replicated, may hold values from 1 to 2048, 32768 in all
- patch_offsets: int32 [8, 1024], P('seq', 'fsdp'), may hold values from 0 to 256, as said below
- patch_counts: int32 [8, 16], P('seq', 'fsdp'), may hold values from 32 to 64, as said below
- w_query: bfloat16 [1280, 1280], replicated, may hold values from -0.15625 to 0.15625
- w_key: bfloat16 [1280, 1280], replicated, may hold values from -0.15625 to 0.15625
- w_value: bfloat16 [1280, 1280], replicated, may hold values from -0.15625 to 0.15625
- w_proj: bfloat16 [1280, 4096], replicated, may hold values from -0.15625 to 0.15625
- norm_gain: float32 [4096], replicated, may hold values from 0.1 to 1.9
- gate_w: bfloat16 [4096, 7168], P('fsdp', 'seq'), may hold values from -0.09375 to 0.09375
- up_w: bfloat16 [4096, 7168], P('fsdp', 'seq'), may hold values from -0.09375 to 0.09375
- d_hidden: bfloat16 [8, 1024, 7168], P(None, 'fsdp', 'seq'), may hold values from -6 to 6
Outputs:
- hidden: bfloat16 [8, 1024, 7168], P(None, 'fsdp', 'seq')
- grad_gate: float32 [4096, 7168], P('fsdp', 'seq')
- grad_up: float32 [4096, 7168], P('fsdp', 'seq')
- d_patches: float32 [8, 1024, 4096], P('seq', 'fsdp')
Inputs may be any that keep to these rules, and one draw needn't show every extreme that they name: `bytes_in`: byte states of order one. `patch_offsets`: in each device block of 64 slots, slot 0 holds 0, the first c slots hold strictly rising offsets, c being the block's entry of patch_counts, and the other slots hold 256. `patch_counts`: patches of one device block; 64 is reached by some block in every draw.
All inputs are finite; a program needn't handle non-finite values.
Results may differ from a plain program's by a relative error of at most 0.022.
Values may be sent and summed in bfloat16 or wider, within the bound.
A program may use at most 192 MiB of HBM per device.

v0:
```python
import math

import jax
import jax.numpy as jnp
from jax import lax
from jax.sharding import PartitionSpec as P

HEAD = 128
WINDOW = 512


epsilon = 1e-05
masked_score = -1e30


def shifted(shard, axis, by):
    devices = lax.axis_size(axis)
    pairs = [(i, i + by) for i in range(devices) if 0 <= i + by < devices]
    return lax.ppermute(shard, axis, pairs)


def laid_out(pieces, dim):
    lengths = list(pieces.shape[1:])
    lengths[dim] *= pieces.shape[0]
    return jnp.moveaxis(pieces, 0, dim).reshape(lengths)


def copy_for_each(shard, axis):
    copies = jnp.broadcast_to(shard, (lax.axis_size(axis), *shard.shape))
    return lax.all_to_all(copies, axis, split_axis=0, concat_axis=0, tiled=True)


def gather_directly(shard, axis, dim):
    return laid_out(copy_for_each(shard, axis), dim)


def in_one_piece(arrays, axis, dim, along):
    both = jnp.concatenate(arrays, axis=along)
    filled, at, finished = (lax.all_gather(both, axis, axis=dim, tiled=True), 0, [])
    for a in arrays:
        finished.append(lax.slice_in_dim(filled, at, at + a.shape[along], axis=along))
        at += a.shape[along]
    return tuple(finished)


def in_blocks(shard, dim, devices):
    lengths = shard.shape
    pieces = shard.reshape(*lengths[:dim], devices, lengths[dim] // devices, *lengths[dim + 1 :])
    return jnp.moveaxis(pieces, dim, 0)


def summed_on_arrival(shard, axis, dim):
    pieces = in_blocks(shard, dim, lax.axis_size(axis))
    arrived = lax.all_to_all(pieces, axis, split_axis=0, concat_axis=0, tiled=True)
    return arrived.astype(jnp.float32).sum(axis=0)


def doc_index(doc_lengths, positions):
    starts = jnp.cumsum(doc_lengths) - doc_lengths
    inside = (starts[None, :] <= positions[:, None]).astype(jnp.int32)
    return jnp.sum(inside, axis=1) - 1


def window_attention(queries, key_rows, values, query_pos, key_pos, query_doc, key_doc):
    row_count = queries.shape[0]
    head_count = queries.shape[1] // HEAD
    query_heads = queries.reshape(row_count, head_count, HEAD)
    key_heads = key_rows.reshape(-1, head_count, HEAD)
    value_heads = values.reshape(-1, head_count, HEAD)
    scores = jnp.einsum(
        "qhd,khd->hqk", query_heads, key_heads, preferred_element_type=jnp.float32
    ) / math.sqrt(HEAD)
    allowed = (key_pos[None, :] <= query_pos[:, None]) & (
        query_pos[:, None] - key_pos[None, :] < WINDOW
    )
    allowed = allowed & (key_pos[None, :] >= 0) & (key_doc[None, :] == query_doc[:, None])
    scores = jnp.where(allowed[None], scores, masked_score)
    row_max = jnp.max(scores, axis=-1, keepdims=True)
    weights = jnp.exp(scores - row_max)
    weights = (weights / jnp.sum(weights, axis=-1, keepdims=True)).astype(jnp.bfloat16)
    mixed = jnp.einsum("hqk,khd->qhd", weights, value_heads, preferred_element_type=jnp.float32)
    return mixed.reshape(row_count, head_count * HEAD)


def pool_patches(states, offsets, count):
    length = states.shape[0]
    slot_count = offsets.shape[0]
    head_count = states.shape[1] // HEAD
    slot_ids = jnp.arange(slot_count, dtype=jnp.int32)
    present = slot_ids < count
    following = jnp.concatenate([offsets[1:], jnp.full((1,), length, jnp.int32)])
    patch_ends = jnp.where(slot_ids == count - 1, length, following)
    byte_ids = jnp.arange(length, dtype=jnp.int32)
    member = (
        present[:, None]
        & (offsets[:, None] <= byte_ids[None, :])
        & (byte_ids[None, :] < patch_ends[:, None])
    )
    patch_sizes = jnp.sum(member.astype(jnp.float32), axis=1, keepdims=True)
    summed = jnp.dot(member.astype(jnp.bfloat16), states, preferred_element_type=jnp.float32)
    pooled = (summed / jnp.maximum(patch_sizes, 1.0)).astype(jnp.bfloat16)
    pooled_heads = pooled.reshape(slot_count, head_count, HEAD)
    state_heads = states.reshape(length, head_count, HEAD)
    scores = jnp.einsum(
        "jhd,bhd->hjb", pooled_heads, state_heads, preferred_element_type=jnp.float32
    ) / math.sqrt(HEAD)
    scores = jnp.where(member[None], scores, masked_score)
    row_max = jnp.max(scores, axis=-1, keepdims=True)
    weights = jnp.exp(scores - row_max)
    weights = (weights / jnp.sum(weights, axis=-1, keepdims=True)).astype(jnp.bfloat16)
    context = jnp.einsum("hjb,bhd->jhd", weights, state_heads, preferred_element_type=jnp.float32)
    context = context.reshape(slot_count, head_count * HEAD)
    return jnp.where(present[:, None], context, 0.0).astype(jnp.bfloat16)


def shards(
    bytes_in,
    doc_lengths,
    patch_offsets,
    patch_counts,
    w_query,
    w_key,
    w_value,
    w_proj,
    norm_gain,
    gate_w,
    up_w,
    d_hidden,
):
    states = bytes_in[0]
    length = states.shape[0]
    hop_count = (WINDOW - 2 + length) // length
    first_pos = lax.axis_index(("seq", "fsdp")) * length
    queries = jnp.dot(states, w_query, preferred_element_type=jnp.float32).astype(jnp.bfloat16)
    key_rows = jnp.dot(states, w_key, preferred_element_type=jnp.float32).astype(jnp.bfloat16)
    values = jnp.dot(states, w_value, preferred_element_type=jnp.float32).astype(jnp.bfloat16)
    key_parts = [key_rows]
    value_parts = [values]
    for distance in range(1, hop_count + 1):
        earlier = shifted(states, ("seq", "fsdp"), distance)
        earlier_keys = jnp.dot(earlier, w_key, preferred_element_type=jnp.float32).astype(
            jnp.bfloat16
        )
        earlier_values = jnp.dot(earlier, w_value, preferred_element_type=jnp.float32).astype(
            jnp.bfloat16
        )
        key_parts.insert(0, earlier_keys)
        value_parts.insert(0, earlier_values)
    key_all = jnp.concatenate(key_parts, axis=0)
    value_all = jnp.concatenate(value_parts, axis=0)
    query_pos = first_pos + jnp.arange(length, dtype=jnp.int32)
    key_pos = first_pos - hop_count * length + jnp.arange((hop_count + 1) * length, dtype=jnp.int32)
    key_doc = doc_index(doc_lengths, key_pos)
    query_doc = key_doc[hop_count * length :]
    mixed = window_attention(queries, key_all, value_all, query_pos, key_pos, query_doc, key_doc)
    hidden_bytes = (states.astype(jnp.float32) + mixed).astype(jnp.bfloat16)
    context = pool_patches(hidden_bytes, patch_offsets[0], patch_counts[0, 0])
    seq_index = lax.axis_index("seq")
    shard_part = gather_directly(context[None], "seq", 0)
    flat_part = shard_part.reshape(-1, shard_part.shape[-1])
    result = jnp.dot(flat_part, w_proj, preferred_element_type=jnp.float32).astype(jnp.bfloat16)
    features = result.reshape(shard_part.shape[0], shard_part.shape[1], -1)
    seq_count, slot_count, model_width = features.shape
    patch_float = features.reshape(seq_count * slot_count, model_width).astype(jnp.float32)
    inverse = lax.rsqrt(jnp.mean(patch_float * patch_float, axis=1, keepdims=True) + epsilon)
    normed = (patch_float * inverse * norm_gain).astype(jnp.bfloat16)
    gate_full, up_full = in_one_piece((gate_w, up_w), "fsdp", 0, 1)
    gate_pre = jnp.dot(normed, gate_full, preferred_element_type=jnp.float32)
    up_pre = jnp.dot(normed, up_full, preferred_element_type=jnp.float32)
    sigmoid_gate = jax.nn.sigmoid(gate_pre)
    hidden = (gate_pre * sigmoid_gate * up_pre).astype(jnp.bfloat16)
    units = gate_w.shape[1]
    cotangent = d_hidden.reshape(seq_count * slot_count, units).astype(jnp.float32)
    gate_grad = (
        cotangent * up_pre * sigmoid_gate * (1.0 + gate_pre * (1.0 - sigmoid_gate))
    ).astype(jnp.bfloat16)
    up_grad = (cotangent * gate_pre * sigmoid_gate).astype(jnp.bfloat16)
    both_grads = jnp.concatenate([gate_grad, up_grad], axis=1)
    weight_partial = lax.dot_general(
        normed, both_grads, (((0,), (0,)), ((), ())), preferred_element_type=jnp.float32
    )
    reduced = lax.psum_scatter(
        weight_partial.astype(jnp.bfloat16), "fsdp", scatter_dimension=0, tiled=True
    ).astype(jnp.float32)
    grad_gate = reduced[:, :units]
    grad_up = reduced[:, units:]
    input_partial = lax.dot_general(
        gate_grad, gate_full, (((1,), (1,)), ((), ())), preferred_element_type=jnp.float32
    )
    input_partial = input_partial + lax.dot_general(
        up_grad, up_full, (((1,), (1,)), ((), ())), preferred_element_type=jnp.float32
    )
    normed_grad = summed_on_arrival(
        input_partial.reshape(seq_count, slot_count, model_width).astype(jnp.bfloat16), "seq", 0
    )[0]
    own_float = lax.dynamic_index_in_dim(
        patch_float.reshape(seq_count, slot_count, model_width), seq_index, 0, keepdims=False
    )
    own_inverse = lax.dynamic_index_in_dim(
        inverse.reshape(seq_count, slot_count, 1), seq_index, 0, keepdims=False
    )
    scaled = norm_gain * normed_grad
    patch_grad = own_inverse * scaled - own_float * (
        own_inverse * own_inverse * own_inverse
    ) * jnp.mean(scaled * own_float, axis=1, keepdims=True)
    return (hidden.reshape(seq_count, slot_count, units), grad_gate, grad_up, patch_grad[None])


def solution(mesh):
    return jax.shard_map(
        shards,
        mesh=mesh,
        in_specs=(
            P("seq", "fsdp", None),
            P(),
            P("seq", "fsdp"),
            P("seq", "fsdp"),
            P(),
            P(),
            P(),
            P(),
            P(),
            P("fsdp", "seq"),
            P("fsdp", "seq"),
            P(None, "fsdp", "seq"),
        ),
        out_specs=(
            P(None, "fsdp", "seq"),
            P("fsdp", "seq"),
            P("fsdp", "seq"),
            P("seq", "fsdp", None),
        ),
        check_vma=False,
    )
```

profile of v0, /device:TPU:0, one launch (start us, length us, event | category | flops | bytes accessed | tf_op | source)
XLA Modules:
  0.0 273.4 jit_solution(3433169040421448245)
XLA Ops:
  7.2 0.0 copy-start
  7.2 0.0 copy-start.12
  7.2 0.0 all-gather.2.cloned.1.call-start
  7.2 2.3 pad_maximum_fusion.2
  9.5 0.0 all-gather.2.cloned.1.call-update
  9.6 0.0 reduce-scatter.2.cloned.1.call-start
  9.6 4.4 %collective-permute-start.1 = (bf16[256,1280]{1,0:T(8,128)(2,1)}, bf16[256,1280]{1,0:T(8,128)(2,1)}, u32[]{:S(2)}, u32[]{:S(2)}) collective-permute-start(bf16[256,1280]{1,0:T(8,128)(2,1)} %bitcast.93), channel_id=1, source_target_pairs={{0,1},{1,2},{2,3},{3,4},{4,5},{5,6},{6,7},{7,8},{8,9},{9,10},{10,1... | collective-permute-start | bytes 1966088 | tf_op jit(solution)/shard_map/ppermute | solution.py:19
  14.0 4.9 %collective-permute-start = (bf16[256,1280]{1,0:T(8,128)(2,1)}, bf16[256,1280]{1,0:T(8,128)(2,1)}, u32[]{:S(2)}, u32[]{:S(2)}) collective-permute-start(bf16[256,1280]{1,0:T(8,128)(2,1)} %bitcast.94), channel_id=1, source_target_pairs={{0,2},{1,3},{2,4},{3,5},{4,6},{5,7},{6,8},{7,9},{8,10},{9,11},{10,... | collective-permute-start | bytes 1966088 | tf_op jit(solution)/shard_map/ppermute | solution.py:19
  18.9 2.4 copy.50
  22.0 0.1 copy.52
  22.1 0.1 reduce-window.9
  22.1 0.1 reduce.1
  22.3 0.1 convert_reduce_fusion.1
  22.4 0.0 copy-start.11
  22.4 4.4 %convolution_convert_fusion.5 = bf16[256,1280]{1,0:T(8,128)(2,1)} fusion(bf16[1280,1280]{1,0:T(8,128)(2,1)} %param.16, bf16[1,256,1280]{2,1,0:T(8,128)(2,1)} %param.12), kind=kOutput, calls=%fused_computation.28 | convolution fusion | flops 839188480 | bytes 4587520 | tf_op jit(solution)/shard_map/dot_general | solution.py:134
  26.8 2.2 copy.53
  29.0 0.1 slice_bitcast_fusion
  29.1 0.1 compare_select_fusion
  29.1 0.2 convert_reduce_fusion.2
  29.3 0.1 fusion.45
  29.4 0.3 fusion.37
  29.8 4.1 %convolution_convert_fusion.2 = bf16[256,1280]{1,0:T(8,128)(2,1)} fusion(bf16[1280,1280]{1,0:T(8,128)(2,1)} %param.17, bf16[1,256,1280]{2,1,0:T(8,128)(2,1)} %param.12), kind=kOutput, calls=%fused_computation.25 | convolution fusion | flops 839188480 | bytes 4587520 | tf_op jit(solution)/shard_map/dot_general | solution.py:135
  33.9 1.0 convolution_convert_fusion.6
  34.9 0.0 collective-permute-done.1
  34.9 2.1 convolution_convert_fusion.7
  37.0 19.2 %collective-permute-done = bf16[256,1280]{1,0:T(8,128)(2,1)} collective-permute-done((bf16[256,1280]{1,0:T(8,128)(2,1)}, bf16[256,1280]{1,0:T(8,128)(2,1)}, u32[]{:S(2)}, u32[]{:S(2)}) %collective-permute-start) | collective-permute-done | bytes 655392 | tf_op jit(solution)/shard_map/ppermute | solution.py:19
  56.3 2.1 convolution_convert_fusion.8
  58.4 0.1 pad_maximum_fusion
  58.5 2.5 copy.51
  61.1 3.3 %convolution_convert_fusion.3 = bf16[256,1280]{1,0:T(8,128)(2,1)S(1)} fusion(bf16[256,1280]{1,0:T(8,128)(2,1)} %collective-permute-done.1, bf16[1280,1280]{1,0:T(8,128)(2,1)} %param.17), kind=kOutput, calls=%fused_computation.26 | convolution fusion | flops 839188480 | bytes 4587520 | tf_op jit(solution)/shard_map/dot_general | solution.py:141
  64.4 0.0 copy-start.9
  64.4 2.2 convolution_convert_fusion.4
  66.6 0.0 copy-start.7
  66.6 0.1 pad_maximum_fusion.1
  66.7 2.5 copy.54
  69.2 8.0 %fusion.56 = (f32[10,256]{1,0:T(8,128)S(1)}, f32[10,256,768]{2,1,0:T(8,128)}) fusion(pred[256,768]{1,0:T(8,128)(4,1)S(1)} %fusion.37, bf16[256,10,128]{0,2,1:T(8,128)(2,1)S(1)} %bitcast.100, bf16[768,10,128]{0,2,1:T(8,128)(2,1)} %bitcast.96), kind=kOutput, calls=%fused_computation.101 | convolution fusion | flops 511181568 | bytes 10692608 | tf_op jit(solution)/shard_map/sub | solution.py:79
  77.2 6.5 %fusion.28 = (bf16[256,10,128]{0,2,1:T(8,128)(2,1)}, f32[10,128,256]{2,1,0:T(8,128)S(1)}) fusion(f32[256,10,128]{0,2,1:T(8,128)S(1)} %bitcast.99, bf16[768,10,128]{0,2,1:T(8,128)(2,1)} %bitcast.95, f32[10,256,768]{2,1,0:T(8,128)} %get-tuple-element.12, f32[10,256]{1,0:T(8,128)S(1)} %get-tuple-element.11), kind=kOutput, calls=%fused_computation.50 | convolution fusion | flops 507904000 | bytes 13117440 | tf_op jit(solution)/shard_map/hqk,khd->qhd/dot_general | solution.py:81
  83.7 0.4 copy.57
  84.1 0.0 copy-start.8
  84.1 0.3 fusion.31
  84.4 1.3 fusion.30
  85.8 0.3 fusion.57
  86.1 1.2 convolution_bitcast_fusion
  87.2 0.1 fusion.40
  87.3 0.1 broadcast_in_dim.49
  87.4 30.2 %all_to_all.10 = bf16[8,1,64,1280]{3,2,1,0:T(8,128)(2,1)S(1)} all-to-all(bf16[8,1,64,1280]{3,2,1,0:T(8,128)(2,1)S(1)} %broadcast_in_dim.49), channel_id=1, replica_groups=mesh['seq'=8,'fsdp'=16] {'seq'}, dimensions={0} | all-to-all | bytes 2621440 | tf_op jit(solution)/shard_map/all_to_all | solution.py:30
  117.7 8.4 %multiply_reduce_fusion = (f32[512]{0:T(512)S(1)}, f32[512,4096]{1,0:T(8,128)S(1)}) fusion(bf16[512,1280]{1,0:T(8,128)(2,1)S(1)} %bitcast.98, bf16[1280,4096]{1,0:T(8,128)(2,1)} %param.19), kind=kOutput, calls=%fused_computation.6 | convolution fusion | flops 5377097216 | bytes 20187136 | tf_op jit(solution)/shard_map/dot_general | solution.py:161
  126.1 3.3 %copy-done.2 = f32[512,4096]{1,0:T(8,128)} copy-done((f32[512,4096]{1,0:T(8,128)}, f32[512,4096]{1,0:T(8,128)S(1)}, u32[]{:S(2)}) %copy-start.2) | copy-done | bytes 8388632
  129.4 3.4 %multiply_convert_fusion = bf16[512,4096]{1,0:T(8,128)(2,1)} fusion(f32[512,4096]{1,0:T(8,128)S(1)} %get-tuple-element.16, f32[4096]{0:T(1024)S(1)} %copy-done.10, f32[512]{0:T(512)S(1)} %add_rsqrt_fusion), kind=kLoop, calls=%fused_computation.5 | loop fusion | flops 6291456 | bytes 12601344 | tf_op jit(solution)/shard_map/convert_element_type | solution.py:166
  132.9 10.2 %fusion.8 = f32[512,896]{1,0:T(8,128)S(1)} fusion(bf16[512,4096]{1,0:T(8,128)(2,1)} %multiply_convert_fusion, bf16[4096,1792]{1,0:T(8,128)(2,1)} %all-gather.2.cloned.1.call-done), kind=kOutput, calls=%fused_computation.16 | convolution fusion | flops 3758096384 | bytes 13369344 | tf_op jit(solution)/shard_map/dot_general | solution.py:168
  143.1 9.2 %fusion.21 = (bf16[512,896]{1,0:T(8,128)(2,1)S(1)}, bf16[512,896]{1,0:T(8,128)(2,1)}, bf16[512,896]{1,0:T(8,128)(2,1)S(1)}) fusion(f32[512,896]{1,0:T(8,128)S(1)} %fusion.8, bf16[8,64,896]{2,1,0:T(8,128)(2,1)S(1)} %copy-done.14, bf16[512,4096]{1,0:T(8,128)(2,1)S(1)} %copy-done.3, bf16[4096,1792]{1,0:T(8,128)(2,1)} %all-gather.2.cloned.1.call-done), kind=kOutput, calls=%fused_computation.40 | convolution fusion | flops 3765895168 | bytes 17039360 | tf_op jit(solution)/shard_map/dot_general | solution.py:169
  152.3 11.1 %convolution_convert_fusion = bf16[4096,1792]{1,0:T(8,128)(2,1)} fusion(bf16[512,4096]{1,0:T(8,128)(2,1)S(1)} %copy-done.3, bf16[512,896]{1,0:T(8,128)(2,1)S(1)} %get-tuple-element.8, bf16[512,896]{1,0:T(8,128)(2,1)S(1)} %get-tuple-element.6), kind=kOutput, calls=%fused_computation.2 | convolution fusion | flops 7527202816 | bytes 20709376 | tf_op jit(solution)/shard_map/dot_general | solution.py:179
  163.4 0.0 reduce-scatter.2.cloned.1.call-update
  163.4 6.9 %fusion.2 = f32[512,4096]{1,0:T(8,128)S(1)} fusion(bf16[512,896]{1,0:T(8,128)(2,1)S(1)} %get-tuple-element.8, bf16[4096,1792]{1,0:T(8,128)(2,1)} %all-gather.2.cloned.1.call-done), kind=kOutput, calls=%fused_computation.10 | convolution fusion | flops 3758096384 | bytes 16646144 | tf_op jit(solution)/shard_map/dot_general | solution.py:190
  170.3 10.1 %add_convert_fusion = bf16[512,4096]{1,0:T(8,128)(2,1)} fusion(f32[512,4096]{1,0:T(8,128)S(1)} %fusion.2, bf16[512,896]{1,0:T(8,128)(2,1)S(1)} %get-tuple-element.6, bf16[4096,1792]{1,0:T(8,128)(2,1)} %all-gather.2.cloned.1.call-done), kind=kOutput, calls=%fused_computation.4 | convolution fusion | flops 3762290688 | bytes 20840448 | tf_op jit(solution)/shard_map/dot_general | solution.py:187
  180.4 4.5 %all-to-all-start.1 = ((bf16[8,1,64,4096]{3,2,1,0:T(8,128)(2,1)}), bf16[8,1,64,4096]{3,2,1,0:T(8,128)(2,1)}, u32[]{:S(2)}, u32[]{:S(2)}) async-start(bf16[8,1,64,4096]{3,2,1,0:T(8,128)(2,1)} %bitcast.92), calls=%async_computation.2 | async-start | bytes 8388608 | tf_op jit(solution)/shard_map/all_to_all | solution.py:54
  185.0 0.1 rsqrt.19
  185.1 49.6 %all-to-all-done.1 = bf16[8,1,64,4096]{3,2,1,0:T(8,128)(2,1)} async-done(((bf16[8,1,64,4096]{3,2,1,0:T(8,128)(2,1)}), bf16[8,1,64,4096]{3,2,1,0:T(8,128)(2,1)}, u32[]{:S(2)}, u32[]{:S(2)}) %all-to-all-start.1) | async-done | bytes 4194336 | tf_op jit(solution)/shard_map/all_to_all | solution.py:54
  234.6 3.1 %convert_reduce_fusion = f32[64,4096]{1,0:T(8,128)S(1)} fusion(bf16[8,1,64,4096]{3,2,1,0:T(8,128)(2,1)} %all-to-all-done.1), kind=kLoop, calls=%fused_computation.3 | loop fusion | flops 3932160 | bytes 5242880 | tf_op jit(solution)/shard_map/reduce_sum | solution.py:55
  237.7 1.4 fusion.32
  239.2 0.0 copy-start.1
  239.2 2.6 fusion.34
  241.8 22.3 %reduce-scatter.2.cloned.1.call-done = bf16[256,1792]{1,0:T(8,128)(2,1)} async-done(((bf16[4096,1792]{1,0:T(8,128)(2,1)}), bf16[256,1792]{1,0:T(8,128)(2,1)}) %reduce-scatter.2.cloned.1.call-update) | async-done | bytes 917520 | tf_op jit(solution)/shard_map/reduce_scatter | solution.py:182
  264.1 2.5 fusion.55
  (34 shorter events, 0.1 us)
Async XLA Ops:
  7.2 26.7 %copy-start = (bf16[1280,1280]{1,0:T(8,128)(2,1)S(1)}, bf16[1280,1280]{1,0:T(8,128)(2,1)}, u32[]{:S(2)}) copy-start(bf16[1280,1280]{1,0:T(8,128)(2,1)} %param.18) | copy-start | bytes 9830404
  7.2 14.8 %copy-start.12 = (s32[32]{0:T(128)S(1)}, s32[32]{0:T(128)}, u32[]{:S(2)}) copy-start(s32[32]{0:T(128)} %param.13) | copy-start | bytes 388
  7.2 125.7 %all-gather.2.cloned.1.call-start = ((), (), s32[]{:S(2)}) async-start(), calls=%async_computation.3 | async-start | bytes 15597568 | tf_op jit(solution)/shard_map/all_gather | solution.py:39
  9.6 254.5 %reduce-scatter.2.cloned.1.call-start = ((), (), s32[]{:S(2)}) async-start(), calls=%async_computation.4 | async-start | bytes 15597568 | tf_op jit(solution)/shard_map/reduce_scatter | solution.py:182
  9.6 25.3 %collective-permute-start.1 = (bf16[256,1280]{1,0:T(8,128)(2,1)}, bf16[256,1280]{1,0:T(8,128)(2,1)}, u32[]{:S(2)}, u32[]{:S(2)}) collective-permute-start(bf16[256,1280]{1,0:T(8,128)(2,1)} %bitcast.93), channel_id=1, source_target_pairs={{0,1},{1,2},{2,3},{3,4},{4,5},{5,6},{6,7},{7,8},{8,9},{9,10},{10,1... | collective-permute-start | bytes 1966088 | tf_op jit(solution)/shard_map/ppermute | solution.py:19
  14.0 42.2 %collective-permute-start = (bf16[256,1280]{1,0:T(8,128)(2,1)}, bf16[256,1280]{1,0:T(8,128)(2,1)}, u32[]{:S(2)}, u32[]{:S(2)}) collective-permute-start(bf16[256,1280]{1,0:T(8,128)(2,1)} %bitcast.94), channel_id=1, source_target_pairs={{0,2},{1,3},{2,4},{3,5},{4,6},{5,7},{6,8},{7,9},{8,10},{9,11},{10,... | collective-permute-start | bytes 1966088 | tf_op jit(solution)/shard_map/ppermute | solution.py:19
  22.4 6.6 %copy-start.11 = (s32[1,64]{1,0:T(1,128)S(1)}, s32[1,64]{1,0:T(1,128)}, u32[]{:S(2)}) copy-start(s32[1,64]{1,0:T(1,128)} %param.14) | copy-start | bytes 772
  29.0 4.9 %copy-start.4 = (bf16[1,256,1280]{2,1,0:T(8,128)(2,1)S(1)}, bf16[1,256,1280]{2,1,0:T(8,128)(2,1)}, u32[]{:S(2)}) copy-start(bf16[1,256,1280]{2,1,0:T(8,128)(2,1)} %param.12) | copy-start | bytes 1966084
  61.0 3.3 %copy-start.13 = (bf16[1280,1280]{1,0:T(8,128)(2,1)S(1)}, bf16[1280,1280]{1,0:T(8,128)(2,1)}, u32[]{:S(2)}) copy-start(bf16[1280,1280]{1,0:T(8,128)(2,1)} %param.17) | copy-start | bytes 9830404
  64.4 2.2 copy-start.9
  66.6 2.6 copy-start.7
  69.2 8.0 %copy-start.6 = (f32[1,256,1280]{1,2,0:T(8,128)S(1)}, f32[1,256,1280]{1,2,0:T(8,128)}, u32[]{:S(2)}) copy-start(f32[1,256,1280]{1,2,0:T(8,128)} %copy.50) | copy-start | bytes 3932164
  77.2 6.9 %copy-start.5 = (bf16[1,256,1280]{2,1,0:T(8,128)(2,1)S(1)}, bf16[1,256,1280]{2,1,0:T(8,128)(2,1)}, u32[]{:S(2)}) copy-start(bf16[1,256,1280]{2,1,0:T(8,128)(2,1)} %param.12) | copy-start | bytes 1966084
  84.1 1.9 copy-start.8
  117.7 11.8 %copy-start.10 = (f32[4096]{0:T(1024)S(1)}, f32[4096]{0:T(1024)}, u32[]{:S(2)}) copy-start(f32[4096]{0:T(1024)} %param.20) | copy-start | bytes 49156
  126.1 3.3 %copy-start.2 = (f32[512,4096]{1,0:T(8,128)}, f32[512,4096]{1,0:T(8,128)S(1)}, u32[]{:S(2)}) copy-start(f32[512,4096]{1,0:T(8,128)S(1)} %get-tuple-element.16) | copy-start | bytes 25165828
  132.9 10.2 %copy-start.14 = (bf16[8,64,896]{2,1,0:T(8,128)(2,1)S(1)}, bf16[8,64,896]{2,1,0:T(8,128)(2,1)}, u32[]{:S(2)}) copy-start(bf16[8,64,896]{2,1,0:T(8,128)(2,1)} %param.23) | copy-start | bytes 2752516
  132.9 10.3 %copy-start.3 = (bf16[512,4096]{1,0:T(8,128)(2,1)S(1)}, bf16[512,4096]{1,0:T(8,128)(2,1)}, u32[]{:S(2)}) copy-start(bf16[512,4096]{1,0:T(8,128)(2,1)} %multiply_convert_fusion) | copy-start | bytes 12582916
  180.4 54.2 %all-to-all-start.1 = ((bf16[8,1,64,4096]{3,2,1,0:T(8,128)(2,1)}), bf16[8,1,64,4096]{3,2,1,0:T(8,128)(2,1)}, u32[]{:S(2)}, u32[]{:S(2)}) async-start(bf16[8,1,64,4096]{3,2,1,0:T(8,128)(2,1)} %bitcast.92), calls=%async_computation.2 | async-start | bytes 8388608 | tf_op jit(solution)/shard_map/all_to_all | solution.py:54
  239.2 27.4 %copy-start.1 = (bf16[1280,1280]{1,0:T(8,128)(2,1)S(1)}, bf16[1280,1280]{1,0:T(8,128)(2,1)}, u32[]{:S(2)}) copy-start(bf16[1280,1280]{1,0:T(8,128)(2,1)} %param.18) | copy-start | bytes 9830404
Sparse Core Ops, SparseCore 0:
  10.7 120.0 all-gather.1
  163.5 100.5 reduce-scatter.1
where the time goes:
time: 275 us; the launch traced here: 273 us
  matrix products  92.4 us (34%)
  waiting for transfers between devices  91.2 us (33%)
  blocking collectives  30.2 us (11%)
  local copies, waits for them, and re-layouts  16.2 us (6%)
  between operations  15 us (5%)
  other arithmetic  14.5 us (5%)
  starting transfers between devices  13.9 us (5%)
    all_to_all x1, waiting for transfers between devices, summed_on_arrival(): lax.all_to_all(pieces, axis, split_axis=0, concat_axis=0, tiled=True)  49.6 us
    all_to_all x1, blocking collectives, copy_for_each(): return lax.all_to_all(copies, axis, split_axis=0, concat_axis=0, tiled=True)  30.2 us
    reduce_scatter x1, waiting for transfers between devices, shards(): lax.psum_scatter(weight_partial.astype(jnp.bfloat16), 'fsdp', scatter_dim...  22.3 us
    ppermute x2, waiting for transfers between devices, shifted(): return lax.ppermute(shard, axis, pairs)  19.2 us
    dot_general x1, matrix products, shards(): lax.dot_general(normed, both_grads, (((0,), (0,)), ((), ())), preferred_e...  11.1 us
    dot_general x1, matrix products, shards(): gate_pre = jnp.dot(normed, gate_full, preferred_element_type=jnp.float32)  10.2 us
    dot_general x1, matrix products, shards(): lax.dot_general(gate_grad, gate_full, (((1,), (1,)), ((), ())), preferred...  10.1 us
    ppermute x2, starting transfers between devices, shifted(): return lax.ppermute(shard, axis, pairs)  9.29 us
  transfers between devices with their start and end apart: 5, of which 3 were waited for; matrix products, arithmetic and copies ran while one was open for 31% of the time, Pallas kernels for 0%

commit v1 on v0

--- a/solution.py
+++ b/solution.py
@@ -3,6 +3,8 @@
 import jax
 import jax.numpy as jnp
 from jax import lax
+from jax.experimental import pallas as pl
+from jax.experimental.pallas import tpu as pltpu
 from jax.sharding import PartitionSpec as P
 
 HEAD = 128
@@ -53,6 +55,176 @@
     pieces = in_blocks(shard, dim, lax.axis_size(axis))
     arrived = lax.all_to_all(pieces, axis, split_axis=0, concat_axis=0, tiled=True)
     return arrived.astype(jnp.float32).sum(axis=0)
+
+
+MESH = pl.DeviceIdType.MESH
+SIDE = 4
+
+
+def wrapped(value):
+    return lax.rem(value + 2 * SIDE, SIDE)
+
+
+def grad_rings(
+    normed_ref, grads_ref, out_ref, first, arrived, second, crossed, put, got, put2, got2
+):
+    seq = lax.axis_index("seq")
+    spot = lax.axis_index("fsdp")
+    z, y = lax.div(spot, SIDE), lax.rem(spot, SIDE)
+    rows = first.shape[2]
+    units = out_ref.shape[2]
+
+    barrier = pltpu.get_barrier_semaphore()
+    around = (
+        wrapped(z + 1) * SIDE + y,
+        wrapped(z - 1) * SIDE + y,
+        z * SIDE + wrapped(y + 1),
+        z * SIDE + wrapped(y - 1),
+    )
+    for neighbour in around:
+        pl.semaphore_signal(barrier, inc=1, device_id=(seq, neighbour), device_id_type=MESH)
+    pl.semaphore_wait(barrier, len(around))
+
+    def place(stream):
+        kind, half = stream // 2, stream % 2
+        step = 1 - 2 * half
+        along, across = (z, y) if kind == 0 else (y, z)
+        if kind == 0:
+            onward, sideways = around[half], around[2 + half]
+        else:
+            onward, sideways = around[2 + half], around[half]
+        return kind, half, step, along, across, onward, sideways
+
+    def own(stream, t, k):
+        kind, half, step, along, across, _, _ = place(stream)
+        far = wrapped(along - step * (1 + t))
+        near = wrapped(across - step * (1 + k))
+        zb, yb = (far, near) if kind == 0 else (near, far)
+        at = pl.multiple_of((zb * SIDE + yb) * 2 * rows + half * rows, rows)
+        return lax.dot_general(
+            normed_ref[:, pl.ds(at, rows)],
+            grads_ref[:, kind * units : (kind + 1) * units],
+            (((0,), (0,)), ((), ())),
+            preferred_element_type=jnp.float32,
+        )
+
+    def hop(stream, source, t, k):
+        onward = place(stream)[5]
+        return pltpu.make_async_remote_copy(
+            src_ref=source,
+            dst_ref=arrived.at[stream, t, k],
+            send_sem=put.at[stream, t, k],
+            recv_sem=got.at[stream, t, k],
+            device_id=(seq, onward),
+            device_id_type=MESH,
+        )
+
+    def hop2(stream, source, k):
+        sideways = place(stream)[6]
+        return pltpu.make_async_remote_copy(
+            src_ref=source,
+            dst_ref=crossed.at[stream, k],
+            send_sem=put2.at[stream, k],
+            recv_sem=got2.at[stream, k],
+            device_id=(seq, sideways),
+            device_id_type=MESH,
+        )
+
+    def opening(k, carry):
+        for stream in range(4):
+            first[stream, k] = own(stream, 0, k).astype(jnp.bfloat16)
+            hop(stream, first.at[stream, k], 0, k).start()
+        return carry
+
+    lax.fori_loop(0, SIDE, opening, 0)
+
+    def middle(index, carry):
+        t, k = lax.div(index, SIDE) + 1, lax.rem(index, SIDE)
+        for stream in range(4):
+            value = own(stream, t, k)
+            hop(stream, first.at[stream, k], t - 1, k).wait_recv()
+            arrived[stream, t - 1, k] = (
+                value + arrived[stream, t - 1, k].astype(jnp.float32)
+            ).astype(jnp.bfloat16)
+            hop(stream, arrived.at[stream, t - 1, k], t, k).start()
+        return carry
+
+    lax.fori_loop(0, 2 * SIDE, middle, 0)
+
+    last = SIDE - 1
+
+    def total(stream, k):
+        value = own(stream, last, k)
+        hop(stream, first.at[stream, k], last - 1, k).wait_recv()
+        return value + arrived[stream, last - 1, k].astype(jnp.float32)
+
+    for stream in range(4):
+        second[stream] = total(stream, 0).astype(jnp.bfloat16)
+        hop2(stream, second.at[stream], 0).start()
+
+    def crossing(k, carry):
+        for stream in range(4):
+            value = total(stream, k)
+            hop2(stream, second.at[stream], k - 1).wait_recv()
+            crossed[stream, k - 1] = (
+                value + crossed[stream, k - 1].astype(jnp.float32)
+            ).astype(jnp.bfloat16)
+            hop2(stream, crossed.at[stream, k - 1], k).start()
+        return carry
+
+    lax.fori_loop(1, last, crossing, 0)
+
+    for stream in range(4):
+        kind, half = stream // 2, stream % 2
+        value = total(stream, last)
+        hop2(stream, second.at[stream], last - 1).wait_recv()
+        out_ref[kind, half * rows : (half + 1) * rows, :] = value + crossed[
+            stream, last - 1
+        ].astype(jnp.float32)
+
+    def sent(index, carry):
+        t, k = lax.div(index, SIDE), lax.rem(index, SIDE)
+        for stream in range(4):
+            hop(stream, first.at[stream, k], t, k).wait_send()
+        return carry
+
+    lax.fori_loop(0, last * SIDE, sent, 0)
+    for stream in range(4):
+        for k in range(last):
+            hop2(stream, second.at[stream], k).wait_send()
+
+
+def weight_grads(normed, grads):
+    tokens, width = normed.shape
+    units = grads.shape[1] // 2
+    rows = width // (SIDE * SIDE)
+    half = rows // 2
+    block = (half, units)
+    return pl.pallas_call(
+        grad_rings,
+        out_shape=jax.ShapeDtypeStruct((2, rows, units), jnp.float32),
+        in_specs=[pl.BlockSpec(memory_space=pltpu.VMEM)] * 2,
+        out_specs=pl.BlockSpec(memory_space=pltpu.VMEM),
+        scratch_shapes=[
+            pltpu.VMEM((4, SIDE, *block), jnp.bfloat16),
+            pltpu.VMEM((4, SIDE - 1, SIDE, *block), jnp.bfloat16),
+            pltpu.VMEM((4, *block), jnp.bfloat16),
+            pltpu.VMEM((4, SIDE - 1, *block), jnp.bfloat16),
+            pltpu.SemaphoreType.DMA((4, SIDE - 1, SIDE)),
+            pltpu.SemaphoreType.DMA((4, SIDE - 1, SIDE)),
+            pltpu.SemaphoreType.DMA((4, SIDE - 1)),
+            pltpu.SemaphoreType.DMA((4, SIDE - 1)),
+        ],
+        compiler_params=pltpu.CompilerParams(
+            collective_id=0, has_side_effects=True, vmem_limit_bytes=48 * 1024 * 1024
+        ),
+        cost_estimate=pl.CostEstimate(
+            flops=2 * tokens * width * 2 * units,
+            bytes_accessed=200_000_000,
+            transcendentals=0,
+        ),
+        name="grad_rings",
+    )(normed, grads)
 
 
 def doc_index(doc_lengths, positions):
@@ -176,23 +348,20 @@
     ).astype(jnp.bfloat16)
     up_grad = (cotangent * gate_pre * sigmoid_gate).astype(jnp.bfloat16)
     both_grads = jnp.concatenate([gate_grad, up_grad], axis=1)
-    weight_partial = lax.dot_general(
-        normed, both_grads, (((0,), (0,)), ((), ())), preferred_element_type=jnp.float32
-    )
-    reduced = lax.psum_scatter(
-        weight_partial.astype(jnp.bfloat16), "fsdp", scatter_dimension=0, tiled=True
-    ).astype(jnp.float32)
-    grad_gate = reduced[:, :units]
-    grad_up = reduced[:, units:]
     input_partial = lax.dot_general(
         gate_grad, gate_full, (((1,), (1,)), ((), ())), preferred_element_type=jnp.float32
     )
     input_partial = input_partial + lax.dot_general(
         up_grad, up_full, (((1,), (1,)), ((), ())), preferred_element_type=jnp.float32
     )
-    normed_grad = summed_on_arrival(
-        input_partial.reshape(seq_count, slot_count, model_width).astype(jnp.bfloat16), "seq", 0
-    )[0]
+    normed_grad = lax.psum_scatter(
+        input_partial.reshape(seq_count, slot_count, model_width).astype(jnp.bfloat16),
+        "seq",
+        scatter_dimension=0,
+        tiled=True,
+    )[0].astype(jnp.float32)
+    totals = weight_grads(normed, both_grads)
+    grad_gate, grad_up = totals[0], totals[1]
     own_float = lax.dynamic_index_in_dim(
         patch_float.reshape(seq_count, slot_count, model_width), seq_index, 0, keepdims=False
     )

time: 275 us -> 264 us (0.960)
  Pallas kernels: 0 us -> 84.6 us
  waiting for transfers between devices: 91.2 us -> 19.3 us
  matrix products: 92.4 us -> 77.2 us
  starting transfers between devices: 13.9 us -> 9.37 us
    pallas_call x0 -> x1, Pallas kernels: none -> 84.6 us  [weight_grads(): pl.pallas_call(grad_rings, out_shape=jax.ShapeDtypeStruct((2, rows, units...]
    all_to_all x1 -> x0, waiting for transfers between devices: 49.6 us -> none  [summed_on_arrival(): lax.all_to_all(pieces, axis, split_axis=0, concat_axis=0, tiled=True)]
    reduce_scatter x1, waiting for transfers between devices: 22.3 us -> 0.01 us  [shards(): lax.psum_scatter(input_partial.reshape(seq_count, slot_count, model_width...]
    dot_general x1 -> x0, matrix products: 11.1 us -> none  [shards(): lax.dot_general(normed, both_grads, (((0,), (0,)), ((), ())), preferred_e...]
    all_to_all x1 -> x0, starting transfers between devices: 4.54 us -> none  [summed_on_arrival(): lax.all_to_all(pieces, axis, split_axis=0, concat_axis=0, tiled=True)]
    dot_general x1, matrix products: 9.16 us -> 6.09 us  [shards(): up_pre = jnp.dot(normed, up_full, preferred_element_type=jnp.float32)]
    reduce_sum x1 -> x0, other arithmetic: 3.06 us -> none  [summed_on_arrival(): return arrived.astype(jnp.float32).sum(axis=0)]
  transfers between devices with their start and end apart: 5 -> 4, of which waited for: 3 -> 1; matrix products, arithmetic and copies ran while one was open for 31% -> 24% of each run, Pallas kernels for 0% -> 32%
where the time goes in v1:
time: 264 us
  Pallas kernels  84.6 us (32%)
  matrix products  77.2 us (29%)
  blocking collectives  30.2 us (11%)
  waiting for transfers between devices  19.3 us (7%)
  local copies, waits for them, and re-layouts  16.5 us (6%)
  between operations  15 us (6%)
  other arithmetic  11.8 us (4%)
  starting transfers between devices  9.37 us (4%)
    pallas_call x1, Pallas kernels, weight_grads(): pl.pallas_call(grad_rings, out_shape=jax.ShapeDtypeStruct((2, rows, units...  84.6 us
    all_to_all x1, blocking collectives, copy_for_each(): return lax.all_to_all(copies, axis, split_axis=0, concat_axis=0, tiled=True)  30.2 us
    ppermute x2, waiting for transfers between devices, shifted(): return lax.ppermute(shard, axis, pairs)  19.2 us
    dot_general x1, matrix products, shards(): lax.dot_general(gate_grad, gate_full, (((1,), (1,)), ((), ())), preferred...  10.4 us
    dot_general x1, matrix products, shards(): gate_pre = jnp.dot(normed, gate_full, preferred_element_type=jnp.float32)  10.2 us
    ppermute x2, starting transfers between devices, shifted(): return lax.ppermute(shard, axis, pairs)  9.29 us
    dot_general x1, matrix products, shards(): jnp.dot(flat_part, w_proj, preferred_element_type=jnp.float32)  8.44 us
    sub x1, matrix products, window_attention(): weights = jnp.exp(scores - row_max)  8.03 us
  transfers between devices with their start and end apart: 4, of which 1 were waited for; matrix products, arithmetic and copies ran while one was open for 24% of the time, Pallas kernels for 32%

profile of v1, /device:TPU:0, one launch (start us, length us, event | category | flops | bytes accessed | tf_op | source)
XLA Modules:
  0.0 263.9 jit_solution(3371760319106762002)
XLA Ops:
  7.2 0.0 copy-start
  7.2 0.0 copy-start.11
  7.2 0.0 all-gather.2.cloned.1.call-start
  7.2 2.3 pad_maximum_fusion.3
  9.5 0.0 all-gather.2.cloned.1.call-update
  9.6 0.0 reduce-scatter.2.cloned.1.call-start
  9.6 4.4 %collective-permute-start.1 = (bf16[256,1280]{1,0:T(8,128)(2,1)}, bf16[256,1280]{1,0:T(8,128)(2,1)}, u32[]{:S(2)}, u32[]{:S(2)}) collective-permute-start(bf16[256,1280]{1,0:T(8,128)(2,1)} %bitcast.94), channel_id=1, source_target_pairs={{0,1},{1,2},{2,3},{3,4},{4,5},{5,6},{6,7},{7,8},{8,9},{9,10},{10,1... | collective-permute-start | bytes 1966088 | tf_op jit(solution)/shard_map/ppermute | solution.py:21
  14.0 4.9 %collective-permute-start = (bf16[256,1280]{1,0:T(8,128)(2,1)}, bf16[256,1280]{1,0:T(8,128)(2,1)}, u32[]{:S(2)}, u32[]{:S(2)}) collective-permute-start(bf16[256,1280]{1,0:T(8,128)(2,1)} %bitcast.95), channel_id=1, source_target_pairs={{0,2},{1,3},{2,4},{3,5},{4,6},{5,7},{6,8},{7,9},{8,10},{9,11},{10,... | collective-permute-start | bytes 1966088 | tf_op jit(solution)/shard_map/ppermute | solution.py:21
  18.9 2.4 copy.37
  22.0 0.1 copy.39
  22.1 0.1 reduce-window.9
  22.1 0.1 reduce
  22.3 0.1 convert_reduce_fusion
  22.4 0.0 copy-start.10
  22.4 4.4 %convolution_convert_fusion.4 = bf16[256,1280]{1,0:T(8,128)(2,1)} fusion(bf16[1280,1280]{1,0:T(8,128)(2,1)} %param.16, bf16[1,256,1280]{2,1,0:T(8,128)(2,1)} %param.12), kind=kOutput, calls=%fused_computation.26 | convolution fusion | flops 839188480 | bytes 4587520 | tf_op jit(solution)/shard_map/dot_general | solution.py:306
  26.8 2.2 copy.40
  29.0 0.1 slice_bitcast_fusion.2
  29.1 0.1 compare_select_fusion
  29.1 0.2 convert_reduce_fusion.1
  29.3 0.1 fusion.44
  29.4 0.3 fusion.36
  29.8 4.1 %convolution_convert_fusion.1 = bf16[256,1280]{1,0:T(8,128)(2,1)} fusion(bf16[1280,1280]{1,0:T(8,128)(2,1)} %param.17, bf16[1,256,1280]{2,1,0:T(8,128)(2,1)} %param.12), kind=kOutput, calls=%fused_computation.23 | convolution fusion | flops 839188480 | bytes 4587520 | tf_op jit(solution)/shard_map/dot_general | solution.py:307
  33.9 0.0 copy-done
  33.9 1.0 convolution_convert_fusion.5
  34.9 0.0 collective-permute-done.1
  34.9 2.1 convolution_convert_fusion.6
  37.0 19.2 %collective-permute-done = bf16[256,1280]{1,0:T(8,128)(2,1)} collective-permute-done((bf16[256,1280]{1,0:T(8,128)(2,1)}, bf16[256,1280]{1,0:T(8,128)(2,1)}, u32[]{:S(2)}, u32[]{:S(2)}) %collective-permute-start) | collective-permute-done | bytes 655392 | tf_op jit(solution)/shard_map/ppermute | solution.py:21
  56.3 2.1 convolution_convert_fusion.7
  58.4 0.1 pad_maximum_fusion
  58.5 2.5 copy.38
  61.1 3.3 %convolution_convert_fusion.2 = bf16[256,1280]{1,0:T(8,128)(2,1)S(1)} fusion(bf16[256,1280]{1,0:T(8,128)(2,1)} %collective-permute-done.1, bf16[1280,1280]{1,0:T(8,128)(2,1)} %param.17), kind=kOutput, calls=%fused_computation.24 | convolution fusion | flops 839188480 | bytes 4587520 | tf_op jit(solution)/shard_map/dot_general | solution.py:313
  64.4 0.0 copy-start.8
  64.4 2.2 convolution_convert_fusion.3
  66.6 0.0 copy-start.7
  66.6 0.1 pad_maximum_fusion.1
  66.7 2.5 copy.41
  69.2 8.0 %fusion.53 = (f32[10,256]{1,0:T(8,128)S(1)}, f32[10,256,768]{2,1,0:T(8,128)}) fusion(pred[256,768]{1,0:T(8,128)(4,1)S(1)} %fusion.36, bf16[256,10,128]{0,2,1:T(8,128)(2,1)S(1)} %bitcast.101, bf16[768,10,128]{0,2,1:T(8,128)(2,1)} %bitcast.97), kind=kOutput, calls=%fused_computation.99 | convolution fusion | flops 511181568 | bytes 10692608 | tf_op jit(solution)/shard_map/sub | solution.py:251
  77.2 6.5 %fusion.25 = (bf16[256,10,128]{0,2,1:T(8,128)(2,1)S(1)}, f32[10,128,256]{2,1,0:T(8,128)}) fusion(f32[256,10,128]{0,2,1:T(8,128)} %bitcast.100, bf16[768,10,128]{0,2,1:T(8,128)(2,1)S(1)} %bitcast.96, f32[10,256,768]{2,1,0:T(8,128)} %get-tuple-element.12, f32[10,256]{1,0:T(8,128)S(1)} %get-tuple-element.11), kind=kOutput, calls=%fused_computation.48 | convolution fusion | flops 507904000 | bytes 13117440 | tf_op jit(solution)/shard_map/hqk,khd->qhd/dot_general | solution.py:253
  83.7 1.8 copy.44
  85.5 0.3 fusion.28
  85.8 0.2 fusion.27
  86.0 0.3 fusion.54
  86.3 1.2 convolution_bitcast_fusion
  87.5 0.1 fusion.39
  87.6 0.1 broadcast_in_dim.49
  87.7 30.2 %all_to_all.5 = bf16[8,1,64,1280]{3,2,1,0:T(8,128)(2,1)S(1)} all-to-all(bf16[8,1,64,1280]{3,2,1,0:T(8,128)(2,1)S(1)} %broadcast_in_dim.49), channel_id=1, replica_groups=mesh['seq'=8,'fsdp'=16] {'seq'}, dimensions={0} | all-to-all | bytes 2621440 | tf_op jit(solution)/shard_map/all_to_all | solution.py:32
  117.9 8.4 %multiply_reduce_fusion = (f32[512]{0:T(512)S(1)}, f32[512,4096]{1,0:T(8,128)S(1)}) fusion(bf16[512,1280]{1,0:T(8,128)(2,1)S(1)} %bitcast.99, bf16[1280,4096]{1,0:T(8,128)(2,1)} %param.19), kind=kOutput, calls=%fused_computation.4 | convolution fusion | flops 5377097216 | bytes 20187136 | tf_op jit(solution)/shard_map/dot_general | solution.py:333
  126.3 0.0 copy-start.2
  126.3 3.3 %copy-done.2 = f32[512,4096]{1,0:T(8,128)} copy-done((f32[512,4096]{1,0:T(8,128)}, f32[512,4096]{1,0:T(8,128)S(1)}, u32[]{:S(2)}) %copy-start.2) | copy-done | bytes 8388632
  129.6 0.0 copy-done.9
  129.6 3.4 %multiply_convert_fusion.normed_ref = bf16[512,4096]{1,0:T(8,128)(2,1)} fusion(f32[512,4096]{1,0:T(8,128)S(1)} %get-tuple-element.16, f32[4096]{0:T(1024)S(1)} %copy-done.9, f32[512]{0:T(512)S(1)} %add_rsqrt_fusion), kind=kLoop, calls=%fused_computation.3 | loop fusion | flops 6291456 | bytes 12601344 | tf_op jit(solution)/shard_map/convert_element_type | solution.py:338
  133.0 10.2 %fusion.8 = f32[512,896]{1,0:T(8,128)S(1)} fusion(bf16[512,4096]{1,0:T(8,128)(2,1)} %multiply_convert_fusion.normed_ref, bf16[4096,1792]{1,0:T(8,128)(2,1)} %all-gather.2.cloned.1.call-done), kind=kOutput, calls=%fused_computation.14 | convolution fusion | flops 3758096384 | bytes 13369344 | tf_op jit(solution)/shard_map/dot_general | solution.py:340
  143.3 0.1 copy-done.12
  143.4 6.1 %fusion.21 = (bf16[512,896]{1,0:T(8,128)(2,1)S(1)}, bf16[512,896]{1,0:T(8,128)(2,1)}, bf16[512,896]{1,0:T(8,128)(2,1)S(1)}) fusion(f32[512,896]{1,0:T(8,128)S(1)} %fusion.8, bf16[8,64,896]{2,1,0:T(8,128)(2,1)S(1)} %copy-done.14, bf16[512,4096]{1,0:T(8,128)(2,1)S(1)} %copy-done.3, bf16[4096,1792]{1,0:T(8,128)(2,1)S(1)} %copy-done.12), kind=kOutput, calls=%fused_computation.38 | convolution fusion | flops 3765895168 | bytes 17039360 | tf_op jit(solution)/shard_map/dot_general | solution.py:341
  149.5 6.7 %fusion.2 = f32[512,4096]{1,0:T(8,128)} fusion(bf16[512,896]{1,0:T(8,128)(2,1)S(1)} %get-tuple-element.8, bf16[4096,1792]{1,0:T(8,128)(2,1)S(1)} %copy-done.12), kind=kOutput, calls=%fused_computation.8 | convolution fusion | flops 3758096384 | bytes 16646144 | tf_op jit(solution)/shard_map/dot_general | solution.py:354
  156.2 10.4 %add_convert_fusion = bf16[512,4096]{1,0:T(8,128)(2,1)} fusion(f32[512,4096]{1,0:T(8,128)} %fusion.2, bf16[512,896]{1,0:T(8,128)(2,1)S(1)} %get-tuple-element.6, bf16[4096,1792]{1,0:T(8,128)(2,1)} %all-gather.2.cloned.1.call-done), kind=kOutput, calls=%fused_computation.2 | convolution fusion | flops 3762290688 | bytes 20840448 | tf_op jit(solution)/shard_map/dot_general | solution.py:351
  166.6 0.0 reduce-scatter.2.cloned.1.call-update
  166.6 0.1 rsqrt.19
  166.7 0.1 pad_maximum_fusion.2.grads_ref
  166.9 0.0 copy-start.1
  166.9 84.6 %grad_rings.1 = f32[2,256,896]{2,1,0:T(8,128)S(1)} custom-call(bf16[512,4096]{1,0:T(8,128)(2,1)} %multiply_convert_fusion.normed_ref, bf16[512,1792]{1,0:T(8,128)(2,1)S(1)} %pad_maximum_fusion.2.grads_ref), custom_call_target="tpu_custom_call" | custom-call | flops 7516192768 | bytes 200000000 | tf_op jit(solution)/shard_map/grad_rings/pallas_call | solution.py:203
  251.5 1.3 slice_bitcast_fusion
  252.8 1.6 fusion.33
  254.5 2.6 fusion.30
  (32 shorter events, 0.1 us)
Async XLA Ops:
  7.2 26.7 %copy-start = (bf16[1280,1280]{1,0:T(8,128)(2,1)S(1)}, bf16[1280,1280]{1,0:T(8,128)(2,1)}, u32[]{:S(2)}) copy-start(bf16[1280,1280]{1,0:T(8,128)(2,1)} %param.18) | copy-start | bytes 9830404
  7.2 14.8 %copy-start.11 = (s32[32]{0:T(128)S(1)}, s32[32]{0:T(128)}, u32[]{:S(2)}) copy-start(s32[32]{0:T(128)} %param.13) | copy-start | bytes 388
  7.2 125.8 %all-gather.2.cloned.1.call-start = ((), (), s32[]{:S(2)}) async-start(), calls=%async_computation.2 | async-start | bytes 15597568 | tf_op jit(solution)/shard_map/all_gather | solution.py:41
  9.6 243.3 %reduce-scatter.2.cloned.1.call-start = ((), (), s32[]{:S(2)}) async-start(), calls=%async_computation.3 | async-start | bytes 4718592 | tf_op jit(solution)/shard_map/reduce_scatter | solution.py:357
  9.6 25.3 %collective-permute-start.1 = (bf16[256,1280]{1,0:T(8,128)(2,1)}, bf16[256,1280]{1,0:T(8,128)(2,1)}, u32[]{:S(2)}, u32[]{:S(2)}) collective-permute-start(bf16[256,1280]{1,0:T(8,128)(2,1)} %bitcast.94), channel_id=1, source_target_pairs={{0,1},{1,2},{2,3},{3,4},{4,5},{5,6},{6,7},{7,8},{8,9},{9,10},{10,1... | collective-permute-start | bytes 1966088 | tf_op jit(solution)/shard_map/ppermute | solution.py:21
  14.0 42.2 %collective-permute-start = (bf16[256,1280]{1,0:T(8,128)(2,1)}, bf16[256,1280]{1,0:T(8,128)(2,1)}, u32[]{:S(2)}, u32[]{:S(2)}) collective-permute-start(bf16[256,1280]{1,0:T(8,128)(2,1)} %bitcast.95), channel_id=1, source_target_pairs={{0,2},{1,3},{2,4},{3,5},{4,6},{5,7},{6,8},{7,9},{8,10},{9,11},{10,... | collective-permute-start | bytes 1966088 | tf_op jit(solution)/shard_map/ppermute | solution.py:21
  22.4 6.6 %copy-start.10 = (s32[1,64]{1,0:T(1,128)S(1)}, s32[1,64]{1,0:T(1,128)}, u32[]{:S(2)}) copy-start(s32[1,64]{1,0:T(1,128)} %param.14) | copy-start | bytes 772
  29.0 4.9 %copy-start.4 = (bf16[1,256,1280]{2,1,0:T(8,128)(2,1)S(1)}, bf16[1,256,1280]{2,1,0:T(8,128)(2,1)}, u32[]{:S(2)}) copy-start(bf16[1,256,1280]{2,1,0:T(8,128)(2,1)} %param.12) | copy-start | bytes 1966084
  61.0 3.3 %copy-start.13 = (bf16[1280,1280]{1,0:T(8,128)(2,1)S(1)}, bf16[1280,1280]{1,0:T(8,128)(2,1)}, u32[]{:S(2)}) copy-start(bf16[1280,1280]{1,0:T(8,128)(2,1)} %param.17) | copy-start | bytes 9830404
  64.4 2.2 copy-start.8
  66.6 2.6 copy-start.7
  69.2 8.0 %copy-start.6 = (bf16[768,1280]{0,1:T(8,128)(2,1)S(1)}, bf16[768,1280]{0,1:T(8,128)(2,1)}, u32[]{:S(2)}) copy-start(bf16[768,1280]{0,1:T(8,128)(2,1)} %copy.38) | copy-start | bytes 5898244
  77.2 8.2 %copy-start.5 = (bf16[1,256,1280]{2,1,0:T(8,128)(2,1)S(1)}, bf16[1,256,1280]{2,1,0:T(8,128)(2,1)}, u32[]{:S(2)}) copy-start(bf16[1,256,1280]{2,1,0:T(8,128)(2,1)} %param.12) | copy-start | bytes 1966084
  117.9 11.7 %copy-start.9 = (f32[4096]{0:T(1024)S(1)}, f32[4096]{0:T(1024)}, u32[]{:S(2)}) copy-start(f32[4096]{0:T(1024)} %param.20) | copy-start | bytes 49156
  126.3 3.3 %copy-start.2 = (f32[512,4096]{1,0:T(8,128)}, f32[512,4096]{1,0:T(8,128)S(1)}, u32[]{:S(2)}) copy-start(f32[512,4096]{1,0:T(8,128)S(1)} %get-tuple-element.16) | copy-start | bytes 25165828
  133.0 10.3 %copy-start.14 = (bf16[8,64,896]{2,1,0:T(8,128)(2,1)S(1)}, bf16[8,64,896]{2,1,0:T(8,128)(2,1)}, u32[]{:S(2)}) copy-start(bf16[8,64,896]{2,1,0:T(8,128)(2,1)} %param.23) | copy-start | bytes 2752516
  133.0 10.3 %copy-start.3 = (bf16[512,4096]{1,0:T(8,128)(2,1)S(1)}, bf16[512,4096]{1,0:T(8,128)(2,1)}, u32[]{:S(2)}) copy-start(bf16[512,4096]{1,0:T(8,128)(2,1)} %multiply_convert_fusion.normed_ref) | copy-start | bytes 12582916
  133.0 10.4 %copy-start.12 = (bf16[4096,1792]{1,0:T(8,128)(2,1)S(1)}, bf16[4096,1792]{1,0:T(8,128)(2,1)}, u32[]{:S(2)}) copy-start(bf16[4096,1792]{1,0:T(8,128)(2,1)} %all-gather.2.cloned.1.call-done) | copy-start | bytes 44040196
  166.9 90.2 %copy-start.1 = (bf16[1280,1280]{1,0:T(8,128)(2,1)S(1)}, bf16[1280,1280]{1,0:T(8,128)(2,1)}, u32[]{:S(2)}) copy-start(bf16[1280,1280]{1,0:T(8,128)(2,1)} %param.18) | copy-start | bytes 9830404
Sparse Core Ops, SparseCore 0:
  10.7 120.0 all-gather.1
  166.8 36.5 reduce-scatter.1

commit v2 on v1

--- a/solution.py
+++ b/solution.py
@@ -15,10 +15,15 @@
 masked_score = -1e30
 
 
-def shifted(shard, axis, by):
-    devices = lax.axis_size(axis)
-    pairs = [(i, i + by) for i in range(devices) if 0 <= i + by < devices]
-    return lax.ppermute(shard, axis, pairs)
+def from_earlier(shard, by):
+    axes = ("seq", "fsdp")
+    devices = lax.axis_size(axes)
+    pairs = [(i, i + by) for i in range(devices) if i + by < devices]
+    if by == 2:
+        via = [i - i % SIDE + (i - 1) % SIDE for i in range(devices)]
+        shard = lax.ppermute(shard, axes, [(i, via[i]) for i in range(devices)])
+        pairs = [(via[i], j) for i, j in pairs if via[i] != j]
+    return lax.ppermute(shard, axes, pairs)
 
 
 def laid_out(pieces, dim):
@@ -36,27 +41,6 @@
     return laid_out(copy_for_each(shard, axis), dim)
 
 
-def in_one_piece(arrays, axis, dim, along):
-    both = jnp.concatenate(arrays, axis=along)
-    filled, at, finished = (lax.all_gather(both, axis, axis=dim, tiled=True), 0, [])
-    for a in arrays:
-        finished.append(lax.slice_in_dim(filled, at, at + a.shape[along], axis=along))
-        at += a.shape[along]
-    return tuple(finished)
-
-
-def in_blocks(shard, dim, devices):
-    lengths = shard.shape
-    pieces = shard.reshape(*lengths[:dim], devices, lengths[dim] // devices, *lengths[dim + 1 :])
-    return jnp.moveaxis(pieces, dim, 0)
-
-
-def summed_on_arrival(shard, axis, dim):
-    pieces = in_blocks(shard, dim, lax.axis_size(axis))
-    arrived = lax.all_to_all(pieces, axis, split_axis=0, concat_axis=0, tiled=True)
-    return arrived.astype(jnp.float32).sum(axis=0)
-
-
 MESH = pl.DeviceIdType.MESH
 SIDE = 4
 
@@ -66,23 +50,52 @@
 
 
 def grad_rings(
-    normed_ref, grads_ref, out_ref, first, arrived, second, crossed, put, got, put2, got2
+    normed_ref,
+    grads_ref,
+    weights_hbm,
+    out_ref,
+    inward_ref,
+    first,
+    arrived,
+    second,
+    crossed,
+    weights,
+    parts,
+    paired,
+    ringed,
+    put,
+    got,
+    put2,
+    got2,
+    loaded,
+    put3,
+    got3,
+    put4,
+    got4,
 ):
     seq = lax.axis_index("seq")
     spot = lax.axis_index("fsdp")
+    x, core = lax.div(seq, 2), lax.rem(seq, 2)
     z, y = lax.div(spot, SIDE), lax.rem(spot, SIDE)
     rows = first.shape[2]
     units = out_ref.shape[2]
-
+    chunks, _, _, slots, wide = parts.shape
+
+    load = pltpu.make_async_copy(weights_hbm, weights, loaded)
+    load.start()
+
+    around = (
+        (seq, wrapped(z + 1) * SIDE + y),
+        (seq, wrapped(z - 1) * SIDE + y),
+        (seq, z * SIDE + wrapped(y + 1)),
+        (seq, z * SIDE + wrapped(y - 1)),
+        (wrapped(x + 1) * 2 + core, spot),
+        (wrapped(x - 1) * 2 + core, spot),
+        (x * 2 + 1 - core, spot),
+    )
     barrier = pltpu.get_barrier_semaphore()
-    around = (
-        wrapped(z + 1) * SIDE + y,
-        wrapped(z - 1) * SIDE + y,
-        z * SIDE + wrapped(y + 1),
-        z * SIDE + wrapped(y - 1),
-    )
     for neighbour in around:
-        pl.semaphore_signal(barrier, inc=1, device_id=(seq, neighbour), device_id_type=MESH)
+        pl.semaphore_signal(barrier, inc=1, device_id=neighbour, device_id_type=MESH)
     pl.semaphore_wait(barrier, len(around))
 
     def place(stream):
@@ -109,24 +122,42 @@
         )
 
     def hop(stream, source, t, k):
-        onward = place(stream)[5]
         return pltpu.make_async_remote_copy(
             src_ref=source,
             dst_ref=arrived.at[stream, t, k],
             send_sem=put.at[stream, t, k],
             recv_sem=got.at[stream, t, k],
-            device_id=(seq, onward),
+            device_id=place(stream)[5],
             device_id_type=MESH,
         )
 
     def hop2(stream, source, k):
-        sideways = place(stream)[6]
         return pltpu.make_async_remote_copy(
             src_ref=source,
             dst_ref=crossed.at[stream, k],
             send_sem=put2.at[stream, k],
             recv_sem=got2.at[stream, k],
-            device_id=(seq, sideways),
+            device_id=place(stream)[6],
+            device_id_type=MESH,
+        )
+
+    def across_cores(n):
+        return pltpu.make_async_remote_copy(
+            src_ref=parts.at[n, 1 - core],
+            dst_ref=paired.at[n],
+            send_sem=put3.at[n],
+            recv_sem=got3.at[n],
+            device_id=around[6],
+            device_id_type=MESH,
+        )
+
+    def x_hop(side, n, source, t):
+        return pltpu.make_async_remote_copy(
+            src_ref=source,
+            dst_ref=ringed.at[t, n],
+            send_sem=put4.at[t, n],
+            recv_sem=got4.at[t, n],
+            device_id=around[4 + side],
             device_id_type=MESH,
         )
 
@@ -137,19 +168,60 @@
         return carry
 
     lax.fori_loop(0, SIDE, opening, 0)
-
-    def middle(index, carry):
-        t, k = lax.div(index, SIDE) + 1, lax.rem(index, SIDE)
-        for stream in range(4):
-            value = own(stream, t, k)
-            hop(stream, first.at[stream, k], t - 1, k).wait_recv()
-            arrived[stream, t - 1, k] = (
-                value + arrived[stream, t - 1, k].astype(jnp.float32)
-            ).astype(jnp.bfloat16)
-            hop(stream, arrived.at[stream, t - 1, k], t, k).start()
-        return carry
-
-    lax.fori_loop(0, 2 * SIDE, middle, 0)
+    load.wait()
+
+    def input_part(n):
+        at = pl.multiple_of(n * wide, wide)
+        value = lax.dot_general(
+            grads_ref[...],
+            weights[pl.ds(at, wide), :],
+            (((1,), (1,)), ((), ())),
+            preferred_element_type=jnp.float32,
+        ).astype(jnp.bfloat16)
+        for block in range(2 * SIDE):
+            parts[n, block % 2, block // 2] = value[block * slots : (block + 1) * slots]
+        across_cores(n).start()
+
+    def middle(t, busy):
+        def body(k, carry):
+            for stream in range(4):
+                value = own(stream, t, k)
+                hop(stream, first.at[stream, k], t - 1, k).wait_recv()
+                arrived[stream, t - 1, k] = (
+                    value + arrived[stream, t - 1, k].astype(jnp.float32)
+                ).astype(jnp.bfloat16)
+                hop(stream, arrived.at[stream, t - 1, k], t, k).start()
+            if busy:
+                input_part(2 * k)
+                input_part(2 * k + 1)
+            return carry
+
+        lax.fori_loop(0, SIDE, body, 0)
+
+    def x_phase(t):
+        def body(m, carry):
+            for side in range(2):
+                n = 2 * m + side
+                block = wrapped(x - (1 - 2 * side) * (1 + t))
+                if t == 0:
+                    across_cores(n).wait_recv()
+                    paired[n] = (
+                        paired[n].astype(jnp.float32) + parts[n, core].astype(jnp.float32)
+                    ).astype(jnp.bfloat16)
+                    x_hop(side, n, paired.at[n, block], 0).start()
+                else:
+                    x_hop(side, n, paired.at[n, block], t - 1).wait_recv()
+                    value = ringed[t - 1, n].astype(jnp.float32) + paired[n, block].astype(
+                        jnp.float32
+                    )
+                    if t < SIDE - 1:
+                        ringed[t - 1, n] = value.astype(jnp.bfloat16)
+                        x_hop(side, n, ringed.at[t - 1, n], t).start()
+                    else:
+                        inward_ref[n] = value
+            return carry
+
+        lax.fori_loop(0, chunks // 2, body, 0)
 
     last = SIDE - 1
 
@@ -158,9 +230,15 @@
         hop(stream, first.at[stream, k], last - 1, k).wait_recv()
         return value + arrived[stream, last - 1, k].astype(jnp.float32)
 
+    middle(1, True)
+    x_phase(0)
+    middle(2, False)
+    x_phase(1)
+
     for stream in range(4):
         second[stream] = total(stream, 0).astype(jnp.bfloat16)
         hop2(stream, second.at[stream], 0).start()
+    x_phase(2)
 
     def crossing(k, carry):
         for stream in range(4):
@@ -173,6 +251,7 @@
         return carry
 
     lax.fori_loop(1, last, crossing, 0)
+    x_phase(3)
 
     for stream in range(4):
         kind, half = stream // 2, stream % 2
@@ -193,38 +272,62 @@
         for k in range(last):
             hop2(stream, second.at[stream], k).wait_send()
 
-
-def weight_grads(normed, grads):
+    def x_sent(m, carry):
+        for side in range(2):
+            n = 2 * m + side
+            across_cores(n).wait_send()
+            for t in range(last):
+                x_hop(side, n, ringed.at[0, n], t).wait_send()
+        return carry
+
+    lax.fori_loop(0, chunks // 2, x_sent, 0)
+
+
+def grad_sums(normed, grads, weights, slots):
     tokens, width = normed.shape
     units = grads.shape[1] // 2
     rows = width // (SIDE * SIDE)
     half = rows // 2
     block = (half, units)
+    chunks, wide = 8, width // 8
+    whole = pl.BlockSpec(memory_space=pltpu.VMEM)
     return pl.pallas_call(
         grad_rings,
-        out_shape=jax.ShapeDtypeStruct((2, rows, units), jnp.float32),
-        in_specs=[pl.BlockSpec(memory_space=pltpu.VMEM)] * 2,
-        out_specs=pl.BlockSpec(memory_space=pltpu.VMEM),
+        out_shape=(
+            jax.ShapeDtypeStruct((2, rows, units), jnp.float32),
+            jax.ShapeDtypeStruct((chunks, slots, wide), jnp.float32),
+        ),
+        in_specs=[whole, whole, pl.BlockSpec(memory_space=pl.ANY)],
+        out_specs=(whole, whole),
         scratch_shapes=[
             pltpu.VMEM((4, SIDE, *block), jnp.bfloat16),
             pltpu.VMEM((4, SIDE - 1, SIDE, *block), jnp.bfloat16),
             pltpu.VMEM((4, *block), jnp.bfloat16),
             pltpu.VMEM((4, SIDE - 1, *block), jnp.bfloat16),
+            pltpu.VMEM(weights.shape, jnp.bfloat16),
+            pltpu.VMEM((chunks, 2, SIDE, slots, wide), jnp.bfloat16),
+            pltpu.VMEM((chunks, SIDE, slots, wide), jnp.bfloat16),
+            pltpu.VMEM((SIDE - 1, chunks, slots, wide), jnp.bfloat16),
             pltpu.SemaphoreType.DMA((4, SIDE - 1, SIDE)),
             pltpu.SemaphoreType.DMA((4, SIDE - 1, SIDE)),
             pltpu.SemaphoreType.DMA((4, SIDE - 1)),
             pltpu.SemaphoreType.DMA((4, SIDE - 1)),
+            pltpu.SemaphoreType.DMA(()),
+            pltpu.SemaphoreType.DMA((chunks,)),
+            pltpu.SemaphoreType.DMA((chunks,)),
+            pltpu.SemaphoreType.DMA((SIDE - 1, chunks)),
+            pltpu.SemaphoreType.DMA((SIDE - 1, chunks)),
         ],
         compiler_params=pltpu.CompilerParams(
-            collective_id=0, has_side_effects=True, vmem_limit_bytes=48 * 1024 * 1024
+            collective_id=0, has_side_effects=True, vmem_limit_bytes=60 * 1024 * 1024
         ),
         cost_estimate=pl.CostEstimate(
-            flops=2 * tokens * width * 2 * units,
+            flops=4 * tokens * width * 2 * units,
             bytes_accessed=200_000_000,
             transcendentals=0,
         ),
         name="grad_rings",
-    )(normed, grads)
+    )(normed, grads, weights)
 
 
 def doc_index(doc_lengths, positions):
@@ -309,7 +412,7 @@
     key_parts = [key_rows]
     value_parts = [values]
     for distance in range(1, hop_count + 1):
-        earlier = shifted(states, ("seq", "fsdp"), distance)
+        earlier = from_earlier(states, distance)
         earlier_keys = jnp.dot(earlier, w_key, preferred_element_type=jnp.float32).astype(
             jnp.bfloat16
         )
@@ -336,32 +439,23 @@
     patch_float = features.reshape(seq_count * slot_count, model_width).astype(jnp.float32)
     inverse = lax.rsqrt(jnp.mean(patch_float * patch_float, axis=1, keepdims=True) + epsilon)
     normed = (patch_float * inverse * norm_gain).astype(jnp.bfloat16)
-    gate_full, up_full = in_one_piece((gate_w, up_w), "fsdp", 0, 1)
-    gate_pre = jnp.dot(normed, gate_full, preferred_element_type=jnp.float32)
-    up_pre = jnp.dot(normed, up_full, preferred_element_type=jnp.float32)
+    units = gate_w.shape[1]
+    weights = lax.all_gather(
+        jnp.concatenate((gate_w, up_w), axis=1), "fsdp", axis=0, tiled=True
+    )
+    gate_pre = jnp.dot(normed, weights[:, :units], preferred_element_type=jnp.float32)
+    up_pre = jnp.dot(normed, weights[:, units:], preferred_element_type=jnp.float32)
     sigmoid_gate = jax.nn.sigmoid(gate_pre)
     hidden = (gate_pre * sigmoid_gate * up_pre).astype(jnp.bfloat16)
-    units = gate_w.shape[1]
     cotangent = d_hidden.reshape(seq_count * slot_count, units).astype(jnp.float32)
     gate_grad = (
         cotangent * up_pre * sigmoid_gate * (1.0 + gate_pre * (1.0 - sigmoid_gate))
     ).astype(jnp.bfloat16)
     up_grad = (cotangent * gate_pre * sigmoid_gate).astype(jnp.bfloat16)
     both_grads = jnp.concatenate([gate_grad, up_grad], axis=1)
-    input_partial = lax.dot_general(
-        gate_grad, gate_full, (((1,), (1,)), ((), ())), preferred_element_type=jnp.float32
-    )
-    input_partial = input_partial + lax.dot_general(
-        up_grad, up_full, (((1,), (1,)), ((), ())), preferred_element_type=jnp.float32
-    )
-    normed_grad = lax.psum_scatter(
-        input_partial.reshape(seq_count, slot_count, model_width).astype(jnp.bfloat16),
-        "seq",
-        scatter_dimension=0,
-        tiled=True,
-    )[0].astype(jnp.float32)
-    totals = weight_grads(normed, both_grads)
+    totals, inward = grad_sums(normed, both_grads, weights, slot_count)
     grad_gate, grad_up = totals[0], totals[1]
+    normed_grad = laid_out(inward, 1)
     own_float = lax.dynamic_index_in_dim(
         patch_float.reshape(seq_count, slot_count, model_width), seq_index, 0, keepdims=False
     )

time: 264 us -> 260 us (0.985); the launches traced: 264 us -> 256 us
  blocking collectives: 30.2 us -> 0 us
  waiting for transfers between devices: 19.3 us -> 35.5 us
  matrix products: 77.2 us -> 62.6 us
  starting transfers between devices: 9.37 us -> 20 us
  other arithmetic: 11.8 us -> 16.1 us
  Pallas kernels: 84.6 us -> 87.7 us
    all_to_all x1 -> x0, blocking collectives: 30.2 us -> none  [copy_for_each(): return lax.all_to_all(copies, axis, split_axis=0, concat_axis=0, tiled=True)]
    all_to_all x0 -> x1, waiting for transfers between devices: none -> 18.7 us  [copy_for_each(): return lax.all_to_all(copies, axis, split_axis=0, concat_axis=0, tiled=True)]
    dot_general x4 -> x2, matrix products: 33.4 us -> 16.3 us  [the longest x1 10.2 us: shards(): jnp.dot(normed, weights[:, :units], preferred_element_type=jnp.float32)]
    all_to_all x0 -> x1, starting transfers between devices: none -> 7.17 us  [copy_for_each(): return lax.all_to_all(copies, axis, split_axis=0, concat_axis=0, tiled=True)]
    ppermute x2 -> x3, starting transfers between devices: 9.29 us -> 12.8 us  [the longest x2 10.5 us: from_earlier(): return lax.ppermute(shard, axes, pairs)]
    dot_general x1, matrix products: 8.44 us -> 11.9 us  [shards(): jnp.dot(flat_part, w_proj, preferred_element_type=jnp.float32)]
    convert_element_type x1, other arithmetic: 3.42 us -> 6.74 us  [shards(): normed = (patch_float * inverse * norm_gain).astype(jnp.bfloat16)]
    pallas_call x1, Pallas kernels: 84.6 us -> 87.7 us  [grad_sums(): pl.pallas_call(grad_rings, out_shape=(jax.ShapeDtypeStruct((2, rows, unit...]
  transfers between devices with their start and end apart: 4 -> 5, of which waited for: 1 -> 3; matrix products, arithmetic and copies ran while one was open for 24% -> 26% of each run, Pallas kernels for 32% -> 0%
where the time goes in v2:
time: 260 us; the launch traced here: 256 us
  Pallas kernels  87.7 us (34%)
  matrix products  62.6 us (24%)
  waiting for transfers between devices  35.5 us (14%)
  starting transfers between devices  20 us (8%)
  local copies, waits for them, and re-layouts  18.5 us (7%)
  other arithmetic  16.1 us (6%)
  between operations  15.3 us (6%)
    pallas_call x1, Pallas kernels, grad_sums(): pl.pallas_call(grad_rings, out_shape=(jax.ShapeDtypeStruct((2, rows, unit...  87.7 us
    all_to_all x1, waiting for transfers between devices, copy_for_each(): return lax.all_to_all(copies, axis, split_axis=0, concat_axis=0, tiled=True)  18.7 us
    dot_general x1, matrix products, shards(): jnp.dot(flat_part, w_proj, preferred_element_type=jnp.float32)  11.9 us
    ppermute x2, starting transfers between devices, from_earlier(): return lax.ppermute(shard, axes, pairs)  10.5 us
    ppermute x2, waiting for transfers between devices, from_earlier(): return lax.ppermute(shard, axes, pairs)  10.4 us
    dot_general x1, matrix products, shards(): jnp.dot(normed, weights[:, :units], preferred_element_type=jnp.float32)  10.2 us
    sub x1, matrix products, window_attention(): weights = jnp.exp(scores - row_max)  7.81 us
    all_to_all x1, starting transfers between devices, copy_for_each(): return lax.all_to_all(copies, axis, split_axis=0, concat_axis=0, tiled=True)  7.17 us
  transfers between devices with their start and end apart: 5, of which 3 were waited for; matrix products, arithmetic and copies ran while one was open for 26% of the time, Pallas kernels for 0%

profile of v2, /device:TPU:0, one launch (start us, length us, event | category | flops | bytes accessed | tf_op | source)
XLA Modules:
  0.0 255.7 jit_solution(5252825429928196837)
XLA Ops:
  7.2 0.0 copy-start
  7.2 0.0 all-gather.2.cloned.1.call-start
  7.2 2.3 pad_maximum_fusion.3
  9.5 0.0 all-gather.2.cloned.1.call-update
  9.6 4.4 %collective-permute-start.2 = (bf16[256,1280]{1,0:T(8,128)(2,1)}, bf16[256,1280]{1,0:T(8,128)(2,1)}, u32[]{:S(2)}, u32[]{:S(2)}) collective-permute-start(bf16[256,1280]{1,0:T(8,128)(2,1)} %bitcast.90), channel_id=1, source_target_pairs={{0,1},{1,2},{2,3},{3,4},{4,5},{5,6},{6,7},{7,8},{8,9},{9,10},{10,1... | collective-permute-start | bytes 1966088 | tf_op jit(solution)/shard_map/ppermute | solution.py:26
  14.0 2.2 collective-permute-start
  16.2 2.5 copy.39
  18.7 0.1 copy.41
  18.8 0.1 reduce-window.9
  18.8 0.1 reduce
  19.0 0.1 convert_reduce_fusion
  19.1 0.0 copy-start.13
  19.1 4.0 %convolution_convert_fusion.4 = bf16[256,1280]{1,0:T(8,128)(2,1)} fusion(bf16[1280,1280]{1,0:T(8,128)(2,1)} %param.16, bf16[1,256,1280]{2,1,0:T(8,128)(2,1)} %param.12), kind=kOutput, calls=%fused_computation.21 | convolution fusion | flops 839188480 | bytes 4587520 | tf_op jit(solution)/shard_map/dot_general | solution.py:409
  23.1 2.3 copy.42
  26.0 0.0 copy-start.5
  26.0 0.0 copy-start.16
  26.0 0.1 slice_bitcast_fusion.2
  26.1 0.1 compare_select_fusion
  26.2 0.2 convert_reduce_fusion.1
  26.4 0.1 fusion.34
  26.5 0.3 fusion.26
  26.9 2.4 convolution_convert_fusion.5
  29.3 1.9 convolution_convert_fusion.1
  31.2 6.4 %collective-permute-done = bf16[256,1280]{1,0:T(8,128)(2,1)} collective-permute-done((bf16[256,1280]{1,0:T(8,128)(2,1)}, bf16[256,1280]{1,0:T(8,128)(2,1)}, u32[]{:S(2)}, u32[]{:S(2)}) %collective-permute-start) | collective-permute-done | bytes 655392 | tf_op jit(solution)/shard_map/ppermute | solution.py:24
  37.5 6.1 %collective-permute-start.1 = (bf16[256,1280]{1,0:T(8,128)(2,1)}, bf16[256,1280]{1,0:T(8,128)(2,1)S(1)}, u32[]{:S(2)}, u32[]{:S(2)}) collective-permute-start(bf16[256,1280]{1,0:T(8,128)(2,1)} %collective-permute-done), channel_id=1, source_target_pairs={{3,2},{0,3},{1,4},{2,5},{7,6},{4,7},{5,8},{6,9},{11,10},{8,11},{9,... | collective-permute-start | bytes 1966088 | tf_op jit(solution)/shard_map/ppermute | solution.py:26
  43.6 0.0 collective-permute-done.2
  43.6 2.1 convolution_convert_fusion.6
  45.7 2.9 %convolution_convert_fusion.2 = bf16[256,1280]{1,0:T(8,128)(2,1)} fusion(bf16[256,1280]{1,0:T(8,128)(2,1)} %collective-permute-done.2, bf16[1280,1280]{1,0:T(8,128)(2,1)S(1)} %copy-done.16), kind=kOutput, calls=%fused_computation.19 | convolution fusion | flops 839188480 | bytes 4587520 | tf_op jit(solution)/shard_map/dot_general | solution.py:416
  48.7 10.4 %collective-permute-done.1 = bf16[256,1280]{1,0:T(8,128)(2,1)S(1)} collective-permute-done((bf16[256,1280]{1,0:T(8,128)(2,1)}, bf16[256,1280]{1,0:T(8,128)(2,1)S(1)}, u32[]{:S(2)}, u32[]{:S(2)}) %collective-permute-start.1) | collective-permute-done | bytes 655392 | tf_op jit(solution)/shard_map/ppermute | solution.py:26
  59.0 0.9 copy-done.18
  59.9 1.0 convolution_convert_fusion.7
  60.9 0.1 pad_maximum_fusion
  61.1 2.4 copy.40
  63.5 3.0 %convolution_convert_fusion.3 = bf16[256,1280]{1,0:T(8,128)(2,1)S(1)} fusion(bf16[256,1280]{1,0:T(8,128)(2,1)S(1)} %copy-done.19, bf16[1280,1280]{1,0:T(8,128)(2,1)} %param.17), kind=kOutput, calls=%fused_computation.20 | convolution fusion | flops 839188480 | bytes 4587520 | tf_op jit(solution)/shard_map/dot_general | solution.py:416
  66.5 0.0 copy-start.8
  66.5 0.1 pad_maximum_fusion.1
  66.7 2.5 copy.43
  69.1 0.0 copy-done.8
  69.1 7.8 %fusion.43 = (f32[10,256]{1,0:T(8,128)S(1)}, f32[10,256,768]{2,1,0:T(8,128)}) fusion(pred[256,768]{1,0:T(8,128)(4,1)S(1)} %fusion.26, bf16[256,10,128]{0,2,1:T(8,128)(2,1)S(1)} %bitcast.97, bf16[768,10,128]{0,2,1:T(8,128)(2,1)} %bitcast.93), kind=kOutput, calls=%fused_computation.90 | convolution fusion | flops 511181568 | bytes 10692608 | tf_op jit(solution)/shard_map/sub | solution.py:354
  77.0 6.5 %fusion.19 = (bf16[256,10,128]{0,2,1:T(8,128)(2,1)}, f32[10,128,256]{2,1,0:T(8,128)S(1)}) fusion(f32[256,10,128]{0,2,1:T(8,128)S(1)} %bitcast.96, bf16[768,10,128]{0,2,1:T(8,128)(2,1)} %bitcast.92, f32[10,256,768]{2,1,0:T(8,128)} %get-tuple-element.16, f32[10,256]{1,0:T(8,128)S(1)} %get-tuple-element.15), kind=kOutput, calls=%fused_computation.41 | convolution fusion | flops 507904000 | bytes 13117440 | tf_op jit(solution)/shard_map/hqk,khd->qhd/dot_general | solution.py:356
  83.4 0.4 copy.46
  83.8 0.0 copy-start.9
  83.9 0.3 fusion.22
  84.1 1.3 fusion.21
  85.5 0.3 fusion.44
  85.8 1.2 convolution_bitcast_fusion
  86.9 0.1 fusion.29
  87.1 1.2 broadcast_in_dim.49
  88.2 7.2 %all-to-all-start = ((bf16[8,1,64,1280]{3,2,1,0:T(8,128)(2,1)}), bf16[8,1,64,1280]{3,2,1,0:T(8,128)(2,1)S(1)}, u32[]{:S(2)}, u32[]{:S(2)}) async-start(bf16[8,1,64,1280]{3,2,1,0:T(8,128)(2,1)} %broadcast_in_dim.49), calls=%async_computation | async-start | bytes 2621440 | tf_op jit(solution)/shard_map/all_to_all | solution.py:37
  95.4 18.7 %all-to-all-done = bf16[8,1,64,1280]{3,2,1,0:T(8,128)(2,1)S(1)} async-done(((bf16[8,1,64,1280]{3,2,1,0:T(8,128)(2,1)}), bf16[8,1,64,1280]{3,2,1,0:T(8,128)(2,1)S(1)}, u32[]{:S(2)}, u32[]{:S(2)}) %all-to-all-start) | async-done | bytes 1310752 | tf_op jit(solution)/shard_map/all_to_all | solution.py:37
  114.1 11.9 %multiply_reduce_fusion = (f32[512]{0:T(512)S(1)}, f32[512,4096]{1,0:T(8,128)}) fusion(bf16[512,1280]{1,0:T(8,128)(2,1)S(1)} %bitcast.94, bf16[1280,4096]{1,0:T(8,128)(2,1)} %param.19), kind=kOutput, calls=%fused_computation.3 | convolution fusion | flops 5377097216 | bytes 20187136 | tf_op jit(solution)/shard_map/dot_general | solution.py:436
  126.0 0.1 rsqrt.19
  126.1 6.7 %multiply_convert_fusion.normed_ref = bf16[512,4096]{1,0:T(8,128)(2,1)} fusion(f32[512,4096]{1,0:T(8,128)} %get-tuple-element.20, f32[4096]{0:T(1024)S(1)} %copy-done.12, f32[512]{0:T(512)S(1)} %add_rsqrt_fusion), kind=kLoop, calls=%fused_computation.2 | loop fusion | flops 6291456 | bytes 12601344 | tf_op jit(solution)/shard_map/convert_element_type | solution.py:441
  132.9 10.2 %fusion.4 = f32[512,896]{1,0:T(8,128)S(1)} fusion(bf16[512,4096]{1,0:T(8,128)(2,1)} %multiply_convert_fusion.normed_ref, bf16[4096,1792]{1,0:T(8,128)(2,1)} %all-gather.2.cloned.1.call-done.weights_hbm), kind=kOutput, calls=%fused_computation.9 | convolution fusion | flops 3758096384 | bytes 13369344 | tf_op jit(solution)/shard_map/dot_general | solution.py:446
  143.1 0.1 copy-done.15
  143.2 6.1 %fusion.15 = (bf16[512,896]{1,0:T(8,128)(2,1)S(1)}, bf16[512,896]{1,0:T(8,128)(2,1)}, bf16[512,896]{1,0:T(8,128)(2,1)S(1)}) fusion(f32[512,896]{1,0:T(8,128)S(1)} %fusion.4, bf16[8,64,896]{2,1,0:T(8,128)(2,1)S(1)} %copy-done.17, bf16[512,4096]{1,0:T(8,128)(2,1)S(1)} %copy-done.4, bf16[4096,1792]{1,0:T(8,128)(2,1)S(1)} %copy-done.15), kind=kOutput, calls=%fused_computation.33 | convolution fusion | flops 3765895168 | bytes 17039360 | tf_op jit(solution)/shard_map/dot_general | solution.py:447
  149.3 1.3 pad_maximum_fusion.2.grads_ref
  150.7 87.7 %grad_rings.1 = (f32[2,256,896]{2,1,0:T(8,128)}, f32[8,64,512]{2,1,0:T(8,128)}) custom-call(bf16[512,4096]{1,0:T(8,128)(2,1)} %multiply_convert_fusion.normed_ref, bf16[512,1792]{1,0:T(8,128)(2,1)} %pad_maximum_fusion.2.grads_ref, bf16[4096,1792]{1,0:T(8,128)(2,1)} %all-gather.2.cloned.1.call-done.weights_hbm), custom_call_target="tpu_custom_call" | custom-call | flops 15032385536 | bytes 200000000 | tf_op jit(solution)/shard_map/grad_rings/pallas_call | solution.py:294
  238.4 2.9 %slice_bitcast_fusion = (f32[256,896]{1,0:T(8,128)}, f32[256,896]{1,0:T(8,128)}) fusion(f32[2,256,896]{2,1,0:T(8,128)} %get-tuple-element.6), kind=kLoop, calls=%fused_computation.52 | loop fusion | bytes 3670016 | tf_op jit(solution)/shard_map/squeeze | solution.py:457
  241.3 0.6 copy.51
  241.9 1.2 reshape.407
  243.1 1.5 copy.59
  244.6 1.6 fusion.23
  246.2 2.5 multiply_subtract_fusion
  (42 shorter events, 0.1 us)
Async XLA Ops:
  7.2 19.7 %copy-start = (bf16[1280,1280]{1,0:T(8,128)(2,1)S(1)}, bf16[1280,1280]{1,0:T(8,128)(2,1)}, u32[]{:S(2)}) copy-start(bf16[1280,1280]{1,0:T(8,128)(2,1)} %param.18) | copy-start | bytes 9830404
  7.2 11.5 %copy-start.14 = (s32[32]{0:T(128)S(1)}, s32[32]{0:T(128)}, u32[]{:S(2)}) copy-start(s32[32]{0:T(128)} %param.13) | copy-start | bytes 388
  7.2 125.7 %all-gather.2.cloned.1.call-start = ((), (), s32[]{:S(2)}) async-start(), calls=%async_computation.1 | async-start | bytes 15597568 | tf_op jit(solution)/shard_map/all_gather | solution.py:443
  9.6 34.1 %collective-permute-start.2 = (bf16[256,1280]{1,0:T(8,128)(2,1)}, bf16[256,1280]{1,0:T(8,128)(2,1)}, u32[]{:S(2)}, u32[]{:S(2)}) collective-permute-start(bf16[256,1280]{1,0:T(8,128)(2,1)} %bitcast.90), channel_id=1, source_target_pairs={{0,1},{1,2},{2,3},{3,4},{4,5},{5,6},{6,7},{7,8},{8,9},{9,10},{10,1... | collective-permute-start | bytes 1966088 | tf_op jit(solution)/shard_map/ppermute | solution.py:26
  14.0 23.5 %collective-permute-start = (bf16[256,1280]{1,0:T(8,128)(2,1)}, bf16[256,1280]{1,0:T(8,128)(2,1)}, u32[]{:S(2)}, u32[]{:S(2)}) collective-permute-start(bf16[256,1280]{1,0:T(8,128)(2,1)} %bitcast.91), channel_id=1, source_target_pairs={{0,3},{1,0},{2,1},{3,2},{4,7},{5,4},{6,5},{7,6},{8,11},{9,8},{10,9... | collective-permute-start | bytes 1966088 | tf_op jit(solution)/shard_map/ppermute | solution.py:24
  19.1 7.0 %copy-start.13 = (s32[1,64]{1,0:T(1,128)S(1)}, s32[1,64]{1,0:T(1,128)}, u32[]{:S(2)}) copy-start(s32[1,64]{1,0:T(1,128)} %param.14) | copy-start | bytes 772
  26.0 3.3 %copy-start.5 = (bf16[1,256,1280]{2,1,0:T(8,128)(2,1)S(1)}, bf16[1,256,1280]{2,1,0:T(8,128)(2,1)}, u32[]{:S(2)}) copy-start(bf16[1,256,1280]{2,1,0:T(8,128)(2,1)} %param.12) | copy-start | bytes 1966084
  26.0 3.3 %copy-start.16 = (bf16[1280,1280]{1,0:T(8,128)(2,1)S(1)}, bf16[1280,1280]{1,0:T(8,128)(2,1)}, u32[]{:S(2)}) copy-start(bf16[1280,1280]{1,0:T(8,128)(2,1)} %param.17) | copy-start | bytes 9830404
  37.5 21.5 %collective-permute-start.1 = (bf16[256,1280]{1,0:T(8,128)(2,1)}, bf16[256,1280]{1,0:T(8,128)(2,1)S(1)}, u32[]{:S(2)}, u32[]{:S(2)}) collective-permute-start(bf16[256,1280]{1,0:T(8,128)(2,1)} %collective-permute-done), channel_id=1, source_target_pairs={{3,2},{0,3},{1,4},{2,5},{7,6},{4,7},{5,8},{6,9},{11,10},{8,11},{9,... | collective-permute-start | bytes 1966088 | tf_op jit(solution)/shard_map/ppermute | solution.py:26
  59.0 0.9 copy-start.18
  60.9 2.5 copy-start.19
  63.5 3.1 %copy-start.10 = (bf16[256,1280]{1,0:T(8,128)(2,1)S(1)}, bf16[256,1280]{1,0:T(8,128)(2,1)}, u32[]{:S(2)}) copy-start(bf16[256,1280]{1,0:T(8,128)(2,1)} %convolution_convert_fusion.1) | copy-start | bytes 1966084
  63.5 3.1 %copy-start.11 = (bf16[256,1280]{1,0:T(8,128)(2,1)S(1)}, bf16[256,1280]{1,0:T(8,128)(2,1)}, u32[]{:S(2)}) copy-start(bf16[256,1280]{1,0:T(8,128)(2,1)} %convolution_convert_fusion.2) | copy-start | bytes 1966084
  66.5 2.6 %copy-start.8 = (bf16[256,1280]{0,1:T(8,128)(2,1)S(1)}, bf16[256,1280]{0,1:T(8,128)(2,1)}, u32[]{:S(2)}) copy-start(bf16[256,1280]{0,1:T(8,128)(2,1)} %copy.42) | copy-start | bytes 1966084
  69.1 7.8 %copy-start.7 = (f32[1,256,1280]{1,2,0:T(8,128)S(1)}, f32[1,256,1280]{1,2,0:T(8,128)}, u32[]{:S(2)}) copy-start(f32[1,256,1280]{1,2,0:T(8,128)} %copy.39) | copy-start | bytes 3932164
  77.0 6.9 %copy-start.6 = (bf16[1,256,1280]{2,1,0:T(8,128)(2,1)S(1)}, bf16[1,256,1280]{2,1,0:T(8,128)(2,1)}, u32[]{:S(2)}) copy-start(bf16[1,256,1280]{2,1,0:T(8,128)(2,1)} %param.12) | copy-start | bytes 1966084
  83.8 1.9 copy-start.9
  88.2 25.9 %all-to-all-start = ((bf16[8,1,64,1280]{3,2,1,0:T(8,128)(2,1)}), bf16[8,1,64,1280]{3,2,1,0:T(8,128)(2,1)S(1)}, u32[]{:S(2)}, u32[]{:S(2)}) async-start(bf16[8,1,64,1280]{3,2,1,0:T(8,128)(2,1)} %broadcast_in_dim.49), calls=%async_computation | async-start | bytes 2621440 | tf_op jit(solution)/shard_map/all_to_all | solution.py:37
  114.1 12.0 %copy-start.12 = (f32[4096]{0:T(1024)S(1)}, f32[4096]{0:T(1024)}, u32[]{:S(2)}) copy-start(f32[4096]{0:T(1024)} %param.20) | copy-start | bytes 49156
  132.8 10.3 %copy-start.17 = (bf16[8,64,896]{2,1,0:T(8,128)(2,1)S(1)}, bf16[8,64,896]{2,1,0:T(8,128)(2,1)}, u32[]{:S(2)}) copy-start(bf16[8,64,896]{2,1,0:T(8,128)(2,1)} %param.23) | copy-start | bytes 2752516
  132.8 10.3 %copy-start.4 = (bf16[512,4096]{1,0:T(8,128)(2,1)S(1)}, bf16[512,4096]{1,0:T(8,128)(2,1)}, u32[]{:S(2)}) copy-start(bf16[512,4096]{1,0:T(8,128)(2,1)} %multiply_convert_fusion.normed_ref) | copy-start | bytes 12582916
  132.8 10.4 %copy-start.15 = (bf16[4096,1792]{1,0:T(8,128)(2,1)S(1)}, bf16[4096,1792]{1,0:T(8,128)(2,1)}, u32[]{:S(2)}) copy-start(bf16[4096,1792]{1,0:T(8,128)(2,1)} %all-gather.2.cloned.1.call-done.weights_hbm) | copy-start | bytes 44040196
  238.4 2.9 %copy-start.2 = (f32[8,64,512]{2,1,0:T(8,128)S(1)}, f32[8,64,512]{2,1,0:T(8,128)}, u32[]{:S(2)}) copy-start(f32[8,64,512]{2,1,0:T(8,128)} %get-tuple-element.7) | copy-start | bytes 3145732
  243.1 3.1 %copy-start.3 = (f32[1,64,4096]{2,1,0:T(8,128)S(1)}, f32[1,64,4096]{2,1,0:T(8,128)}, u32[]{:S(2)}) copy-start(f32[1,64,4096]{2,1,0:T(8,128)} %reshape.407) | copy-start | bytes 3145732
  243.1 5.5 %copy-start.1 = (bf16[1280,1280]{1,0:T(8,128)(2,1)S(1)}, bf16[1280,1280]{1,0:T(8,128)(2,1)}, u32[]{:S(2)}) copy-start(bf16[1280,1280]{1,0:T(8,128)(2,1)} %param.18) | copy-start | bytes 9830404
Sparse Core Ops, SparseCore 0:
  10.7 119.3 all-gather.1

commit v3 on v2

--- a/solution.py
+++ b/solution.py
@@ -15,30 +15,10 @@
 masked_score = -1e30
 
 
-def from_earlier(shard, by):
-    axes = ("seq", "fsdp")
-    devices = lax.axis_size(axes)
-    pairs = [(i, i + by) for i in range(devices) if i + by < devices]
-    if by == 2:
-        via = [i - i % SIDE + (i - 1) % SIDE for i in range(devices)]
-        shard = lax.ppermute(shard, axes, [(i, via[i]) for i in range(devices)])
-        pairs = [(via[i], j) for i, j in pairs if via[i] != j]
-    return lax.ppermute(shard, axes, pairs)
-
-
 def laid_out(pieces, dim):
     lengths = list(pieces.shape[1:])
     lengths[dim] *= pieces.shape[0]
     return jnp.moveaxis(pieces, 0, dim).reshape(lengths)
-
-
-def copy_for_each(shard, axis):
-    copies = jnp.broadcast_to(shard, (lax.axis_size(axis), *shard.shape))
-    return lax.all_to_all(copies, axis, split_axis=0, concat_axis=0, tiled=True)
-
-
-def gather_directly(shard, axis, dim):
-    return laid_out(copy_for_each(shard, axis), dim)
 
 
 MESH = pl.DeviceIdType.MESH
@@ -330,62 +310,399 @@
     )(normed, grads, weights)
 
 
+def front(
+    states_ref,
+    query_doc_ref,
+    key_doc_ref,
+    spans_ref,
+    gain_ref,
+    gate_hbm,
+    up_hbm,
+    query_hbm,
+    key_hbm,
+    value_hbm,
+    proj_hbm,
+    weights_ref,
+    normed_ref,
+    own_features_ref,
+    square,
+    proj,
+    earlier,
+    passing,
+    queries,
+    keys,
+    values,
+    bias,
+    mixed,
+    pooled,
+    contexts,
+    loads,
+    put_a,
+    got_a,
+    put_b,
+    got_b,
+    put_s,
+    got_s,
+    put_x,
+    got_x,
+    put_c,
+    got_c,
+):
+    seq = lax.axis_index("seq")
+    spot = lax.axis_index("fsdp")
+    x, core = lax.div(seq, 2), lax.rem(seq, 2)
+    z, y = lax.div(spot, SIDE), lax.rem(spot, SIDE)
+    groups, spots = 2 * SIDE, SIDE * SIDE
+    devices = groups * spots
+    length, width = states_ref.shape
+    slots = spans_ref.shape[0]
+    heads = width // HEAD
+    units = gate_hbm.shape[1]
+    rows = gate_hbm.shape[0]
+    half_rows = rows // 2
+    model = proj_hbm.shape[1]
+    split = 9 * units // 7
+
+    def device_of(position):
+        position = lax.rem(position + devices, devices)
+        return lax.div(position, spots), lax.rem(position, spots)
+
+    here = seq * spots + spot
+    around = (
+        (seq, wrapped(z + 1) * SIDE + y),
+        (seq, wrapped(z - 1) * SIDE + y),
+        (seq, z * SIDE + wrapped(y + 1)),
+        (seq, z * SIDE + wrapped(y - 1)),
+    )
+    next_block = device_of(here + 1)
+    relayed_to = device_of(seq * spots + z * SIDE + wrapped(y + 1) + 2)
+    origin_seq, origin_spot = device_of(here - 2)
+    origin_z, origin_y = lax.div(origin_spot, SIDE), lax.rem(origin_spot, SIDE)
+    relayed_from = (origin_seq, origin_z * SIDE + wrapped(origin_y - 1))
+    other_core = (x * 2 + 1 - core, spot)
+    along_x = tuple((wrapped(x + by) * 2 + core, spot) for by in range(1, SIDE))
+
+    places = [
+        (weights_ref.at[pl.ds(pl.multiple_of(spot * rows, rows), rows), 0:units], gate_hbm),
+        (weights_ref.at[pl.ds(pl.multiple_of(spot * rows, rows), rows), units:], up_hbm),
+        (square.at[0], query_hbm),
+        (square.at[1], key_hbm),
+        (square.at[2], value_hbm),
+        (proj, proj_hbm),
+    ]
+    load = [
+        pltpu.make_async_copy(source, target, loads.at[i])
+        for i, (target, source) in enumerate(places)
+    ]
+    for copy in load:
+        copy.start()
+
+    greeted = (
+        *around,
+        next_block,
+        device_of(here - 1),
+        relayed_to,
+        relayed_from,
+        other_core,
+        *along_x,
+    )
+    barrier = pltpu.get_barrier_semaphore()
+    for neighbour in greeted:
+        pl.semaphore_signal(barrier, inc=1, device_id=neighbour, device_id_type=MESH)
+    pl.semaphore_wait(barrier, len(greeted))
+
+    def remote(source, target, sent, arrived, device):
+        return pltpu.make_async_remote_copy(
+            src_ref=source,
+            dst_ref=target,
+            send_sem=sent,
+            recv_sem=arrived,
+            device_id=device,
+            device_id_type=MESH,
+        )
+
+    recent = earlier.at[length : 2 * length]
+    oldest = earlier.at[0:length]
+    to_next = remote(states_ref, recent, put_s.at[0], got_s.at[0], next_block)
+    to_relay = remote(states_ref, passing, put_s.at[1], got_s.at[1], around[3])
+    relay = remote(passing, oldest, put_s.at[2], got_s.at[2], relayed_to)
+    to_next.start()
+    to_relay.start()
+    load[0].wait()
+    load[1].wait()
+
+    def piece(stream, t, k):
+        kind, half = stream // 2, stream % 2
+        step = 1 - 2 * half
+        along, across = (z, y) if kind == 0 else (y, z)
+        far, near = wrapped(along - step * t), wrapped(across - step * k)
+        zb, yb = (far, near) if kind == 0 else (near, far)
+        at = pl.multiple_of((zb * SIDE + yb) * rows + half * half_rows, half_rows)
+        columns = slice(0, split) if kind == 0 else slice(split, 2 * units)
+        return weights_ref.at[pl.ds(at, half_rows), columns]
+
+    def small(stream, k):
+        kind, half = stream // 2, stream % 2
+        device = around[2 + half] if kind == 0 else around[half]
+        region = piece(stream, 0, k)
+        return remote(region, region, put_a.at[stream, k], got_a.at[stream, k], device)
+
+    def large(stream, t, k):
+        kind, half = stream // 2, stream % 2
+        device = around[half] if kind == 0 else around[2 + half]
+        region = piece(stream, t, k)
+        return remote(
+            region, region, put_b.at[stream, t, k], got_b.at[stream, t, k], device
+        )
+
+    last = SIDE - 1
+
+    def spread(k):
+        for stream in range(4):
+            if k > 0:
+                small(stream, k - 1).wait_recv()
+            if k < last:
+                small(stream, k).start()
+            large(stream, 0, k).start()
+
+    def pass_on(t, k):
+        for stream in range(4):
+            large(stream, t - 1, k).wait_recv()
+            large(stream, t, k).start()
+
+    spread(0)
+
+    chunk = 2 * HEAD
+    scale = 1.0 / math.sqrt(HEAD)
+
+    def dot(a, b):
+        return jnp.dot(a, b, preferred_element_type=jnp.float32)
+
+    def dot_t(a, b):
+        return lax.dot_general(
+            a, b, (((1,), (1,)), ((), ())), preferred_element_type=jnp.float32
+        )
+
+    load[2].wait()
+
+    def make_queries(n, carry):
+        at = pl.ds(pl.multiple_of(n * chunk, chunk), chunk)
+        queries[:, at] = dot(states_ref[...], square[0, :, at]).astype(jnp.bfloat16)
+        return carry
+
+    lax.fori_loop(0, width // chunk, make_queries, 0)
+    spread(1)
+    load[3].wait()
+    load[4].wait()
+
+    def keys_and_values(source, row):
+        def body(n, carry):
+            at = pl.ds(pl.multiple_of(n * chunk, chunk), chunk)
+            keys[row : row + length, at] = dot(source[...], square[1, :, at]).astype(
+                jnp.bfloat16
+            )
+            values[row : row + length, at] = dot(source[...], square[2, :, at]).astype(
+                jnp.bfloat16
+            )
+            return carry
+
+        lax.fori_loop(0, width // chunk, body, 0)
+
+    keys_and_values(states_ref, 2 * length)
+    pass_on(1, 0)
+    to_relay.wait_recv()
+    relay.start()
+    spread(2)
+
+    span = WINDOW + HEAD
+    parts = length // HEAD
+    for r in range(parts):
+        row = lax.broadcasted_iota(jnp.int32, (HEAD, span), 0)
+        column = lax.broadcasted_iota(jnp.int32, (HEAD, span), 1)
+        allowed = (column > row) & (column <= row + WINDOW)
+        start = 2 * length - WINDOW + r * HEAD
+        allowed = allowed & (
+            key_doc_ref[:, start : start + span] == query_doc_ref[r * HEAD : (r + 1) * HEAD, :]
+        )
+        bias[r] = jnp.where(allowed, 0.0, masked_score)
+
+    to_next.wait_recv()
+    keys_and_values(recent, length)
+    pass_on(1, 1)
+    spread(3)
+    relay.wait_recv()
+    keys_and_values(oldest, 0)
+    pass_on(2, 0)
+    pass_on(1, 2)
+
+    def attend(h, carry):
+        at = pl.ds(pl.multiple_of(h * HEAD, HEAD), HEAD)
+        for r in range(parts):
+            here_rows = slice(r * HEAD, (r + 1) * HEAD)
+            start = 2 * length - WINDOW + r * HEAD
+            scores = dot_t(queries[here_rows, at], keys[start : start + span, at])
+            scores = scores * scale + bias[r]
+            weights = jnp.exp(scores - jnp.max(scores, axis=1, keepdims=True))
+            total = jnp.sum(weights, axis=1, keepdims=True)
+            summed = dot(weights.astype(jnp.bfloat16), values[start : start + span, at])
+            mixed[here_rows, at] = (
+                states_ref[here_rows, at].astype(jnp.float32) + summed / total
+            ).astype(jnp.bfloat16)
+        return carry
+
+    lax.fori_loop(0, heads // 2, attend, 0)
+    pass_on(2, 1)
+    lax.fori_loop(heads // 2, heads, attend, 0)
+    pass_on(1, 3)
+
+    begins, ends = spans_ref[:, 0:1], spans_ref[:, 1:2]
+    present = spans_ref[:, 2:3] > 0
+    byte = lax.broadcasted_iota(jnp.int32, (slots, length), 1)
+    member = (byte >= begins) & (byte < ends)
+    ones = jnp.where(member, 1.0, 0.0)
+    pool_bias = jnp.where(member, 0.0, masked_score)
+    sizes = jnp.maximum(jnp.sum(ones, axis=1, keepdims=True), 1.0)
+    pooled[...] = (dot(ones.astype(jnp.bfloat16), mixed[...]) / sizes).astype(jnp.bfloat16)
+    mine = pl.ds(pl.multiple_of(seq * slots, slots), slots)
+
+    def pool(h, carry):
+        at = pl.ds(pl.multiple_of(h * HEAD, HEAD), HEAD)
+        scores = dot_t(pooled[:, at], mixed[:, at]) * scale + pool_bias
+        weights = jnp.exp(scores - jnp.max(scores, axis=1, keepdims=True))
+        total = jnp.sum(weights, axis=1, keepdims=True)
+        summed = dot(weights.astype(jnp.bfloat16), mixed[:, at]) / total
+        contexts[mine, at] = jnp.where(present, summed, 0.0).astype(jnp.bfloat16)
+        return carry
+
+    lax.fori_loop(0, heads, pool, 0)
+
+    def context_of(group):
+        return contexts.at[pl.ds(pl.multiple_of(group * slots, slots), slots)]
+
+    def x_send(by):
+        region = context_of(seq)
+        return remote(region, region, put_x.at[by - 1], got_x.at[by - 1], along_x[by - 1])
+
+    def core_send(by):
+        region = context_of(wrapped(x - by) * 2 + core)
+        return remote(region, region, put_c.at[by], got_c.at[by], other_core)
+
+    for by in range(1, SIDE):
+        x_send(by).start()
+    core_send(0).start()
+    pass_on(2, 2)
+    for by in (1, 3, 2):
+        x_send(by).wait_recv()
+        core_send(by).start()
+    for by in range(SIDE):
+        core_send(by).wait_recv()
+    load[5].wait()
+
+    wide = 4 * HEAD
+
+    def project(n, squares):
+        at = pl.ds(pl.multiple_of(n * wide, wide), wide)
+        features = dot(contexts[...], proj[:, at]).astype(jnp.bfloat16)
+        normed_ref[:, at] = features
+        full = features.astype(jnp.float32)
+        return squares + jnp.sum(full * full, axis=1, keepdims=True)
+
+    squares = jnp.zeros((groups * slots, 1), jnp.float32)
+    squares = lax.fori_loop(0, model // wide // 2, project, squares)
+    pass_on(2, 3)
+    squares = lax.fori_loop(model // wide // 2, model // wide, project, squares)
+    inverse = lax.rsqrt(squares / model + epsilon)
+    own_features_ref[...] = normed_ref[mine, :]
+
+    def normalize(n, carry):
+        at = pl.ds(pl.multiple_of(n * wide, wide), wide)
+        normed_ref[:, at] = (
+            normed_ref[:, at].astype(jnp.float32) * inverse * gain_ref[:, at]
+        ).astype(jnp.bfloat16)
+        return carry
+
+    lax.fori_loop(0, model // wide, normalize, 0)
+
+    for stream in range(4):
+        for k in range(SIDE):
+            large(stream, last - 1, k).wait_recv()
+    for copy in (to_next, to_relay, relay):
+        copy.wait_send()
+    for stream in range(4):
+        for k in range(SIDE):
+            if k < last:
+                small(stream, k).wait_send()
+            for t in range(last):
+                large(stream, t, k).wait_send()
+    for by in range(SIDE):
+        if by > 0:
+            x_send(by).wait_send()
+        core_send(by).wait_send()
+
+
+def front_part(states, query_doc, key_doc, spans, gain, gate_w, up_w, squares, w_proj):
+    length, width = states.shape
+    slots = spans.shape[0]
+    rows, units = gate_w.shape
+    model = w_proj.shape[1]
+    tokens = 2 * SIDE * slots
+    dma = pltpu.SemaphoreType.DMA
+    whole = pl.BlockSpec(memory_space=pltpu.VMEM)
+    anywhere = pl.BlockSpec(memory_space=pl.ANY)
+    half = jnp.bfloat16
+    return pl.pallas_call(
+        front,
+        out_shape=(
+            jax.ShapeDtypeStruct((SIDE * SIDE * rows, 2 * units), half),
+            jax.ShapeDtypeStruct((tokens, model), half),
+            jax.ShapeDtypeStruct((slots, model), half),
+        ),
+        in_specs=[whole] * 5 + [anywhere] * 6,
+        out_specs=(anywhere, whole, whole),
+        scratch_shapes=[
+            pltpu.VMEM((3, width, width), half),
+            pltpu.VMEM((width, model), half),
+            pltpu.VMEM((2 * length, width), half),
+            pltpu.VMEM((length, width), half),
+            pltpu.VMEM((length, width), half),
+            pltpu.VMEM((3 * length, width), half),
+            pltpu.VMEM((3 * length, width), half),
+            pltpu.VMEM((length // HEAD, HEAD, WINDOW + HEAD), jnp.float32),
+            pltpu.VMEM((length, width), half),
+            pltpu.VMEM((slots, width), half),
+            pltpu.VMEM((tokens, width), half),
+            dma((6,)),
+            dma((4, SIDE - 1)),
+            dma((4, SIDE - 1)),
+            dma((4, SIDE - 1, SIDE)),
+            dma((4, SIDE - 1, SIDE)),
+            dma((3,)),
+            dma((3,)),
+            dma((SIDE - 1,)),
+            dma((SIDE - 1,)),
+            dma((SIDE,)),
+            dma((SIDE,)),
+        ],
+        compiler_params=pltpu.CompilerParams(
+            collective_id=1, has_side_effects=True, vmem_limit_bytes=56 * 1024 * 1024
+        ),
+        name="front",
+    )(states, query_doc, key_doc, spans, gain, gate_w, up_w, *squares, w_proj)
+
+
 def doc_index(doc_lengths, positions):
     starts = jnp.cumsum(doc_lengths) - doc_lengths
     inside = (starts[None, :] <= positions[:, None]).astype(jnp.int32)
     return jnp.sum(inside, axis=1) - 1
 
 
-def window_attention(queries, key_rows, values, query_pos, key_pos, query_doc, key_doc):
-    row_count = queries.shape[0]
-    head_count = queries.shape[1] // HEAD
-    query_heads = queries.reshape(row_count, head_count, HEAD)
-    key_heads = key_rows.reshape(-1, head_count, HEAD)
-    value_heads = values.reshape(-1, head_count, HEAD)
-    scores = jnp.einsum(
-        "qhd,khd->hqk", query_heads, key_heads, preferred_element_type=jnp.float32
-    ) / math.sqrt(HEAD)
-    allowed = (key_pos[None, :] <= query_pos[:, None]) & (
-        query_pos[:, None] - key_pos[None, :] < WINDOW
-    )
-    allowed = allowed & (key_pos[None, :] >= 0) & (key_doc[None, :] == query_doc[:, None])
-    scores = jnp.where(allowed[None], scores, masked_score)
-    row_max = jnp.max(scores, axis=-1, keepdims=True)
-    weights = jnp.exp(scores - row_max)
-    weights = (weights / jnp.sum(weights, axis=-1, keepdims=True)).astype(jnp.bfloat16)
-    mixed = jnp.einsum("hqk,khd->qhd", weights, value_heads, preferred_element_type=jnp.float32)
-    return mixed.reshape(row_count, head_count * HEAD)
-
-
-def pool_patches(states, offsets, count):
-    length = states.shape[0]
-    slot_count = offsets.shape[0]
-    head_count = states.shape[1] // HEAD
-    slot_ids = jnp.arange(slot_count, dtype=jnp.int32)
+def slot_spans(offsets, count, length):
+    slot_ids = jnp.arange(offsets.shape[0], dtype=jnp.int32)
+    following = jnp.concatenate([offsets[1:], jnp.full((1,), length, jnp.int32)])
+    ends = jnp.where(slot_ids == count - 1, length, following)
     present = slot_ids < count
-    following = jnp.concatenate([offsets[1:], jnp.full((1,), length, jnp.int32)])
-    patch_ends = jnp.where(slot_ids == count - 1, length, following)
-    byte_ids = jnp.arange(length, dtype=jnp.int32)
-    member = (
-        present[:, None]
-        & (offsets[:, None] <= byte_ids[None, :])
-        & (byte_ids[None, :] < patch_ends[:, None])
-    )
-    patch_sizes = jnp.sum(member.astype(jnp.float32), axis=1, keepdims=True)
-    summed = jnp.dot(member.astype(jnp.bfloat16), states, preferred_element_type=jnp.float32)
-    pooled = (summed / jnp.maximum(patch_sizes, 1.0)).astype(jnp.bfloat16)
-    pooled_heads = pooled.reshape(slot_count, head_count, HEAD)
-    state_heads = states.reshape(length, head_count, HEAD)
-    scores = jnp.einsum(
-        "jhd,bhd->hjb", pooled_heads, state_heads, preferred_element_type=jnp.float32
-    ) / math.sqrt(HEAD)
-    scores = jnp.where(member[None], scores, masked_score)
-    row_max = jnp.max(scores, axis=-1, keepdims=True)
-    weights = jnp.exp(scores - row_max)
-    weights = (weights / jnp.sum(weights, axis=-1, keepdims=True)).astype(jnp.bfloat16)
-    context = jnp.einsum("hjb,bhd->jhd", weights, state_heads, preferred_element_type=jnp.float32)
-    context = context.reshape(slot_count, head_count * HEAD)
-    return jnp.where(present[:, None], context, 0.0).astype(jnp.bfloat16)
+    begins, ends = jnp.where(present, offsets, 0), jnp.where(present, ends, 0)
+    return jnp.stack([begins, ends, present.astype(jnp.int32)], axis=1)
 
 
 def shards(
@@ -404,45 +721,24 @@
 ):
     states = bytes_in[0]
     length = states.shape[0]
-    hop_count = (WINDOW - 2 + length) // length
     first_pos = lax.axis_index(("seq", "fsdp")) * length
-    queries = jnp.dot(states, w_query, preferred_element_type=jnp.float32).astype(jnp.bfloat16)
-    key_rows = jnp.dot(states, w_key, preferred_element_type=jnp.float32).astype(jnp.bfloat16)
-    values = jnp.dot(states, w_value, preferred_element_type=jnp.float32).astype(jnp.bfloat16)
-    key_parts = [key_rows]
-    value_parts = [values]
-    for distance in range(1, hop_count + 1):
-        earlier = from_earlier(states, distance)
-        earlier_keys = jnp.dot(earlier, w_key, preferred_element_type=jnp.float32).astype(
-            jnp.bfloat16
-        )
-        earlier_values = jnp.dot(earlier, w_value, preferred_element_type=jnp.float32).astype(
-            jnp.bfloat16
-        )
-        key_parts.insert(0, earlier_keys)
-        value_parts.insert(0, earlier_values)
-    key_all = jnp.concatenate(key_parts, axis=0)
-    value_all = jnp.concatenate(value_parts, axis=0)
-    query_pos = first_pos + jnp.arange(length, dtype=jnp.int32)
-    key_pos = first_pos - hop_count * length + jnp.arange((hop_count + 1) * length, dtype=jnp.int32)
+    key_pos = first_pos - 2 * length + jnp.arange(3 * length, dtype=jnp.int32)
     key_doc = doc_index(doc_lengths, key_pos)
-    query_doc = key_doc[hop_count * length :]
-    mixed = window_attention(queries, key_all, value_all, query_pos, key_pos, query_doc, key_doc)
-    hidden_bytes = (states.astype(jnp.float32) + mixed).astype(jnp.bfloat16)
-    context = pool_patches(hidden_bytes, patch_offsets[0], patch_counts[0, 0])
-    seq_index = lax.axis_index("seq")
-    shard_part = gather_directly(context[None], "seq", 0)
-    flat_part = shard_part.reshape(-1, shard_part.shape[-1])
-    result = jnp.dot(flat_part, w_proj, preferred_element_type=jnp.float32).astype(jnp.bfloat16)
-    features = result.reshape(shard_part.shape[0], shard_part.shape[1], -1)
-    seq_count, slot_count, model_width = features.shape
-    patch_float = features.reshape(seq_count * slot_count, model_width).astype(jnp.float32)
-    inverse = lax.rsqrt(jnp.mean(patch_float * patch_float, axis=1, keepdims=True) + epsilon)
-    normed = (patch_float * inverse * norm_gain).astype(jnp.bfloat16)
+    spans = slot_spans(patch_offsets[0], patch_counts[0, 0], length)
     units = gate_w.shape[1]
-    weights = lax.all_gather(
-        jnp.concatenate((gate_w, up_w), axis=1), "fsdp", axis=0, tiled=True
+    weights, normed, own_features = front_part(
+        states,
+        key_doc[2 * length :, None],
+        key_doc[None],
+        spans,
+        norm_gain[None],
+        gate_w,
+        up_w,
+        (w_query, w_key, w_value),
+        w_proj,
     )
+    slot_count, model_width = own_features.shape
+    seq_count = normed.shape[0] // slot_count
     gate_pre = jnp.dot(normed, weights[:, :units], preferred_element_type=jnp.float32)
     up_pre = jnp.dot(normed, weights[:, units:], preferred_element_type=jnp.float32)
     sigmoid_gate = jax.nn.sigmoid(gate_pre)
@@ -456,11 +752,9 @@
     totals, inward = grad_sums(normed, both_grads, weights, slot_count)
     grad_gate, grad_up = totals[0], totals[1]
     normed_grad = laid_out(inward, 1)
-    own_float = lax.dynamic_index_in_dim(
-        patch_float.reshape(seq_count, slot_count, model_width), seq_index, 0, keepdims=False
-    )
-    own_inverse = lax.dynamic_index_in_dim(
-        inverse.reshape(seq_count, slot_count, 1), seq_index, 0, keepdims=False
+    own_float = own_features.astype(jnp.float32)
+    own_inverse = lax.rsqrt(
+        jnp.mean(own_float * own_float, axis=1, keepdims=True) + epsilon
     )
     scaled = norm_gain * normed_grad
     patch_grad = own_inverse * scaled - own_float * (

time: 260 us -> 260 us (level); the launches traced: 256 us -> 260 us
  Pallas kernels: 87.7 us -> 231 us
  matrix products: 62.6 us -> 16.5 us
  waiting for transfers between devices: 35.5 us -> 0 us
  starting transfers between devices: 20 us -> 0 us
  between operations: 15.3 us -> 1.41 us
  local copies, waits for them, and re-layouts: 18.5 us -> 6.73 us
  other arithmetic: 16.1 us -> 4.63 us
    pallas_call x0 -> x1, Pallas kernels: none -> 139 us  [front_part(): pl.pallas_call(front, out_shape=(jax.ShapeDtypeStruct((SIDE * SIDE * rows...]
    dot_general x12 -> x0, matrix products: 38.5 us -> none  [the longest x1 11.9 us: shards(): jnp.dot(flat_part, w_proj, preferred_element_type=jnp.float32)]
    all_to_all x1 -> x0, waiting for transfers between devices: 18.7 us -> none  [copy_for_each(): return lax.all_to_all(copies, axis, split_axis=0, concat_axis=0, tiled=True)]
    ppermute x3 -> x0, waiting for transfers between devices: 16.7 us -> none  [the longest x2 10.4 us: from_earlier(): return lax.ppermute(shard, axes, pairs)]
    ppermute x3 -> x0, starting transfers between devices: 12.8 us -> none  [the longest x2 10.5 us: from_earlier(): return lax.ppermute(shard, axes, pairs)]
    sub x1 -> x0, matrix products: 7.81 us -> none  [window_attention(): weights = jnp.exp(scores - row_max)]
    all_to_all x1 -> x0, starting transfers between devices: 7.17 us -> none  [copy_for_each(): return lax.all_to_all(copies, axis, split_axis=0, concat_axis=0, tiled=True)]
    convert_element_type x2 -> x1, other arithmetic: 6.86 us -> 0.01 us  [slot_spans(): return jnp.stack([begins, ends, present.astype(jnp.int32)], axis=1)]
  transfers between devices with their start and end apart: 5 -> 0, of which waited for: 3 -> 0; matrix products, arithmetic and copies ran while one was open for 26% -> 0% of each run, Pallas kernels for 0% -> 0%
where the time goes in v3:
time: 260 us
  Pallas kernels  231 us (89%)
  matrix products  16.5 us (6%)
  local copies, waits for them, and re-layouts  6.73 us (3%)
  other arithmetic  4.63 us (2%)
    pallas_call x1, Pallas kernels, front_part(): pl.pallas_call(front, out_shape=(jax.ShapeDtypeStruct((SIDE * SIDE * rows...  139 us
    pallas_call x1, Pallas kernels, grad_sums(): pl.pallas_call(grad_rings, out_shape=(jax.ShapeDtypeStruct((2, rows, unit...  91.6 us
    dot_general x1, matrix products, shards(): jnp.dot(normed, weights[:, :units], preferred_element_type=jnp.float32)  10.4 us
    dot_general x1, matrix products, shards(): jnp.dot(normed, weights[:, units:], preferred_element_type=jnp.float32)  6.1 us

profile of v3, /device:TPU:0, one launch (start us, length us, event | category | flops | bytes accessed | tf_op | source)
XLA Modules:
  0.0 260.1 jit_solution(18124845525400897005)
XLA Ops:
  1.3 0.7 slice_bitcast_fusion.2
  2.0 0.7 fusion.14
  2.8 0.7 copy.28
  3.5 0.1 reduce-window.9
  3.6 0.1 reduce
  3.7 0.7 sub.21
  4.3 0.1 convert_reduce_fusion
  4.5 0.6 sub.24.key_doc_ref
  5.0 0.7 copy.30.spans_ref
  5.8 0.8 copy.29.query_doc_ref
  6.5 139.2 %front.1 = (bf16[4096,1792]{1,0:T(8,128)(2,1)}, bf16[512,4096]{1,0:T(8,128)(2,1)}, bf16[64,4096]{1,0:T(8,128)(2,1)}) custom-call(bf16[256,1280]{1,0:T(8,128)(2,1)} %bitcast.31, s32[256,1]{1,0:T(8,128)} %copy.29.query_doc_ref, s32[1,768]{1,0:T(1,128)} %sub.24.key_doc_ref, s32[64,3]{1,0:T(8,128)} %copy.30.spans_ref, f32[1,4096]{1,0:T(1,128)} %bitcast.32, ...), custom_call_target="tpu_custom_call" | custom-call | tf_op jit(solution)/shard_map/front/pallas_call | solution.py:653
  145.8 0.0 copy-start.3
  145.8 0.0 copy-start.4
  145.8 0.0 copy-start.5
  145.8 10.4 %fusion.2 = f32[512,896]{1,0:T(8,128)S(1)} fusion(bf16[512,4096]{1,0:T(8,128)(2,1)} %get-tuple-element.9.normed_ref, bf16[4096,1792]{1,0:T(8,128)(2,1)} %get-tuple-element.10.weights_hbm), kind=kOutput, calls=%fused_computation.2 | convolution fusion | flops 3758096384 | bytes 13369344 | tf_op jit(solution)/shard_map/dot_general | solution.py:742
  156.2 0.0 copy-done.3
  156.3 0.0 copy-done.4
  156.3 0.0 copy-done.5
  156.3 6.1 %fusion.6 = (bf16[512,896]{1,0:T(8,128)(2,1)S(1)}, bf16[512,896]{1,0:T(8,128)(2,1)}, bf16[512,896]{1,0:T(8,128)(2,1)S(1)}) fusion(f32[512,896]{1,0:T(8,128)S(1)} %fusion.2, bf16[8,64,896]{2,1,0:T(8,128)(2,1)S(1)} %copy-done.5, bf16[512,4096]{1,0:T(8,128)(2,1)S(1)} %copy-done.4, bf16[4096,1792]{1,0:T(8,128)(2,1)S(1)} %copy-done.3), kind=kOutput, calls=%fused_computation.8 | convolution fusion | flops 3765895168 | bytes 17039360 | tf_op jit(solution)/shard_map/dot_general | solution.py:743
  162.4 1.4 pad_maximum_fusion.grads_ref
  163.8 91.6 %grad_rings.1 = (f32[2,256,896]{2,1,0:T(8,128)}, f32[8,64,512]{2,1,0:T(8,128)}) custom-call(bf16[512,4096]{1,0:T(8,128)(2,1)} %get-tuple-element.9.normed_ref, bf16[512,1792]{1,0:T(8,128)(2,1)} %pad_maximum_fusion.grads_ref, bf16[4096,1792]{1,0:T(8,128)(2,1)} %get-tuple-element.10.weights_hbm), custom_call_target="tpu_custom_call" | custom-call | flops 15032385536 | bytes 200000000 | tf_op jit(solution)/shard_map/grad_rings/pallas_call | solution.py:274
  255.3 0.0 copy-start.1
  255.3 1.4 copy.32
  256.8 0.4 copy-done.1
  257.2 0.0 copy-start
  257.2 0.0 copy-start.2
  257.2 1.3 slice_bitcast_fusion
  258.5 0.0 copy-done
  258.5 0.0 copy-done.2
  258.5 0.3 fusion.9
  258.9 1.2 fusion.12
  (7 shorter events, 0.0 us)
Async XLA Ops:
  145.8 10.5 %copy-start.3 = (bf16[4096,1792]{1,0:T(8,128)(2,1)S(1)}, bf16[4096,1792]{1,0:T(8,128)(2,1)}, u32[]{:S(2)}) copy-start(bf16[4096,1792]{1,0:T(8,128)(2,1)} %get-tuple-element.10.weights_hbm) | copy-start | bytes 44040196
  145.8 10.5 %copy-start.4 = (bf16[512,4096]{1,0:T(8,128)(2,1)S(1)}, bf16[512,4096]{1,0:T(8,128)(2,1)}, u32[]{:S(2)}) copy-start(bf16[512,4096]{1,0:T(8,128)(2,1)} %get-tuple-element.9.normed_ref) | copy-start | bytes 12582916
  145.8 10.5 %copy-start.5 = (bf16[8,64,896]{2,1,0:T(8,128)(2,1)S(1)}, bf16[8,64,896]{2,1,0:T(8,128)(2,1)}, u32[]{:S(2)}) copy-start(bf16[8,64,896]{2,1,0:T(8,128)(2,1)} %param.23) | copy-start | bytes 2752516
  255.3 1.8 copy-start.1
  257.2 1.3 copy-start
  257.2 1.4 copy-start.2

commit v4 on v3

--- a/solution.py
+++ b/solution.py
@@ -316,6 +316,7 @@
     key_doc_ref,
     spans_ref,
     gain_ref,
+    cotangent_ref,
     gate_hbm,
     up_hbm,
     query_hbm,
@@ -325,10 +326,14 @@
     weights_ref,
     normed_ref,
     own_features_ref,
-    square,
-    proj,
+    hidden_ref,
+    grads_ref,
+    gates,
+    ups,
+    maps,
+    crossed,
+    sums,
     earlier,
-    passing,
     queries,
     keys,
     values,
@@ -337,6 +342,7 @@
     pooled,
     contexts,
     loads,
+    stores,
     put_a,
     got_a,
     put_b,
@@ -359,9 +365,8 @@
     heads = width // HEAD
     units = gate_hbm.shape[1]
     rows = gate_hbm.shape[0]
-    half_rows = rows // 2
     model = proj_hbm.shape[1]
-    split = 9 * units // 7
+    ranges = (slice(0, 3 * HEAD), slice(3 * HEAD, units))
 
     def device_of(position):
         position = lax.rem(position + devices, devices)
@@ -375,34 +380,31 @@
         (seq, z * SIDE + wrapped(y - 1)),
     )
     next_block = device_of(here + 1)
-    relayed_to = device_of(seq * spots + z * SIDE + wrapped(y + 1) + 2)
-    origin_seq, origin_spot = device_of(here - 2)
-    origin_z, origin_y = lax.div(origin_spot, SIDE), lax.rem(origin_spot, SIDE)
-    relayed_from = (origin_seq, origin_z * SIDE + wrapped(origin_y - 1))
+    after_next = device_of(here + 2)
     other_core = (x * 2 + 1 - core, spot)
     along_x = tuple((wrapped(x + by) * 2 + core, spot) for by in range(1, SIDE))
 
     places = [
-        (weights_ref.at[pl.ds(pl.multiple_of(spot * rows, rows), rows), 0:units], gate_hbm),
-        (weights_ref.at[pl.ds(pl.multiple_of(spot * rows, rows), rows), units:], up_hbm),
-        (square.at[0], query_hbm),
-        (square.at[1], key_hbm),
-        (square.at[2], value_hbm),
-        (proj, proj_hbm),
+        (gates.at[z, y], gate_hbm),
+        (ups.at[y, z], up_hbm),
+        (maps.at[:, 0:width], query_hbm),
+        (maps.at[:, width : 2 * width], key_hbm),
+        (maps.at[:, 2 * width : 3 * width], value_hbm),
+        (maps, proj_hbm),
     ]
     load = [
         pltpu.make_async_copy(source, target, loads.at[i])
         for i, (target, source) in enumerate(places)
     ]
-    for copy in load:
+    for copy in load[:5]:
         copy.start()
 
     greeted = (
         *around,
         next_block,
         device_of(here - 1),
-        relayed_to,
-        relayed_from,
+        after_next,
+        device_of(here - 2),
         other_core,
         *along_x,
     )
@@ -424,22 +426,22 @@
     recent = earlier.at[length : 2 * length]
     oldest = earlier.at[0:length]
     to_next = remote(states_ref, recent, put_s.at[0], got_s.at[0], next_block)
-    to_relay = remote(states_ref, passing, put_s.at[1], got_s.at[1], around[3])
-    relay = remote(passing, oldest, put_s.at[2], got_s.at[2], relayed_to)
+    to_after = remote(states_ref, oldest, put_s.at[1], got_s.at[1], after_next)
     to_next.start()
-    to_relay.start()
+    to_after.start()
     load[0].wait()
     load[1].wait()
 
+    def place(stream, t):
+        kind, half = stream // 2, stream % 2
+        along = z if kind == 0 else y
+        return (gates, ups)[kind], wrapped(along - (1 - 2 * half) * t), ranges[half]
+
     def piece(stream, t, k):
         kind, half = stream // 2, stream % 2
-        step = 1 - 2 * half
-        along, across = (z, y) if kind == 0 else (y, z)
-        far, near = wrapped(along - step * t), wrapped(across - step * k)
-        zb, yb = (far, near) if kind == 0 else (near, far)
-        at = pl.multiple_of((zb * SIDE + yb) * rows + half * half_rows, half_rows)
-        columns = slice(0, split) if kind == 0 else slice(split, 2 * units)
-        return weights_ref.at[pl.ds(at, half_rows), columns]
+        across = y if kind == 0 else z
+        buffer, far, columns = place(stream, t)
+        return buffer.at[far, wrapped(across - (1 - 2 * half) * k), :, columns]
 
     def small(stream, k):
         kind, half = stream // 2, stream % 2
@@ -453,6 +455,18 @@
         region = piece(stream, t, k)
         return remote(
             region, region, put_b.at[stream, t, k], got_b.at[stream, t, k], device
+        )
+
+    def store(stream, t):
+        kind, half = stream // 2, stream % 2
+        buffer, far, columns = place(stream, t)
+        target = slice(kind * units + columns.start, kind * units + columns.stop)
+        if kind == 0:
+            target = weights_ref.at[far, :, :, target]
+        else:
+            target = weights_ref.at[:, far, :, target]
+        return pltpu.make_async_copy(
+            buffer.at[far, :, :, columns], target, stores.at[stream, t]
         )
 
     last = SIDE - 1
@@ -487,7 +501,7 @@
 
     def make_queries(n, carry):
         at = pl.ds(pl.multiple_of(n * chunk, chunk), chunk)
-        queries[:, at] = dot(states_ref[...], square[0, :, at]).astype(jnp.bfloat16)
+        queries[:, at] = dot(states_ref[...], maps[:, at]).astype(jnp.bfloat16)
         return carry
 
     lax.fori_loop(0, width // chunk, make_queries, 0)
@@ -498,20 +512,17 @@
     def keys_and_values(source, row):
         def body(n, carry):
             at = pl.ds(pl.multiple_of(n * chunk, chunk), chunk)
-            keys[row : row + length, at] = dot(source[...], square[1, :, at]).astype(
-                jnp.bfloat16
-            )
-            values[row : row + length, at] = dot(source[...], square[2, :, at]).astype(
-                jnp.bfloat16
-            )
+            key_at = pl.ds(pl.multiple_of(width + n * chunk, chunk), chunk)
+            value_at = pl.ds(pl.multiple_of(2 * width + n * chunk, chunk), chunk)
+            into = slice(row, row + length)
+            keys[into, at] = dot(source[...], maps[:, key_at]).astype(jnp.bfloat16)
+            values[into, at] = dot(source[...], maps[:, value_at]).astype(jnp.bfloat16)
             return carry
 
         lax.fori_loop(0, width // chunk, body, 0)
 
     keys_and_values(states_ref, 2 * length)
     pass_on(1, 0)
-    to_relay.wait_recv()
-    relay.start()
     spread(2)
 
     span = WINDOW + HEAD
@@ -530,8 +541,9 @@
     keys_and_values(recent, length)
     pass_on(1, 1)
     spread(3)
-    relay.wait_recv()
+    to_after.wait_recv()
     keys_and_values(oldest, 0)
+    load[5].start()
     pass_on(2, 0)
     pass_on(1, 2)
 
@@ -602,7 +614,7 @@
 
     def project(n, squares):
         at = pl.ds(pl.multiple_of(n * wide, wide), wide)
-        features = dot(contexts[...], proj[:, at]).astype(jnp.bfloat16)
+        features = dot(contexts[...], maps[:, at]).astype(jnp.bfloat16)
         normed_ref[:, at] = features
         full = features.astype(jnp.float32)
         return squares + jnp.sum(full * full, axis=1, keepdims=True)
@@ -615,32 +627,70 @@
     own_features_ref[...] = normed_ref[mine, :]
 
     def normalize(n, carry):
-        at = pl.ds(pl.multiple_of(n * wide, wide), wide)
-        normed_ref[:, at] = (
-            normed_ref[:, at].astype(jnp.float32) * inverse * gain_ref[:, at]
+        at = pl.ds(pl.multiple_of(n * rows, rows), rows)
+        turned = (n % SIDE) * SIDE + n // SIDE
+        value = (normed_ref[:, at].astype(jnp.float32) * inverse * gain_ref[:, at]).astype(
+            jnp.bfloat16
+        )
+        normed_ref[:, at] = value
+        crossed[:, pl.ds(pl.multiple_of(turned * rows, rows), rows)] = value
+        return carry
+
+    lax.fori_loop(0, model // rows, normalize, 0)
+    sums[...] = jnp.zeros_like(sums)
+
+    def accumulate(t, carry):
+        @pl.when(t == last)
+        def _():
+            for stream in range(4):
+                for k in range(SIDE):
+                    large(stream, last - 1, k).wait_recv()
+
+        for stream in range(4):
+            store(stream, t).start()
+            buffer, far, columns = place(stream, t)
+            kind, count = stream // 2, columns.stop - columns.start
+            deep = SIDE * rows
+            at = pl.ds(pl.multiple_of(far * deep, deep), deep)
+            block = buffer[far, :, :, columns].reshape(deep, count)
+            sums[kind, :, columns] += dot((normed_ref, crossed)[kind][:, at], block)
+        return carry
+
+    lax.fori_loop(0, SIDE, accumulate, 0)
+
+    def gating(n, carry):
+        at = pl.ds(pl.multiple_of(n * slots, slots), slots)
+        gate_pre, up_pre = sums[0, at], sums[1, at]
+        sigmoid_gate = jax.nn.sigmoid(gate_pre)
+        swish = gate_pre * sigmoid_gate
+        cotangent = cotangent_ref[at, :].astype(jnp.float32)
+        hidden_ref[at, :] = (swish * up_pre).astype(jnp.bfloat16)
+        grads_ref[at, 0:units] = (
+            cotangent * up_pre * sigmoid_gate * (1.0 + gate_pre * (1.0 - sigmoid_gate))
         ).astype(jnp.bfloat16)
-        return carry
-
-    lax.fori_loop(0, model // wide, normalize, 0)
-
-    for stream in range(4):
-        for k in range(SIDE):
-            large(stream, last - 1, k).wait_recv()
-    for copy in (to_next, to_relay, relay):
-        copy.wait_send()
+        grads_ref[at, units : 2 * units] = (cotangent * swish).astype(jnp.bfloat16)
+        return carry
+
+    lax.fori_loop(0, groups, gating, 0)
+
+    to_next.wait_send()
+    to_after.wait_send()
     for stream in range(4):
         for k in range(SIDE):
             if k < last:
                 small(stream, k).wait_send()
             for t in range(last):
                 large(stream, t, k).wait_send()
+            store(stream, k).wait()
     for by in range(SIDE):
         if by > 0:
             x_send(by).wait_send()
         core_send(by).wait_send()
 
 
-def front_part(states, query_doc, key_doc, spans, gain, gate_w, up_w, squares, w_proj):
+def front_part(
+    states, query_doc, key_doc, spans, gain, cotangent, gate_w, up_w, squares, w_proj
+):
     length, width = states.shape
     slots = spans.shape[0]
     rows, units = gate_w.shape
@@ -653,17 +703,21 @@
     return pl.pallas_call(
         front,
         out_shape=(
-            jax.ShapeDtypeStruct((SIDE * SIDE * rows, 2 * units), half),
+            jax.ShapeDtypeStruct((SIDE, SIDE, rows, 2 * units), half),
             jax.ShapeDtypeStruct((tokens, model), half),
             jax.ShapeDtypeStruct((slots, model), half),
+            jax.ShapeDtypeStruct((tokens, units), half),
+            jax.ShapeDtypeStruct((tokens, 2 * units), half),
         ),
-        in_specs=[whole] * 5 + [anywhere] * 6,
-        out_specs=(anywhere, whole, whole),
+        in_specs=[whole] * 6 + [anywhere] * 6,
+        out_specs=(anywhere, whole, whole, whole, whole),
         scratch_shapes=[
-            pltpu.VMEM((3, width, width), half),
+            pltpu.VMEM((SIDE, SIDE, rows, units), half),
+            pltpu.VMEM((SIDE, SIDE, rows, units), half),
             pltpu.VMEM((width, model), half),
+            pltpu.VMEM((tokens, model), half),
+            pltpu.VMEM((2, tokens, units), jnp.float32),
             pltpu.VMEM((2 * length, width), half),
-            pltpu.VMEM((length, width), half),
             pltpu.VMEM((length, width), half),
             pltpu.VMEM((3 * length, width), half),
             pltpu.VMEM((3 * length, width), half),
@@ -672,22 +726,23 @@
             pltpu.VMEM((slots, width), half),
             pltpu.VMEM((tokens, width), half),
             dma((6,)),
+            dma((4, SIDE)),
             dma((4, SIDE - 1)),
             dma((4, SIDE - 1)),
             dma((4, SIDE - 1, SIDE)),
             dma((4, SIDE - 1, SIDE)),
-            dma((3,)),
-            dma((3,)),
+            dma((2,)),
+            dma((2,)),
             dma((SIDE - 1,)),
             dma((SIDE - 1,)),
             dma((SIDE,)),
             dma((SIDE,)),
         ],
         compiler_params=pltpu.CompilerParams(
-            collective_id=1, has_side_effects=True, vmem_limit_bytes=56 * 1024 * 1024
+            collective_id=1, has_side_effects=True, vmem_limit_bytes=62 * 1024 * 1024
         ),
         name="front",
-    )(states, query_doc, key_doc, spans, gain, gate_w, up_w, *squares, w_proj)
+    )(states, query_doc, key_doc, spans, gain, cotangent, gate_w, up_w, *squares, w_proj)
 
 
 def doc_index(doc_lengths, positions):
@@ -726,12 +781,13 @@
     key_doc = doc_index(doc_lengths, key_pos)
     spans = slot_spans(patch_offsets[0], patch_counts[0, 0], length)
     units = gate_w.shape[1]
-    weights, normed, own_features = front_part(
+    weights, normed, own_features, hidden, both_grads = front_part(
         states,
         key_doc[2 * length :, None],
         key_doc[None],
         spans,
         norm_gain[None],
+        d_hidden.reshape(-1, units),
         gate_w,
         up_w,
         (w_query, w_key, w_value),
@@ -739,17 +795,9 @@
     )
     slot_count, model_width = own_features.shape
     seq_count = normed.shape[0] // slot_count
-    gate_pre = jnp.dot(normed, weights[:, :units], preferred_element_type=jnp.float32)
-    up_pre = jnp.dot(normed, weights[:, units:], preferred_element_type=jnp.float32)
-    sigmoid_gate = jax.nn.sigmoid(gate_pre)
-    hidden = (gate_pre * sigmoid_gate * up_pre).astype(jnp.bfloat16)
-    cotangent = d_hidden.reshape(seq_count * slot_count, units).astype(jnp.float32)
-    gate_grad = (
-        cotangent * up_pre * sigmoid_gate * (1.0 + gate_pre * (1.0 - sigmoid_gate))
-    ).astype(jnp.bfloat16)
-    up_grad = (cotangent * gate_pre * sigmoid_gate).astype(jnp.bfloat16)
-    both_grads = jnp.concatenate([gate_grad, up_grad], axis=1)
-    totals, inward = grad_sums(normed, both_grads, weights, slot_count)
+    totals, inward = grad_sums(
+        normed, both_grads, weights.reshape(model_width, 2 * units), slot_count
+    )
     grad_gate, grad_up = totals[0], totals[1]
     normed_grad = laid_out(inward, 1)
     own_float = own_features.astype(jnp.float32)

time: 260 us -> 236 us (0.908)
  matrix products: 16.5 us -> 0 us
  Pallas kernels: 231 us -> 221 us
    dot_general x2 -> x0, matrix products: 16.5 us -> none  [the longest x1 10.4 us: shards(): jnp.dot(normed, weights[:, :units], preferred_element_type=jnp.float32)]
    pallas_call x1, Pallas kernels: 139 us -> 130 us  [front_part(): pl.pallas_call(front, out_shape=(jax.ShapeDtypeStruct((SIDE, SIDE, rows,...]
where the time goes in v4:
time: 236 us; the launch traced here: 234 us
  Pallas kernels  221 us (94%)
  local copies, waits for them, and re-layouts  8.74 us (4%)
  other arithmetic  3.25 us (1%)
    pallas_call x1, Pallas kernels, front_part(): pl.pallas_call(front, out_shape=(jax.ShapeDtypeStruct((SIDE, SIDE, rows,...  130 us
    pallas_call x1, Pallas kernels, grad_sums(): pl.pallas_call(grad_rings, out_shape=(jax.ShapeDtypeStruct((2, rows, unit...  91.4 us

profile of v4, /device:TPU:0, one launch (start us, length us, event | category | flops | bytes accessed | tf_op | source)
XLA Modules:
  0.0 234.5 jit_solution(17967461151461739169)
XLA Ops:
  1.3 0.7 slice_bitcast_fusion.2
  2.0 0.7 fusion.5
  2.8 0.7 copy.28
  3.5 0.1 reduce-window.9
  3.6 0.1 reduce
  3.7 0.7 sub.18
  4.3 0.1 convert_reduce_fusion
  4.5 0.6 sub.21.key_doc_ref
  5.0 0.7 copy.30.spans_ref
  5.8 0.8 copy.29.query_doc_ref
  6.5 129.7 %front.1 = (bf16[4,4,256,1792]{3,2,1,0:T(8,128)(2,1)}, bf16[512,4096]{1,0:T(8,128)(2,1)}, bf16[64,4096]{1,0:T(8,128)(2,1)}, bf16[512,896]{1,0:T(8,128)(2,1)}, bf16[512,1792]{1,0:T(8,128)(2,1)}) custom-call(bf16[256,1280]{1,0:T(8,128)(2,1)} %bitcast.29, s32[256,1]{1,0:T(8,128)} %copy.29.query_doc_ref, s32[1,768]{1,0:T(1,128)} %sub.21.key_doc_ref, ...), custom_call_target="tpu_custom_call" | custom-call | tf_op jit(solution)/shard_map/front/pallas_call | solution.py:703
  136.3 91.4 %grad_rings.1 = (f32[2,256,896]{2,1,0:T(8,128)}, f32[8,64,512]{2,1,0:T(8,128)}) custom-call(bf16[512,4096]{1,0:T(8,128)(2,1)} %get-tuple-element.12.normed_ref, bf16[512,1792]{1,0:T(8,128)(2,1)} %get-tuple-element.13.grads_ref, bf16[4096,1792]{1,0:T(8,128)(2,1)} %bitcast.33), custom_call_target="tpu_custom_call" | custom-call | flops 15032385536 | bytes 200000000 | tf_op jit(solution)/shard_map/grad_rings/pallas_call | solution.py:274
  227.7 0.0 copy-start
  227.7 0.0 copy-start.2
  227.7 1.4 copy.32
  229.1 0.0 copy-start.1
  229.1 2.9 %slice_bitcast_fusion = (f32[256,896]{1,0:T(8,128)}, f32[256,896]{1,0:T(8,128)}) fusion(f32[2,256,896]{2,1,0:T(8,128)} %get-tuple-element.15), kind=kLoop, calls=%fused_computation.8 | loop fusion | bytes 3670016 | tf_op jit(solution)/shard_map/squeeze | solution.py:801
  232.0 0.0 copy-done
  232.0 0.0 copy-done.2
  232.0 0.3 fusion
  232.3 1.2 fusion.3
  233.6 0.0 copy-done.1
  233.6 0.9 copy.35
  (7 shorter events, 0.0 us)
Async XLA Ops:
  227.7 4.3 %copy-start = (bf16[64,4096]{1,0:T(8,128)(2,1)S(1)}, bf16[64,4096]{1,0:T(8,128)(2,1)}, u32[]{:S(2)}) copy-start(bf16[64,4096]{1,0:T(8,128)(2,1)} %get-tuple-element.16) | copy-start | bytes 1572868
  227.7 4.3 %copy-start.2 = (f32[4096]{0:T(1024)S(1)}, f32[4096]{0:T(1024)}, u32[]{:S(2)}) copy-start(f32[4096]{0:T(1024)} %param.20) | copy-start | bytes 49156
  229.1 4.5 %copy-start.1 = (bf16[512,896]{1,0:T(8,128)(2,1)S(1)}, bf16[512,896]{1,0:T(8,128)(2,1)}, u32[]{:S(2)}) copy-start(bf16[512,896]{1,0:T(8,128)(2,1)} %get-tuple-element.11) | copy-start | bytes 2752516

commit v5 on v4

--- a/solution.py
+++ b/solution.py
@@ -15,12 +15,6 @@
 masked_score = -1e30
 
 
-def laid_out(pieces, dim):
-    lengths = list(pieces.shape[1:])
-    lengths[dim] *= pieces.shape[0]
-    return jnp.moveaxis(pieces, 0, dim).reshape(lengths)
-
-
 MESH = pl.DeviceIdType.MESH
 SIDE = 4
 
@@ -32,9 +26,13 @@
 def grad_rings(
     normed_ref,
     grads_ref,
+    features_ref,
+    gain_ref,
     weights_hbm,
-    out_ref,
-    inward_ref,
+    gate_ref,
+    up_ref,
+    patch_ref,
+    inward,
     first,
     arrived,
     second,
@@ -58,7 +56,7 @@
     x, core = lax.div(seq, 2), lax.rem(seq, 2)
     z, y = lax.div(spot, SIDE), lax.rem(spot, SIDE)
     rows = first.shape[2]
-    units = out_ref.shape[2]
+    units = gate_ref.shape[1]
     chunks, _, _, slots, wide = parts.shape
 
     load = pltpu.make_async_copy(weights_hbm, weights, loaded)
@@ -198,7 +196,7 @@
                         ringed[t - 1, n] = value.astype(jnp.bfloat16)
                         x_hop(side, n, ringed.at[t - 1, n], t).start()
                     else:
-                        inward_ref[n] = value
+                        inward[n] = value
             return carry
 
         lax.fori_loop(0, chunks // 2, body, 0)
@@ -233,11 +231,34 @@
     lax.fori_loop(1, last, crossing, 0)
     x_phase(3)
 
+    def columns_of(n):
+        at = pl.ds(pl.multiple_of(n * wide, wide), wide)
+        return at, features_ref[:, at].astype(jnp.float32), gain_ref[:, at] * inward[n]
+
+    def means(n, carry):
+        _, features, scaled = columns_of(n)
+        return (
+            carry[0] + jnp.sum(features * features, axis=1, keepdims=True),
+            carry[1] + jnp.sum(features * scaled, axis=1, keepdims=True),
+        )
+
+    nothing = jnp.zeros((slots, 1), jnp.float32)
+    squares, products = lax.fori_loop(0, chunks, means, (nothing, nothing))
+    inverse = lax.rsqrt(squares / (chunks * wide) + epsilon)
+    factor = inverse * inverse * inverse * (products / (chunks * wide))
+
+    def patch_part(n, carry):
+        at, features, scaled = columns_of(n)
+        patch_ref[:, at] = inverse * scaled - features * factor
+        return carry
+
+    lax.fori_loop(0, chunks, patch_part, 0)
+
     for stream in range(4):
         kind, half = stream // 2, stream % 2
         value = total(stream, last)
         hop2(stream, second.at[stream], last - 1).wait_recv()
-        out_ref[kind, half * rows : (half + 1) * rows, :] = value + crossed[
+        (gate_ref, up_ref)[kind][half * rows : (half + 1) * rows, :] = value + crossed[
             stream, last - 1
         ].astype(jnp.float32)
 
@@ -263,8 +284,9 @@
     lax.fori_loop(0, chunks // 2, x_sent, 0)
 
 
-def grad_sums(normed, grads, weights, slots):
+def grad_sums(normed, grads, features, gain, weights):
     tokens, width = normed.shape
+    slots = features.shape[0]
     units = grads.shape[1] // 2
     rows = width // (SIDE * SIDE)
     half = rows // 2
@@ -274,12 +296,14 @@
     return pl.pallas_call(
         grad_rings,
         out_shape=(
-            jax.ShapeDtypeStruct((2, rows, units), jnp.float32),
-            jax.ShapeDtypeStruct((chunks, slots, wide), jnp.float32),
+            jax.ShapeDtypeStruct((rows, units), jnp.float32),
+            jax.ShapeDtypeStruct((rows, units), jnp.float32),
+            jax.ShapeDtypeStruct((slots, width), jnp.float32),
         ),
-        in_specs=[whole, whole, pl.BlockSpec(memory_space=pl.ANY)],
-        out_specs=(whole, whole),
+        in_specs=[whole] * 4 + [pl.BlockSpec(memory_space=pl.ANY)],
+        out_specs=(whole, whole, whole),
         scratch_shapes=[
+            pltpu.VMEM((chunks, slots, wide), jnp.float32),
             pltpu.VMEM((4, SIDE, *block), jnp.bfloat16),
             pltpu.VMEM((4, SIDE - 1, SIDE, *block), jnp.bfloat16),
             pltpu.VMEM((4, *block), jnp.bfloat16),
@@ -307,14 +331,30 @@
             transcendentals=0,
         ),
         name="grad_rings",
-    )(normed, grads, weights)
+    )(normed, grads, features, gain, weights)
+
+
+ORDER = (
+    "a0 b00",
+    "A0 a1 b01",
+    "B00 b10",
+    "A1 a2 b02",
+    "B01 b11",
+    "A2 b03",
+    "B10 b20",
+    "B02 b12",
+    "B11 b21",
+    "B03 b13",
+    "B12 b22",
+    "B13 b23"
+)
 
 
 def front(
     states_ref,
-    query_doc_ref,
-    key_doc_ref,
-    spans_ref,
+    lengths_ref,
+    offsets_ref,
+    count_ref,
     gain_ref,
     cotangent_ref,
     gate_hbm,
@@ -324,10 +364,11 @@
     value_hbm,
     proj_hbm,
     weights_ref,
-    normed_ref,
+    normed_hbm,
     own_features_ref,
     hidden_ref,
     grads_ref,
+    normed_ref,
     gates,
     ups,
     maps,
@@ -361,7 +402,7 @@
     groups, spots = 2 * SIDE, SIDE * SIDE
     devices = groups * spots
     length, width = states_ref.shape
-    slots = spans_ref.shape[0]
+    slots = offsets_ref.shape[1]
     heads = width // HEAD
     units = gate_hbm.shape[1]
     rows = gate_hbm.shape[0]
@@ -396,15 +437,13 @@
         pltpu.make_async_copy(source, target, loads.at[i])
         for i, (target, source) in enumerate(places)
     ]
-    for copy in load[:5]:
+    for copy in load[:2]:
         copy.start()
 
     greeted = (
         *around,
         next_block,
         device_of(here - 1),
-        after_next,
-        device_of(here - 2),
         other_core,
         *along_x,
     )
@@ -426,9 +465,8 @@
     recent = earlier.at[length : 2 * length]
     oldest = earlier.at[0:length]
     to_next = remote(states_ref, recent, put_s.at[0], got_s.at[0], next_block)
-    to_after = remote(states_ref, oldest, put_s.at[1], got_s.at[1], after_next)
+    to_after = remote(recent, oldest, put_s.at[1], got_s.at[1], next_block)
     to_next.start()
-    to_after.start()
     load[0].wait()
     load[1].wait()
 
@@ -471,20 +509,21 @@
 
     last = SIDE - 1
 
-    def spread(k):
+    steps = {
+        "a": lambda stream, k: small(stream, k).start(),
+        "A": lambda stream, k: small(stream, k).wait_recv(),
+        "b": lambda stream, t, k: large(stream, t, k).start(),
+        "B": lambda stream, t, k: large(stream, t, k).wait_recv(),
+    }
+
+    def tick(number):
         for stream in range(4):
-            if k > 0:
-                small(stream, k - 1).wait_recv()
-            if k < last:
-                small(stream, k).start()
-            large(stream, 0, k).start()
-
-    def pass_on(t, k):
-        for stream in range(4):
-            large(stream, t - 1, k).wait_recv()
-            large(stream, t, k).start()
-
-    spread(0)
+            for step in ORDER[number].split():
+                steps[step[0]](stream, *(int(digit) for digit in step[1:]))
+
+    tick(0)
+    for copy in load[2:5]:
+        copy.start()
 
     chunk = 2 * HEAD
     scale = 1.0 / math.sqrt(HEAD)
@@ -505,7 +544,10 @@
         return carry
 
     lax.fori_loop(0, width // chunk, make_queries, 0)
-    spread(1)
+    tick(1)
+    to_next.wait_recv()
+    to_after.start()
+    tick(2)
     load[3].wait()
     load[4].wait()
 
@@ -522,30 +564,50 @@
         lax.fori_loop(0, width // chunk, body, 0)
 
     keys_and_values(states_ref, 2 * length)
-    pass_on(1, 0)
-    spread(2)
+    tick(3)
 
     span = WINDOW + HEAD
     parts = length // HEAD
+
+    def iota(shape, dim):
+        return lax.broadcasted_iota(jnp.int32, shape, dim)
+
+    def turned(line, by):
+        count = line.shape[1]
+        picked = iota((count, count), 1) == iota((count, count), 0) + by
+        return jnp.sum(jnp.where(picked, line, 0.0), axis=1, keepdims=True)
+
+    docs = lengths_ref.shape[1]
+    lengths = lengths_ref[...].astype(jnp.float32)
+    earlier_docs = iota((docs, docs), 1) < iota((docs, docs), 0)
+    start_column = jnp.sum(jnp.where(earlier_docs, lengths, 0.0), axis=1, keepdims=True)
+    same = iota((docs, docs), 1) == iota((docs, docs), 0)
+    start_line = jnp.sum(jnp.where(same, start_column, 0.0), axis=0, keepdims=True)
+    key_pos = (here - 2) * length + iota((docs, 3 * length), 1)
+    query_pos = here * length + iota((length, docs), 0)
+    key_doc = jnp.sum(
+        jnp.where(start_column <= key_pos.astype(jnp.float32), 1.0, 0.0), axis=0, keepdims=True
+    )
+    query_doc = jnp.sum(
+        jnp.where(start_line <= query_pos.astype(jnp.float32), 1.0, 0.0), axis=1, keepdims=True
+    )
     for r in range(parts):
         row = lax.broadcasted_iota(jnp.int32, (HEAD, span), 0)
         column = lax.broadcasted_iota(jnp.int32, (HEAD, span), 1)
         allowed = (column > row) & (column <= row + WINDOW)
         start = 2 * length - WINDOW + r * HEAD
         allowed = allowed & (
-            key_doc_ref[:, start : start + span] == query_doc_ref[r * HEAD : (r + 1) * HEAD, :]
+            key_doc[:, start : start + span] == query_doc[r * HEAD : (r + 1) * HEAD, :]
         )
         bias[r] = jnp.where(allowed, 0.0, masked_score)
 
-    to_next.wait_recv()
     keys_and_values(recent, length)
-    pass_on(1, 1)
-    spread(3)
+    tick(4)
+    tick(5)
     to_after.wait_recv()
     keys_and_values(oldest, 0)
     load[5].start()
-    pass_on(2, 0)
-    pass_on(1, 2)
+    tick(6)
 
     def attend(h, carry):
         at = pl.ds(pl.multiple_of(h * HEAD, HEAD), HEAD)
@@ -563,13 +625,19 @@
         return carry
 
     lax.fori_loop(0, heads // 2, attend, 0)
-    pass_on(2, 1)
+    tick(7)
     lax.fori_loop(heads // 2, heads, attend, 0)
-    pass_on(1, 3)
-
-    begins, ends = spans_ref[:, 0:1], spans_ref[:, 1:2]
-    present = spans_ref[:, 2:3] > 0
-    byte = lax.broadcasted_iota(jnp.int32, (slots, length), 1)
+    tick(8)
+    tick(9)
+
+    offsets = offsets_ref[...].astype(jnp.float32)
+    count = count_ref[...].astype(jnp.float32)
+    slot = iota((slots, 1), 0).astype(jnp.float32)
+    present = slot < count
+    begins = turned(offsets, 0)
+    ends = jnp.where((slot == count - 1.0) | (slot == slots - 1.0), 1.0 * length, turned(offsets, 1))
+    begins, ends = jnp.where(present, begins, 0.0), jnp.where(present, ends, 0.0)
+    byte = iota((slots, length), 1).astype(jnp.float32)
     member = (byte >= begins) & (byte < ends)
     ones = jnp.where(member, 1.0, 0.0)
     pool_bias = jnp.where(member, 0.0, masked_score)
@@ -602,7 +670,7 @@
     for by in range(1, SIDE):
         x_send(by).start()
     core_send(0).start()
-    pass_on(2, 2)
+    tick(10)
     for by in (1, 3, 2):
         x_send(by).wait_recv()
         core_send(by).start()
@@ -621,22 +689,24 @@
 
     squares = jnp.zeros((groups * slots, 1), jnp.float32)
     squares = lax.fori_loop(0, model // wide // 2, project, squares)
-    pass_on(2, 3)
+    tick(11)
     squares = lax.fori_loop(model // wide // 2, model // wide, project, squares)
     inverse = lax.rsqrt(squares / model + epsilon)
     own_features_ref[...] = normed_ref[mine, :]
 
     def normalize(n, carry):
         at = pl.ds(pl.multiple_of(n * rows, rows), rows)
-        turned = (n % SIDE) * SIDE + n // SIDE
+        place_turned = (n % SIDE) * SIDE + n // SIDE
         value = (normed_ref[:, at].astype(jnp.float32) * inverse * gain_ref[:, at]).astype(
             jnp.bfloat16
         )
         normed_ref[:, at] = value
-        crossed[:, pl.ds(pl.multiple_of(turned * rows, rows), rows)] = value
+        crossed[:, pl.ds(pl.multiple_of(place_turned * rows, rows), rows)] = value
         return carry
 
     lax.fori_loop(0, model // rows, normalize, 0)
+    keep = pltpu.make_async_copy(normed_ref, normed_hbm, loads.at[6])
+    keep.start()
     sums[...] = jnp.zeros_like(sums)
 
     def accumulate(t, carry):
@@ -675,6 +745,7 @@
 
     to_next.wait_send()
     to_after.wait_send()
+    keep.wait()
     for stream in range(4):
         for k in range(SIDE):
             if k < last:
@@ -689,10 +760,10 @@
 
 
 def front_part(
-    states, query_doc, key_doc, spans, gain, cotangent, gate_w, up_w, squares, w_proj
+    states, lengths, offsets, count, gain, cotangent, gate_w, up_w, squares, w_proj
 ):
     length, width = states.shape
-    slots = spans.shape[0]
+    slots = offsets.shape[1]
     rows, units = gate_w.shape
     model = w_proj.shape[1]
     tokens = 2 * SIDE * slots
@@ -710,8 +781,9 @@
             jax.ShapeDtypeStruct((tokens, 2 * units), half),
         ),
         in_specs=[whole] * 6 + [anywhere] * 6,
-        out_specs=(anywhere, whole, whole, whole, whole),
+        out_specs=(anywhere, anywhere, whole, whole, whole),
         scratch_shapes=[
+            pltpu.VMEM((tokens, model), half),
             pltpu.VMEM((SIDE, SIDE, rows, units), half),
             pltpu.VMEM((SIDE, SIDE, rows, units), half),
             pltpu.VMEM((width, model), half),
@@ -725,7 +797,7 @@
             pltpu.VMEM((length, width), half),
             pltpu.VMEM((slots, width), half),
             pltpu.VMEM((tokens, width), half),
-            dma((6,)),
+            dma((7,)),
             dma((4, SIDE)),
             dma((4, SIDE - 1)),
             dma((4, SIDE - 1)),
@@ -742,22 +814,7 @@
             collective_id=1, has_side_effects=True, vmem_limit_bytes=62 * 1024 * 1024
         ),
         name="front",
-    )(states, query_doc, key_doc, spans, gain, cotangent, gate_w, up_w, *squares, w_proj)
-
-
-def doc_index(doc_lengths, positions):
-    starts = jnp.cumsum(doc_lengths) - doc_lengths
-    inside = (starts[None, :] <= positions[:, None]).astype(jnp.int32)
-    return jnp.sum(inside, axis=1) - 1
-
-
-def slot_spans(offsets, count, length):
-    slot_ids = jnp.arange(offsets.shape[0], dtype=jnp.int32)
-    following = jnp.concatenate([offsets[1:], jnp.full((1,), length, jnp.int32)])
-    ends = jnp.where(slot_ids == count - 1, length, following)
-    present = slot_ids < count
-    begins, ends = jnp.where(present, offsets, 0), jnp.where(present, ends, 0)
-    return jnp.stack([begins, ends, present.astype(jnp.int32)], axis=1)
+    )(states, lengths, offsets, count, gain, cotangent, gate_w, up_w, *squares, w_proj)
 
 
 def shards(
@@ -774,18 +831,12 @@
     up_w,
     d_hidden,
 ):
-    states = bytes_in[0]
-    length = states.shape[0]
-    first_pos = lax.axis_index(("seq", "fsdp")) * length
-    key_pos = first_pos - 2 * length + jnp.arange(3 * length, dtype=jnp.int32)
-    key_doc = doc_index(doc_lengths, key_pos)
-    spans = slot_spans(patch_offsets[0], patch_counts[0, 0], length)
     units = gate_w.shape[1]
     weights, normed, own_features, hidden, both_grads = front_part(
-        states,
-        key_doc[2 * length :, None],
-        key_doc[None],
-        spans,
+        bytes_in[0],
+        doc_lengths[None],
+        patch_offsets,
+        patch_counts,
         norm_gain[None],
         d_hidden.reshape(-1, units),
         gate_w,
@@ -793,22 +844,15 @@
         (w_query, w_key, w_value),
         w_proj,
     )
-    slot_count, model_width = own_features.shape
-    seq_count = normed.shape[0] // slot_count
-    totals, inward = grad_sums(
-        normed, both_grads, weights.reshape(model_width, 2 * units), slot_count
+    model_width = normed.shape[1]
+    grad_gate, grad_up, patch_grad = grad_sums(
+        normed,
+        both_grads,
+        own_features,
+        norm_gain[None],
+        weights.reshape(model_width, 2 * units),
     )
-    grad_gate, grad_up = totals[0], totals[1]
-    normed_grad = laid_out(inward, 1)
-    own_float = own_features.astype(jnp.float32)
-    own_inverse = lax.rsqrt(
-        jnp.mean(own_float * own_float, axis=1, keepdims=True) + epsilon
-    )
-    scaled = norm_gain * normed_grad
-    patch_grad = own_inverse * scaled - own_float * (
-        own_inverse * own_inverse * own_inverse
-    ) * jnp.mean(scaled * own_float, axis=1, keepdims=True)
-    return (hidden.reshape(seq_count, slot_count, units), grad_gate, grad_up, patch_grad[None])
+    return (hidden.reshape(d_hidden.shape), grad_gate, grad_up, patch_grad[None])
 
 
 def solution(mesh):

time: 236 us -> 218 us (0.924)
  Pallas kernels: 221 us -> 212 us
  local copies, waits for them, and re-layouts: 8.74 us -> 4.99 us
  other arithmetic: 3.25 us -> 0 us
    pallas_call x1, Pallas kernels: 130 us -> 119 us  [front_part(): pl.pallas_call(front, out_shape=(jax.ShapeDtypeStruct((SIDE, SIDE, rows,...]
    unnamed x7 -> x10, local copies, waits for them, and re-layouts: 0.94 us -> 4.99 us
    squeeze x1 -> x0, local copies, waits for them, and re-layouts: 2.88 us -> none  [shards(): grad_gate, grad_up = (totals[0], totals[1])]
where the time goes in v5:
time: 218 us
  Pallas kernels  212 us (97%)
  local copies, waits for them, and re-layouts  4.99 us (2%)
    pallas_call x1, Pallas kernels, front_part(): pl.pallas_call(front, out_shape=(jax.ShapeDtypeStruct((SIDE, SIDE, rows,...  119 us
    pallas_call x1, Pallas kernels, grad_sums(): pl.pallas_call(grad_rings, out_shape=(jax.ShapeDtypeStruct((rows, units),...  93 us
    unnamed x10, local copies, waits for them, and re-layouts  4.99 us

profile of v5, /device:TPU:0, one launch (start us, length us, event | category | flops | bytes accessed | tf_op | source)
XLA Modules:
  0.0 218.1 jit_solution(10725706446288910531)
XLA Ops:
  1.3 118.8 %front.1 = (bf16[4,4,256,1792]{3,2,1,0:T(8,128)(2,1)}, bf16[512,4096]{1,0:T(8,128)(2,1)}, bf16[64,4096]{1,0:T(8,128)(2,1)}, bf16[512,896]{1,0:T(8,128)(2,1)}, bf16[512,1792]{1,0:T(8,128)(2,1)}) custom-call(bf16[256,1280]{1,0:T(8,128)(2,1)} %bitcast.10, s32[1,32]{1,0:T(1,128)} %bitcast.13, s32[1,64]{1,0:T(1,128)} %offsets_ref.1, s32[1,1]{1,0:T(1,128)S(6)} %copy.20.count_ref, ...), custom_call_target="tpu_custom_call" | custom-call | tf_op jit(solution)/shard_map/front/pallas_call | solution.py:774
  120.1 0.0 copy-start.1
  120.1 93.0 %grad_rings.1 = (f32[256,896]{1,0:T(8,128)}, f32[256,896]{1,0:T(8,128)}, f32[64,4096]{1,0:T(8,128)}) custom-call(bf16[512,4096]{1,0:T(8,128)(2,1)} %get-tuple-element.13.normed_ref, bf16[512,1792]{1,0:T(8,128)(2,1)} %get-tuple-element.14.grads_ref, bf16[64,4096]{1,0:T(8,128)(2,1)} %get-tuple-element.15.features_ref, f32[1,4096]{1,0:T(1,128)} %bitcast.12, ...), custom_call_target="tpu_custom_call" | custom-call | flops 15032385536 | bytes 200000000 | tf_op jit(solution)/shard_map/grad_rings/pallas_call | solution.py:296
  213.1 0.0 copy-start.2
  213.1 0.0 copy-start
  213.1 0.0 copy-done.1
  213.1 0.9 copy.21
  214.1 2.2 copy.22
  216.2 0.0 copy-done.2
  216.2 0.9 copy.23
  217.2 0.0 copy-done
  217.2 1.0 copy.24
Async XLA Ops:
  120.1 93.0 %copy-start.1 = (bf16[512,896]{1,0:T(8,128)(2,1)S(1)}, bf16[512,896]{1,0:T(8,128)(2,1)}, u32[]{:S(2)}) copy-start(bf16[512,896]{1,0:T(8,128)(2,1)} %get-tuple-element.12) | copy-start | bytes 2752516
  213.1 3.1 %copy-start.2 = (f32[256,896]{1,0:T(8,128)S(1)}, f32[256,896]{1,0:T(8,128)}, u32[]{:S(2)}) copy-start(f32[256,896]{1,0:T(8,128)} %get-tuple-element.26) | copy-start | bytes 2752516
  213.1 4.0 %copy-start = (f32[64,4096]{1,0:T(8,128)S(1)}, f32[64,4096]{1,0:T(8,128)}, u32[]{:S(2)}) copy-start(f32[64,4096]{1,0:T(8,128)} %get-tuple-element.19) | copy-start | bytes 3145732

commit v6 on v5

--- a/solution.py
+++ b/solution.py
@@ -28,7 +28,8 @@
     grads_ref,
     features_ref,
     gain_ref,
-    weights_hbm,
+    gates,
+    ups,
     gate_ref,
     up_ref,
     patch_ref,
@@ -37,7 +38,6 @@
     arrived,
     second,
     crossed,
-    weights,
     parts,
     paired,
     ringed,
@@ -45,11 +45,11 @@
     got,
     put2,
     got2,
-    loaded,
     put3,
     got3,
     put4,
     got4,
+    ready,
 ):
     seq = lax.axis_index("seq")
     spot = lax.axis_index("fsdp")
@@ -58,9 +58,6 @@
     rows = first.shape[2]
     units = gate_ref.shape[1]
     chunks, _, _, slots, wide = parts.shape
-
-    load = pltpu.make_async_copy(weights_hbm, weights, loaded)
-    load.start()
 
     around = (
         (seq, wrapped(z + 1) * SIDE + y),
@@ -71,10 +68,9 @@
         (wrapped(x - 1) * 2 + core, spot),
         (x * 2 + 1 - core, spot),
     )
-    barrier = pltpu.get_barrier_semaphore()
     for neighbour in around:
-        pl.semaphore_signal(barrier, inc=1, device_id=neighbour, device_id_type=MESH)
-    pl.semaphore_wait(barrier, len(around))
+        pl.semaphore_signal(ready, inc=1, device_id=neighbour, device_id_type=MESH)
+    pl.semaphore_wait(ready, len(around))
 
     def place(stream):
         kind, half = stream // 2, stream % 2
@@ -146,18 +142,24 @@
         return carry
 
     lax.fori_loop(0, SIDE, opening, 0)
-    load.wait()
 
     def input_part(n):
-        at = pl.multiple_of(n * wide, wide)
-        value = lax.dot_general(
-            grads_ref[...],
-            weights[pl.ds(at, wide), :],
-            (((1,), (1,)), ((), ())),
-            preferred_element_type=jnp.float32,
-        ).astype(jnp.bfloat16)
-        for block in range(2 * SIDE):
-            parts[n, block % 2, block // 2] = value[block * slots : (block + 1) * slots]
+        depth = 2 * rows
+        for column in range(wide // depth):
+            zb, yb = lax.div(n, 2), 2 * lax.rem(n, 2) + column
+            value = 0.0
+            for kind, block in enumerate((gates[zb, yb], ups[yb, zb])):
+                value += lax.dot_general(
+                    grads_ref[:, kind * units : (kind + 1) * units],
+                    block,
+                    (((1,), (1,)), ((), ())),
+                    preferred_element_type=jnp.float32,
+                )
+            value = value.astype(jnp.bfloat16)
+            for block in range(2 * SIDE):
+                parts[n, block % 2, block // 2, :, column * depth : (column + 1) * depth] = (
+                    value[block * slots : (block + 1) * slots]
+                )
         across_cores(n).start()
 
     def middle(t, busy):
@@ -284,56 +286,6 @@
     lax.fori_loop(0, chunks // 2, x_sent, 0)
 
 
-def grad_sums(normed, grads, features, gain, weights):
-    tokens, width = normed.shape
-    slots = features.shape[0]
-    units = grads.shape[1] // 2
-    rows = width // (SIDE * SIDE)
-    half = rows // 2
-    block = (half, units)
-    chunks, wide = 8, width // 8
-    whole = pl.BlockSpec(memory_space=pltpu.VMEM)
-    return pl.pallas_call(
-        grad_rings,
-        out_shape=(
-            jax.ShapeDtypeStruct((rows, units), jnp.float32),
-            jax.ShapeDtypeStruct((rows, units), jnp.float32),
-            jax.ShapeDtypeStruct((slots, width), jnp.float32),
-        ),
-        in_specs=[whole] * 4 + [pl.BlockSpec(memory_space=pl.ANY)],
-        out_specs=(whole, whole, whole),
-        scratch_shapes=[
-            pltpu.VMEM((chunks, slots, wide), jnp.float32),
-            pltpu.VMEM((4, SIDE, *block), jnp.bfloat16),
-            pltpu.VMEM((4, SIDE - 1, SIDE, *block), jnp.bfloat16),
-            pltpu.VMEM((4, *block), jnp.bfloat16),
-            pltpu.VMEM((4, SIDE - 1, *block), jnp.bfloat16),
-            pltpu.VMEM(weights.shape, jnp.bfloat16),
-            pltpu.VMEM((chunks, 2, SIDE, slots, wide), jnp.bfloat16),
-            pltpu.VMEM((chunks, SIDE, slots, wide), jnp.bfloat16),
-            pltpu.VMEM((SIDE - 1, chunks, slots, wide), jnp.bfloat16),
-            pltpu.SemaphoreType.DMA((4, SIDE - 1, SIDE)),
-            pltpu.SemaphoreType.DMA((4, SIDE - 1, SIDE)),
-            pltpu.SemaphoreType.DMA((4, SIDE - 1)),
-            pltpu.SemaphoreType.DMA((4, SIDE - 1)),
-            pltpu.SemaphoreType.DMA(()),
-            pltpu.SemaphoreType.DMA((chunks,)),
-            pltpu.SemaphoreType.DMA((chunks,)),
-            pltpu.SemaphoreType.DMA((SIDE - 1, chunks)),
-            pltpu.SemaphoreType.DMA((SIDE - 1, chunks)),
-        ],
-        compiler_params=pltpu.CompilerParams(
-            collective_id=0, has_side_effects=True, vmem_limit_bytes=60 * 1024 * 1024
-        ),
-        cost_estimate=pl.CostEstimate(
-            flops=4 * tokens * width * 2 * units,
-            bytes_accessed=200_000_000,
-            transcendentals=0,
-        ),
-        name="grad_rings",
-    )(normed, grads, features, gain, weights)
-
-
 ORDER = (
     "a0 b00",
     "A0 a1 b01",
@@ -363,8 +315,6 @@
     key_hbm,
     value_hbm,
     proj_hbm,
-    weights_ref,
-    normed_hbm,
     own_features_ref,
     hidden_ref,
     grads_ref,
@@ -383,7 +333,6 @@
     pooled,
     contexts,
     loads,
-    stores,
     put_a,
     got_a,
     put_b,
@@ -495,18 +444,6 @@
             region, region, put_b.at[stream, t, k], got_b.at[stream, t, k], device
         )
 
-    def store(stream, t):
-        kind, half = stream // 2, stream % 2
-        buffer, far, columns = place(stream, t)
-        target = slice(kind * units + columns.start, kind * units + columns.stop)
-        if kind == 0:
-            target = weights_ref.at[far, :, :, target]
-        else:
-            target = weights_ref.at[:, far, :, target]
-        return pltpu.make_async_copy(
-            buffer.at[far, :, :, columns], target, stores.at[stream, t]
-        )
-
     last = SIDE - 1
 
     steps = {
@@ -705,8 +642,6 @@
         return carry
 
     lax.fori_loop(0, model // rows, normalize, 0)
-    keep = pltpu.make_async_copy(normed_ref, normed_hbm, loads.at[6])
-    keep.start()
     sums[...] = jnp.zeros_like(sums)
 
     def accumulate(t, carry):
@@ -717,7 +652,6 @@
                     large(stream, last - 1, k).wait_recv()
 
         for stream in range(4):
-            store(stream, t).start()
             buffer, far, columns = place(stream, t)
             kind, count = stream // 2, columns.stop - columns.start
             deep = SIDE * rows
@@ -745,21 +679,128 @@
 
     to_next.wait_send()
     to_after.wait_send()
-    keep.wait()
     for stream in range(4):
         for k in range(SIDE):
             if k < last:
                 small(stream, k).wait_send()
             for t in range(last):
                 large(stream, t, k).wait_send()
-            store(stream, k).wait()
     for by in range(SIDE):
         if by > 0:
             x_send(by).wait_send()
         core_send(by).wait_send()
 
 
-def front_part(
+def layer(
+    states_ref,
+    lengths_ref,
+    offsets_ref,
+    count_ref,
+    gain_ref,
+    cotangent_ref,
+    gate_hbm,
+    up_hbm,
+    query_hbm,
+    key_hbm,
+    value_hbm,
+    proj_hbm,
+    hidden_ref,
+    gate_ref,
+    up_ref,
+    patch_ref,
+    own_features,
+    grads,
+    normed,
+    gates,
+    ups,
+    earlier,
+    contexts,
+    *semaphores,
+):
+    half, full = jnp.bfloat16, jnp.float32
+    length, width = states_ref.shape
+    rows, units = gate_hbm.shape
+    tokens, model = normed.shape
+    slots = patch_ref.shape[0]
+    chunks, wide = 8, model // 8
+    block = (rows // 2, units)
+
+    def first_scope(maps, crossed, sums, queries, keys, values, bias, mixed, pooled):
+        front(
+            states_ref,
+            lengths_ref,
+            offsets_ref,
+            count_ref,
+            gain_ref,
+            cotangent_ref,
+            gate_hbm,
+            up_hbm,
+            query_hbm,
+            key_hbm,
+            value_hbm,
+            proj_hbm,
+            own_features,
+            hidden_ref,
+            grads,
+            normed,
+            gates,
+            ups,
+            maps,
+            crossed,
+            sums,
+            earlier,
+            queries,
+            keys,
+            values,
+            bias,
+            mixed,
+            pooled,
+            contexts,
+            *semaphores[:11],
+        )
+
+    pl.run_scoped(
+        first_scope,
+        pltpu.VMEM((width, model), half),
+        pltpu.VMEM((tokens, model), half),
+        pltpu.VMEM((2, tokens, units), full),
+        pltpu.VMEM((length, width), half),
+        pltpu.VMEM((3 * length, width), half),
+        pltpu.VMEM((3 * length, width), half),
+        pltpu.VMEM((length // HEAD, HEAD, WINDOW + HEAD), full),
+        pltpu.VMEM((length, width), half),
+        pltpu.VMEM((slots, width), half),
+    )
+
+    def second_scope(*scratch):
+        grad_rings(
+            normed,
+            grads,
+            own_features,
+            gain_ref,
+            gates,
+            ups,
+            gate_ref,
+            up_ref,
+            patch_ref,
+            *scratch,
+            *semaphores[11:],
+        )
+
+    pl.run_scoped(
+        second_scope,
+        pltpu.VMEM((chunks, slots, wide), full),
+        pltpu.VMEM((4, SIDE, *block), half),
+        pltpu.VMEM((4, SIDE - 1, SIDE, *block), half),
+        pltpu.VMEM((4, *block), half),
+        pltpu.VMEM((4, SIDE - 1, *block), half),
+        pltpu.VMEM((chunks, 2, SIDE, slots, wide), half),
+        pltpu.VMEM((chunks, SIDE, slots, wide), half),
+        pltpu.VMEM((SIDE - 1, chunks, slots, wide), half),
+    )
+
+
+def whole_layer(
     states, lengths, offsets, count, gain, cotangent, gate_w, up_w, squares, w_proj
 ):
     length, width = states.shape
@@ -767,38 +808,30 @@
     rows, units = gate_w.shape
     model = w_proj.shape[1]
     tokens = 2 * SIDE * slots
+    chunks = 8
     dma = pltpu.SemaphoreType.DMA
     whole = pl.BlockSpec(memory_space=pltpu.VMEM)
     anywhere = pl.BlockSpec(memory_space=pl.ANY)
-    half = jnp.bfloat16
+    half, full = jnp.bfloat16, jnp.float32
     return pl.pallas_call(
-        front,
+        layer,
         out_shape=(
-            jax.ShapeDtypeStruct((SIDE, SIDE, rows, 2 * units), half),
-            jax.ShapeDtypeStruct((tokens, model), half),
-            jax.ShapeDtypeStruct((slots, model), half),
             jax.ShapeDtypeStruct((tokens, units), half),
-            jax.ShapeDtypeStruct((tokens, 2 * units), half),
+            jax.ShapeDtypeStruct((rows, units), full),
+            jax.ShapeDtypeStruct((rows, units), full),
+            jax.ShapeDtypeStruct((slots, model), full),
         ),
         in_specs=[whole] * 6 + [anywhere] * 6,
-        out_specs=(anywhere, anywhere, whole, whole, whole),
+        out_specs=(whole,) * 4,
         scratch_shapes=[
+            pltpu.VMEM((slots, model), half),
+            pltpu.VMEM((tokens, 2 * units), half),
             pltpu.VMEM((tokens, model), half),
             pltpu.VMEM((SIDE, SIDE, rows, units), half),
             pltpu.VMEM((SIDE, SIDE, rows, units), half),
-            pltpu.VMEM((width, model), half),
-            pltpu.VMEM((tokens, model), half),
-            pltpu.VMEM((2, tokens, units), jnp.float32),
             pltpu.VMEM((2 * length, width), half),
-            pltpu.VMEM((length, width), half),
-            pltpu.VMEM((3 * length, width), half),
-            pltpu.VMEM((3 * length, width), half),
-            pltpu.VMEM((length // HEAD, HEAD, WINDOW + HEAD), jnp.float32),
-            pltpu.VMEM((length, width), half),
-            pltpu.VMEM((slots, width), half),
             pltpu.VMEM((tokens, width), half),
-            dma((7,)),
-            dma((4, SIDE)),
+            dma((6,)),
             dma((4, SIDE - 1)),
             dma((4, SIDE - 1)),
             dma((4, SIDE - 1, SIDE)),
@@ -809,11 +842,20 @@
             dma((SIDE - 1,)),
             dma((SIDE,)),
             dma((SIDE,)),
+            dma((4, SIDE - 1, SIDE)),
+            dma((4, SIDE - 1, SIDE)),
+            dma((4, SIDE - 1)),
+            dma((4, SIDE - 1)),
+            dma((chunks,)),
+            dma((chunks,)),
+            dma((SIDE - 1, chunks)),
+            dma((SIDE - 1, chunks)),
+            pltpu.SemaphoreType.REGULAR,
         ],
         compiler_params=pltpu.CompilerParams(
-            collective_id=1, has_side_effects=True, vmem_limit_bytes=62 * 1024 * 1024
+            collective_id=0, has_side_effects=True, vmem_limit_bytes=62 * 1024 * 1024
         ),
-        name="front",
+        name="layer",
     )(states, lengths, offsets, count, gain, cotangent, gate_w, up_w, *squares, w_proj)
 
 
@@ -832,7 +874,7 @@
     d_hidden,
 ):
     units = gate_w.shape[1]
-    weights, normed, own_features, hidden, both_grads = front_part(
+    hidden, grad_gate, grad_up, patch_grad = whole_layer(
         bytes_in[0],
         doc_lengths[None],
         patch_offsets,
@@ -843,14 +885,6 @@
         up_w,
         (w_query, w_key, w_value),
         w_proj,
-    )
-    model_width = normed.shape[1]
-    grad_gate, grad_up, patch_grad = grad_sums(
-        normed,
-        both_grads,
-        own_features,
-        norm_gain[None],
-        weights.reshape(model_width, 2 * units),
     )
     return (hidden.reshape(d_hidden.shape), grad_gate, grad_up, patch_grad[None])
 

time: 218 us -> 214 us (0.982)
  Pallas kernels: 212 us -> 206 us
    pallas_call x2 -> x1, Pallas kernels: 212 us -> 206 us  [whole_layer(): pl.pallas_call(layer, out_shape=(jax.ShapeDtypeStruct((tokens, units), ha...]
    unnamed x10 -> x8, local copies, waits for them, and re-layouts: 4.99 us -> 6.37 us
where the time goes in v6:
time: 214 us
  Pallas kernels  206 us (96%)
  local copies, waits for them, and re-layouts  6.37 us (3%)
    pallas_call x1, Pallas kernels, whole_layer(): pl.pallas_call(layer, out_shape=(jax.ShapeDtypeStruct((tokens, units), ha...  206 us
    unnamed x8, local copies, waits for them, and re-layouts  6.37 us

profile of v6, /device:TPU:0, one launch (start us, length us, event | category | flops | bytes accessed | tf_op | source)
XLA Modules:
  0.0 214.0 jit_solution(6735560849876130806)
XLA Ops:
  1.3 206.3 %layer.1 = (bf16[512,896]{1,0:T(8,128)(2,1)}, f32[256,896]{1,0:T(8,128)}, f32[256,896]{1,0:T(8,128)}, f32[64,4096]{1,0:T(8,128)}) custom-call(bf16[256,1280]{1,0:T(8,128)(2,1)} %bitcast.9, s32[1,32]{1,0:T(1,128)} %bitcast.11, s32[1,64]{1,0:T(1,128)} %offsets_ref.1, s32[1,1]{1,0:T(1,128)S(6)} %copy.20.count_ref, f32[1,4096]{1,0:T(1,128)} %bitcast.10, ...), custom_call_target="tpu_custom_call" | custom-call | tf_op jit(solution)/shard_map/layer/pallas_call | solution.py:816
  207.6 0.0 copy-start.1
  207.6 0.0 copy-start
  207.6 2.3 %copy.21 = bf16[8,64,896]{2,1,0:T(8,128)(2,1)} copy(bf16[8,64,896]{2,1,0:T(8,128)(2,1)} %bitcast.7) | data formatting | bytes 1835008
  210.0 2.2 %copy.22 = f32[256,896]{1,0:T(8,128)} copy(f32[256,896]{1,0:T(8,128)} %get-tuple-element.17) | data formatting | bytes 1835008
  212.1 0.0 copy-done.1
  212.1 0.9 copy.23
  213.0 0.0 copy-done
  213.1 1.0 copy.24
Async XLA Ops:
  207.6 4.5 %copy-start.1 = (f32[256,896]{1,0:T(8,128)S(1)}, f32[256,896]{1,0:T(8,128)}, u32[]{:S(2)}) copy-start(f32[256,896]{1,0:T(8,128)} %get-tuple-element.18) | copy-start | bytes 2752516
  207.6 5.4 %copy-start = (f32[64,4096]{1,0:T(8,128)S(1)}, f32[64,4096]{1,0:T(8,128)}, u32[]{:S(2)}) copy-start(f32[64,4096]{1,0:T(8,128)} %get-tuple-element.11) | copy-start | bytes 3145732

commit v7 on v6

--- a/solution.py
+++ b/solution.py
@@ -540,6 +540,19 @@
 
     keys_and_values(recent, length)
     tick(4)
+    offsets = offsets_ref[...].astype(jnp.float32)
+    count = count_ref[...].astype(jnp.float32)
+    slot = iota((slots, 1), 0).astype(jnp.float32)
+    present = slot < count
+    begins = turned(offsets, 0)
+    ends = jnp.where((slot == count - 1.0) | (slot == slots - 1.0), 1.0 * length, turned(offsets, 1))
+    begins, ends = jnp.where(present, begins, 0.0), jnp.where(present, ends, 0.0)
+    byte = iota((slots, length), 1).astype(jnp.float32)
+    member = (byte >= begins) & (byte < ends)
+    ones = jnp.where(member, 1.0, 0.0)
+    pool_bias = jnp.where(member, 0.0, masked_score)
+    sizes = jnp.maximum(jnp.sum(ones, axis=1, keepdims=True), 1.0)
+    members = ones.astype(jnp.bfloat16)
     tick(5)
     to_after.wait_recv()
     keys_and_values(oldest, 0)
@@ -561,25 +574,6 @@
             ).astype(jnp.bfloat16)
         return carry
 
-    lax.fori_loop(0, heads // 2, attend, 0)
-    tick(7)
-    lax.fori_loop(heads // 2, heads, attend, 0)
-    tick(8)
-    tick(9)
-
-    offsets = offsets_ref[...].astype(jnp.float32)
-    count = count_ref[...].astype(jnp.float32)
-    slot = iota((slots, 1), 0).astype(jnp.float32)
-    present = slot < count
-    begins = turned(offsets, 0)
-    ends = jnp.where((slot == count - 1.0) | (slot == slots - 1.0), 1.0 * length, turned(offsets, 1))
-    begins, ends = jnp.where(present, begins, 0.0), jnp.where(present, ends, 0.0)
-    byte = iota((slots, length), 1).astype(jnp.float32)
-    member = (byte >= begins) & (byte < ends)
-    ones = jnp.where(member, 1.0, 0.0)
-    pool_bias = jnp.where(member, 0.0, masked_score)
-    sizes = jnp.maximum(jnp.sum(ones, axis=1, keepdims=True), 1.0)
-    pooled[...] = (dot(ones.astype(jnp.bfloat16), mixed[...]) / sizes).astype(jnp.bfloat16)
     mine = pl.ds(pl.multiple_of(seq * slots, slots), slots)
 
     def pool(h, carry):
@@ -591,28 +585,46 @@
         contexts[mine, at] = jnp.where(present, summed, 0.0).astype(jnp.bfloat16)
         return carry
 
-    lax.fori_loop(0, heads, pool, 0)
-
-    def context_of(group):
-        return contexts.at[pl.ds(pl.multiple_of(group * slots, slots), slots)]
-
-    def x_send(by):
-        region = context_of(seq)
-        return remote(region, region, put_x.at[by - 1], got_x.at[by - 1], along_x[by - 1])
-
-    def core_send(by):
-        region = context_of(wrapped(x - by) * 2 + core)
-        return remote(region, region, put_c.at[by], got_c.at[by], other_core)
-
-    for by in range(1, SIDE):
-        x_send(by).start()
-    core_send(0).start()
-    tick(10)
-    for by in (1, 3, 2):
-        x_send(by).wait_recv()
-        core_send(by).start()
-    for by in range(SIDE):
-        core_send(by).wait_recv()
+    def context_of(group, part):
+        at = pl.ds(pl.multiple_of(group * slots, slots), slots)
+        return contexts.at[at, part * width // 2 : (part + 1) * width // 2]
+
+    def x_send(by, part):
+        region = context_of(seq, part)
+        return remote(
+            region,
+            region,
+            put_x.at[part, by - 1],
+            got_x.at[part, by - 1],
+            along_x[by - 1],
+        )
+
+    def core_send(by, part):
+        region = context_of(wrapped(x - by) * 2 + core, part)
+        return remote(
+            region, region, put_c.at[part, by], got_c.at[part, by], other_core
+        )
+
+    for part in range(2):
+        first_head, stop_head = part * heads // 2, (part + 1) * heads // 2
+        some = slice(first_head * HEAD, stop_head * HEAD)
+        lax.fori_loop(first_head, stop_head, attend, 0)
+        pooled[:, some] = (dot(members, mixed[:, some]) / sizes).astype(jnp.bfloat16)
+        lax.fori_loop(first_head, stop_head, pool, 0)
+        for by in range(1, SIDE):
+            x_send(by, part).start()
+        core_send(0, part).start()
+        tick(7 + part)
+    tick(9)
+    for part in range(2):
+        for by in (1, 3, 2):
+            x_send(by, part).wait_recv()
+            core_send(by, part).start()
+        if part == 0:
+            tick(10)
+    for part in range(2):
+        for by in range(SIDE):
+            core_send(by, part).wait_recv()
     load[5].wait()
 
     wide = 4 * HEAD
@@ -685,10 +697,11 @@
                 small(stream, k).wait_send()
             for t in range(last):
                 large(stream, t, k).wait_send()
-    for by in range(SIDE):
-        if by > 0:
-            x_send(by).wait_send()
-        core_send(by).wait_send()
+    for part in range(2):
+        for by in range(SIDE):
+            if by > 0:
+                x_send(by, part).wait_send()
+            core_send(by, part).wait_send()
 
 
 def layer(
@@ -838,10 +851,10 @@
             dma((4, SIDE - 1, SIDE)),
             dma((2,)),
             dma((2,)),
-            dma((SIDE - 1,)),
-            dma((SIDE - 1,)),
-            dma((SIDE,)),
-            dma((SIDE,)),
+            dma((2, SIDE - 1)),
+            dma((2, SIDE - 1)),
+            dma((2, SIDE)),
+            dma((2, SIDE)),
             dma((4, SIDE - 1, SIDE)),
             dma((4, SIDE - 1, SIDE)),
             dma((4, SIDE - 1)),
@@ -859,6 +872,38 @@
     )(states, lengths, offsets, count, gain, cotangent, gate_w, up_w, *squares, w_proj)
 
 
+def deliver(*refs):
+    count = len(refs) // 3
+    sources, targets = refs[:count], refs[count : 2 * count]
+    buffers, got, put = refs[2 * count : 3 * count], refs[-2], refs[-1]
+    inward = [
+        pltpu.make_async_copy(sources[i], buffers[i], got.at[i]) for i in range(count)
+    ]
+    outward = [
+        pltpu.make_async_copy(buffers[i], targets[i], put.at[i]) for i in range(count)
+    ]
+    for copy in inward:
+        copy.start()
+    for before, after in zip(inward, outward):
+        before.wait()
+        after.start()
+    for copy in outward:
+        copy.wait()
+
+
+def delivered(arrays):
+    anywhere = pl.BlockSpec(memory_space=pl.ANY)
+    return pl.pallas_call(
+        deliver,
+        out_shape=tuple(jax.ShapeDtypeStruct(a.shape, a.dtype) for a in arrays),
+        in_specs=[anywhere] * len(arrays),
+        out_specs=(anywhere,) * len(arrays),
+        scratch_shapes=[pltpu.VMEM(a.shape, a.dtype) for a in arrays]
+        + [pltpu.SemaphoreType.DMA((len(arrays),))] * 2,
+        name="deliver",
+    )(*arrays)
+
+
 def shards(
     bytes_in,
     doc_lengths,
@@ -874,7 +919,7 @@
     d_hidden,
 ):
     units = gate_w.shape[1]
-    hidden, grad_gate, grad_up, patch_grad = whole_layer(
+    results = whole_layer(
         bytes_in[0],
         doc_lengths[None],
         patch_offsets,
@@ -886,6 +931,7 @@
         (w_query, w_key, w_value),
         w_proj,
     )
+    hidden, grad_gate, grad_up, patch_grad = delivered(results)
     return (hidden.reshape(d_hidden.shape), grad_gate, grad_up, patch_grad[None])
 
 

time: 214 us -> 210 us (0.981)
  local copies, waits for them, and re-layouts: 6.37 us -> 0 us
    unnamed x8 -> x0, local copies, waits for them, and re-layouts: 6.37 us -> none
    pallas_call x0 -> x1, Pallas kernels: none -> 3.12 us  [delivered(): pl.pallas_call(deliver, out_shape=tuple((jax.ShapeDtypeStruct(a.shape, a....]
where the time goes in v7:
time: 210 us; the launch traced here: 209 us
  Pallas kernels  208 us (99%)
    pallas_call x1, Pallas kernels, whole_layer(): pl.pallas_call(layer, out_shape=(jax.ShapeDtypeStruct((tokens, units), ha...  205 us

profile of v7, /device:TPU:0, one launch (start us, length us, event | category | flops | bytes accessed | tf_op | source)
XLA Modules:
  0.0 209.5 jit_solution(6992539217800327386)
XLA Ops:
  1.3 204.9 %layer.1 = (bf16[512,896]{1,0:T(8,128)(2,1)}, f32[256,896]{1,0:T(8,128)}, f32[256,896]{1,0:T(8,128)}, f32[64,4096]{1,0:T(8,128)}) custom-call(bf16[256,1280]{1,0:T(8,128)(2,1)} %bitcast.7, s32[1,32]{1,0:T(1,128)} %bitcast.9, s32[1,64]{1,0:T(1,128)} %offsets_ref.1, s32[1,1]{1,0:T(1,128)S(6)} %copy.16.count_ref, f32[1,4096]{1,0:T(1,128)} %bitcast.8, ...), custom_call_target="tpu_custom_call" | custom-call | tf_op jit(solution)/shard_map/layer/pallas_call | solution.py:829
  206.2 3.1 %deliver.1 = (bf16[512,896]{1,0:T(8,128)(2,1)}, f32[256,896]{1,0:T(8,128)}, f32[256,896]{1,0:T(8,128)}, f32[64,4096]{1,0:T(8,128)}) custom-call(bf16[512,896]{1,0:T(8,128)(2,1)} %get-tuple-element.12.refs_0_, f32[256,896]{1,0:T(8,128)} %get-tuple-element.13.refs_1_, f32[256,896]{1,0:T(8,128)} %get-tuple-element.14.refs_2_, f32[64,4096]{1,0:T(8,128)} %get-tuple-element.15.refs_3_), custom_call_target="tpu_custom_call" | custom-call | tf_op jit(solution)/shard_map/deliver/pallas_call | solution.py:896

commit v8 on v7

--- a/solution.py
+++ b/solution.py
@@ -135,14 +135,6 @@
             device_id_type=MESH,
         )
 
-    def opening(k, carry):
-        for stream in range(4):
-            first[stream, k] = own(stream, 0, k).astype(jnp.bfloat16)
-            hop(stream, first.at[stream, k], 0, k).start()
-        return carry
-
-    lax.fori_loop(0, SIDE, opening, 0)
-
     def input_part(n):
         depth = 2 * rows
         for column in range(wide // depth):
@@ -161,22 +153,6 @@
                     value[block * slots : (block + 1) * slots]
                 )
         across_cores(n).start()
-
-    def middle(t, busy):
-        def body(k, carry):
-            for stream in range(4):
-                value = own(stream, t, k)
-                hop(stream, first.at[stream, k], t - 1, k).wait_recv()
-                arrived[stream, t - 1, k] = (
-                    value + arrived[stream, t - 1, k].astype(jnp.float32)
-                ).astype(jnp.bfloat16)
-                hop(stream, arrived.at[stream, t - 1, k], t, k).start()
-            if busy:
-                input_part(2 * k)
-                input_part(2 * k + 1)
-            return carry
-
-        lax.fori_loop(0, SIDE, body, 0)
 
     def x_phase(t):
         def body(m, carry):
@@ -210,28 +186,61 @@
         hop(stream, first.at[stream, k], last - 1, k).wait_recv()
         return value + arrived[stream, last - 1, k].astype(jnp.float32)
 
-    middle(1, True)
-    x_phase(0)
-    middle(2, False)
-    x_phase(1)
-
-    for stream in range(4):
-        second[stream] = total(stream, 0).astype(jnp.bfloat16)
-        hop2(stream, second.at[stream], 0).start()
-    x_phase(2)
-
-    def crossing(k, carry):
-        for stream in range(4):
-            value = total(stream, k)
-            hop2(stream, second.at[stream], k - 1).wait_recv()
-            crossed[stream, k - 1] = (
-                value + crossed[stream, k - 1].astype(jnp.float32)
-            ).astype(jnp.bfloat16)
-            hop2(stream, crossed.at[stream, k - 1], k).start()
+    def wave(number, carry):
+        @pl.when(number < SIDE)
+        def _():
+            for stream in range(4):
+                first[stream, number] = own(stream, 0, number).astype(jnp.bfloat16)
+                hop(stream, first.at[stream, number], 0, number).start()
+
+        for t in (1, 2):
+
+            @pl.when((number >= t) & (number < t + SIDE))
+            def _(t=t):
+                k = number - t
+                for stream in range(4):
+                    value = own(stream, t, k)
+                    hop(stream, first.at[stream, k], t - 1, k).wait_recv()
+                    arrived[stream, t - 1, k] = (
+                        value + arrived[stream, t - 1, k].astype(jnp.float32)
+                    ).astype(jnp.bfloat16)
+                    hop(stream, arrived.at[stream, t - 1, k], t, k).start()
+
+        @pl.when(number == last)
+        def _():
+            for stream in range(4):
+                second[stream] = total(stream, 0).astype(jnp.bfloat16)
+                hop2(stream, second.at[stream], 0).start()
+
+        @pl.when(number > last)
+        def _():
+            k = number - last
+            for stream in range(4):
+                value = total(stream, k)
+                hop2(stream, second.at[stream], k - 1).wait_recv()
+                crossed[stream, k - 1] = (
+                    value + crossed[stream, k - 1].astype(jnp.float32)
+                ).astype(jnp.bfloat16)
+                hop2(stream, crossed.at[stream, k - 1], k).start()
+
+        @pl.when((number == 1) | (number == 2))
+        def _():
+            def part_of(index, inner):
+                input_part(index)
+                return inner
+
+            lax.fori_loop((number - 1) * SIDE, number * SIDE, part_of, 0)
+
+        for phase in range(last):
+
+            @pl.when(number == last + phase)
+            def _(phase=phase):
+                x_phase(phase)
+
         return carry
 
-    lax.fori_loop(1, last, crossing, 0)
-    x_phase(3)
+    lax.fori_loop(0, 2 * last, wave, 0)
+    x_phase(last)
 
     def columns_of(n):
         at = pl.ds(pl.multiple_of(n * wide, wide), wide)

time: 210 us -> 209 us (level)
  no operation moved by 1% of the time
where the time goes in v8:
time: 209 us; the launch traced here: 208 us
  Pallas kernels  207 us (99%)
    pallas_call x1, Pallas kernels, whole_layer(): pl.pallas_call(layer, out_shape=(jax.ShapeDtypeStruct((tokens, units), ha...  204 us

profile of v8, /device:TPU:0, one launch (start us, length us, event | category | flops | bytes accessed | tf_op | source)
XLA Modules:
  0.0 208.4 jit_solution(6888503547077122404)
XLA Ops:
  1.3 203.9 %layer.1 = (bf16[512,896]{1,0:T(8,128)(2,1)}, f32[256,896]{1,0:T(8,128)}, f32[256,896]{1,0:T(8,128)}, f32[64,4096]{1,0:T(8,128)}) custom-call(bf16[256,1280]{1,0:T(8,128)(2,1)} %bitcast.7, s32[1,32]{1,0:T(1,128)} %bitcast.9, s32[1,64]{1,0:T(1,128)} %offsets_ref.1, s32[1,1]{1,0:T(1,128)S(6)} %copy.16.count_ref, f32[1,4096]{1,0:T(1,128)} %bitcast.8, ...), custom_call_target="tpu_custom_call" | custom-call | tf_op jit(solution)/shard_map/layer/pallas_call | solution.py:838
  205.1 3.1 %deliver.1 = (bf16[512,896]{1,0:T(8,128)(2,1)}, f32[256,896]{1,0:T(8,128)}, f32[256,896]{1,0:T(8,128)}, f32[64,4096]{1,0:T(8,128)}) custom-call(bf16[512,896]{1,0:T(8,128)(2,1)} %get-tuple-element.12.refs_0_, f32[256,896]{1,0:T(8,128)} %get-tuple-element.13.refs_1_, f32[256,896]{1,0:T(8,128)} %get-tuple-element.14.refs_2_, f32[64,4096]{1,0:T(8,128)} %get-tuple-element.15.refs_3_), custom_call_target="tpu_custom_call" | custom-call | tf_op jit(solution)/shard_map/deliver/pallas_call | solution.py:905

commit v9 on v8

--- a/solution.py
+++ b/solution.py
@@ -422,9 +422,17 @@
 
     recent = earlier.at[length : 2 * length]
     oldest = earlier.at[0:length]
-    to_next = remote(states_ref, recent, put_s.at[0], got_s.at[0], next_block)
-    to_after = remote(recent, oldest, put_s.at[1], got_s.at[1], next_block)
-    to_next.start()
+    halves = [slice(p * length // 2, (p + 1) * length // 2) for p in range(2)]
+    to_next = [
+        remote(states_ref.at[at], recent.at[at], put_s.at[p], got_s.at[p], next_block)
+        for p, at in enumerate(halves)
+    ]
+    to_after = [
+        remote(recent.at[at], oldest.at[at], put_s.at[2 + p], got_s.at[2 + p], next_block)
+        for p, at in enumerate(halves)
+    ]
+    for copy in to_next:
+        copy.start()
     load[0].wait()
     load[1].wait()
 
@@ -491,8 +499,9 @@
 
     lax.fori_loop(0, width // chunk, make_queries, 0)
     tick(1)
-    to_next.wait_recv()
-    to_after.start()
+    for before, after in zip(to_next, to_after):
+        before.wait_recv()
+        after.start()
     tick(2)
     load[3].wait()
     load[4].wait()
@@ -563,7 +572,8 @@
     sizes = jnp.maximum(jnp.sum(ones, axis=1, keepdims=True), 1.0)
     members = ones.astype(jnp.bfloat16)
     tick(5)
-    to_after.wait_recv()
+    for copy in to_after:
+        copy.wait_recv()
     keys_and_values(oldest, 0)
     load[5].start()
     tick(6)
@@ -698,8 +708,8 @@
 
     lax.fori_loop(0, groups, gating, 0)
 
-    to_next.wait_send()
-    to_after.wait_send()
+    for copy in (*to_next, *to_after):
+        copy.wait_send()
     for stream in range(4):
         for k in range(SIDE):
             if k < last:
@@ -858,8 +868,8 @@
             dma((4, SIDE - 1)),
             dma((4, SIDE - 1, SIDE)),
             dma((4, SIDE - 1, SIDE)),
-            dma((2,)),
-            dma((2,)),
+            dma((4,)),
+            dma((4,)),
             dma((2, SIDE - 1)),
             dma((2, SIDE - 1)),
             dma((2, SIDE)),

time: 209 us -> 209 us (level)
  no operation moved by 1% of the time
where the time goes in v9:
time: 209 us; the launch traced here: 208 us
  Pallas kernels  207 us (99%)
    pallas_call x1, Pallas kernels, whole_layer(): pl.pallas_call(layer, out_shape=(jax.ShapeDtypeStruct((tokens, units), ha...  204 us

profile of v9, /device:TPU:0, one launch (start us, length us, event | category | flops | bytes accessed | tf_op | source)
XLA Modules:
  0.0 208.5 jit_solution(13853861939275714459)
XLA Ops:
  1.3 203.9 %layer.1 = (bf16[512,896]{1,0:T(8,128)(2,1)}, f32[256,896]{1,0:T(8,128)}, f32[256,896]{1,0:T(8,128)}, f32[64,4096]{1,0:T(8,128)}) custom-call(bf16[256,1280]{1,0:T(8,128)(2,1)} %bitcast.7, s32[1,32]{1,0:T(1,128)} %bitcast.9, s32[1,64]{1,0:T(1,128)} %offsets_ref.1, s32[1,1]{1,0:T(1,128)S(6)} %copy.16.count_ref, f32[1,4096]{1,0:T(1,128)} %bitcast.8, ...), custom_call_target="tpu_custom_call" | custom-call | tf_op jit(solution)/shard_map/layer/pallas_call | solution.py:848
  205.2 3.1 %deliver.1 = (bf16[512,896]{1,0:T(8,128)(2,1)}, f32[256,896]{1,0:T(8,128)}, f32[256,896]{1,0:T(8,128)}, f32[64,4096]{1,0:T(8,128)}) custom-call(bf16[512,896]{1,0:T(8,128)(2,1)} %get-tuple-element.12.refs_0_, f32[256,896]{1,0:T(8,128)} %get-tuple-element.13.refs_1_, f32[256,896]{1,0:T(8,128)} %get-tuple-element.14.refs_2_, f32[64,4096]{1,0:T(8,128)} %get-tuple-element.15.refs_3_), custom_call_target="tpu_custom_call" | custom-call | tf_op jit(solution)/shard_map/deliver/pallas_call | solution.py:915

commit v10 on v9

--- a/solution.py
+++ b/solution.py
@@ -70,7 +70,6 @@
     )
     for neighbour in around:
         pl.semaphore_signal(ready, inc=1, device_id=neighbour, device_id_type=MESH)
-    pl.semaphore_wait(ready, len(around))
 
     def place(stream):
         kind, half = stream // 2, stream % 2
@@ -187,7 +186,7 @@
         return value + arrived[stream, last - 1, k].astype(jnp.float32)
 
     def wave(number, carry):
-        @pl.when(number < SIDE)
+        @pl.when((number > 0) & (number < SIDE))
         def _():
             for stream in range(4):
                 first[stream, number] = own(stream, 0, number).astype(jnp.bfloat16)
@@ -239,7 +238,12 @@
 
         return carry
 
-    lax.fori_loop(0, 2 * last, wave, 0)
+    for stream in range(4):
+        first[stream, 0] = own(stream, 0, 0).astype(jnp.bfloat16)
+    pl.semaphore_wait(ready, len(around))
+    for stream in range(4):
+        hop(stream, first.at[stream, 0], 0, 0).start()
+    lax.fori_loop(1, 2 * last, wave, 0)
     x_phase(last)
 
     def columns_of(n):

time: 209 us -> 208 us (level)
  no operation moved by 1% of the time
where the time goes in v10:
time: 208 us
  Pallas kernels  207 us (100%)
    pallas_call x1, Pallas kernels, whole_layer(): pl.pallas_call(layer, out_shape=(jax.ShapeDtypeStruct((tokens, units), ha...  204 us

profile of v10, /device:TPU:0, one launch (start us, length us, event | category | flops | bytes accessed | tf_op | source)
XLA Modules:
  0.0 208.1 jit_solution(699865224079122644)
XLA Ops:
  1.3 203.5 %layer.1 = (bf16[512,896]{1,0:T(8,128)(2,1)}, f32[256,896]{1,0:T(8,128)}, f32[256,896]{1,0:T(8,128)}, f32[64,4096]{1,0:T(8,128)}) custom-call(bf16[256,1280]{1,0:T(8,128)(2,1)} %bitcast.7, s32[1,32]{1,0:T(1,128)} %bitcast.9, s32[1,64]{1,0:T(1,128)} %offsets_ref.1, s32[1,1]{1,0:T(1,128)S(6)} %copy.16.count_ref, f32[1,4096]{1,0:T(1,128)} %bitcast.8, ...), custom_call_target="tpu_custom_call" | custom-call | tf_op jit(solution)/shard_map/layer/pallas_call | solution.py:852
  204.8 3.1 %deliver.1 = (bf16[512,896]{1,0:T(8,128)(2,1)}, f32[256,896]{1,0:T(8,128)}, f32[256,896]{1,0:T(8,128)}, f32[64,4096]{1,0:T(8,128)}) custom-call(bf16[512,896]{1,0:T(8,128)(2,1)} %get-tuple-element.12.refs_0_, f32[256,896]{1,0:T(8,128)} %get-tuple-element.13.refs_1_, f32[256,896]{1,0:T(8,128)} %get-tuple-element.14.refs_2_, f32[64,4096]{1,0:T(8,128)} %get-tuple-element.15.refs_3_), custom_call_target="tpu_custom_call" | custom-call | tf_op jit(solution)/shard_map/deliver/pallas_call | solution.py:919
